TPU v7x, 32 devices: a whole 2x2x4 slice. The times are simulated.
32 devices in a mesh: expert: 4 (over y, x), etp: 8 (over z, core).
Axes of the slice: x: 2, y: 2, z: 4, core: 2. Of those that a mesh axis runs over, the one named last changes fastest.
Arguments:
- tokens: bfloat16 [512, 2880], P('expert', 'etp'), may hold values from -6 to 6
- grad_out: bfloat16 [512, 2880], P('expert', 'etp'), may hold values from -6 to 6
- gates: float32 [512, 4], P('expert'), may hold values from 0.05 to 0.6
- routes: int32 [512, 4], P('expert'), may hold values from 0 to 7, all different within a row; in each aligned block of 128 rows (0 to 127, 128 to 255, ...) at most 96 rows name the same one
- w_gate: bfloat16 [8, 2880, 2880], P('expert', 'etp'), may hold values from -0.109375 to 0.109375
- w_up: bfloat16 [8, 2880, 2880], P('expert', 'etp'), may hold values from -0.109375 to 0.109375
- w_down: bfloat16 [8, 2880, 2880], P('expert', 'etp'), may hold values from -0.109375 to 0.109375
Outputs:
- d_tokens: bfloat16 [512, 2880], P('expert', 'etp')
- d_gate: bfloat16 [8, 2880, 2880], P('expert', 'etp')
- d_up: bfloat16 [8, 2880, 2880], P('expert', 'etp')
- d_down: bfloat16 [8, 2880, 2880], P('expert', 'etp')
Inputs may be any that keep to these rules, and one draw needn't show every extreme that they name: `routes`: each row names 4 different experts. In each aligned block of 128 rows (the tokens of one index of expert) no expert is named by more than 96 rows, and in some block one expert is named by exactly 96 rows.
All inputs are finite; a program needn't handle non-finite values.
Results may differ from a plain program's by a relative error of at most 0.0058.
Values may be sent and summed in bfloat16 or wider, within the bound.
No kernel may reach another device: no remote copies, remote signals or barrier semaphores. Data moves between devices by JAX's collectives and lax.ppermute only.
A program may use at most 128 MiB of HBM per device.

v0:
```python
import jax
import jax.numpy as jnp
from jax import lax
from jax.sharding import PartitionSpec as P


def body(tokens, grad_out, gates, routes, w_gate, w_up, w_down):
    groups = lax.axis_size("expert")
    local = w_gate.shape[0]
    experts = groups * local
    tok_rows = tokens.shape[0]
    topk = routes.shape[1]
    capacity = 3 * topk * tok_rows // (2 * experts)
    pairs = tok_rows * topk
    flat = routes.reshape(-1)
    onehot = (flat[:, None] == jnp.arange(experts, dtype=jnp.int32)[None, :]).astype(jnp.int32)
    ranking = jnp.sum(jnp.cumsum(onehot, 0) * onehot, 1) - 1
    slot_of = flat * capacity + ranking
    owner = (
        jnp.zeros((experts * capacity,), jnp.int32)
        .at[slot_of]
        .set(jnp.arange(pairs, dtype=jnp.int32))
    )
    filled = jnp.zeros((experts * capacity,), jnp.int32).at[slot_of].set(1) > 0
    source_tok = owner // topk
    weight_of = gates.reshape(-1)[owner]
    whole_x, whole_g = (
        lax.all_gather(tokens, "etp", axis=1, tiled=True),
        lax.all_gather(grad_out, "etp", axis=1, tiled=True),
    )
    width = whole_x.shape[1]
    x_send = jnp.where(filled[:, None], whole_x[source_tok], 0)
    g_send = jnp.where(
        filled[:, None], weight_of[:, None] * whole_g[source_tok].astype(jnp.float32), 0.0
    )
    g_send = g_send.astype(jnp.bfloat16)
    layout = (groups, local, capacity, width)
    send_x = x_send.reshape(layout)
    send_g = g_send.reshape(layout)
    routed_x, routed_g = (
        lax.all_to_all(send_x, "expert", split_axis=0, concat_axis=0, tiled=True),
        lax.all_to_all(send_g, "expert", split_axis=0, concat_axis=0, tiled=True),
    )
    pre_gate = jnp.einsum("secd,efd->secf", routed_x, w_gate, preferred_element_type=jnp.float32)
    pre_up = jnp.einsum("secd,efd->secf", routed_x, w_up, preferred_element_type=jnp.float32)
    d_act = jnp.einsum("secd,efd->secf", routed_g, w_down, preferred_element_type=jnp.float32)
    sig = jax.nn.sigmoid(1.702 * pre_gate)
    glu = pre_gate * sig
    act = (glu * (pre_up + 1.0)).astype(jnp.bfloat16)
    d_pre_gate = (d_act * (pre_up + 1.0) * (sig + 1.702 * pre_gate * sig * (1.0 - sig))).astype(
        jnp.bfloat16
    )
    d_pre_up = (d_act * glu).astype(jnp.bfloat16)
    d_gate = jnp.einsum(
        "secf,secd->efd", d_pre_gate, routed_x, preferred_element_type=jnp.float32
    ).astype(jnp.bfloat16)
    d_up = jnp.einsum(
        "secf,secd->efd", d_pre_up, routed_x, preferred_element_type=jnp.float32
    ).astype(jnp.bfloat16)
    d_down = jnp.einsum("secf,secd->efd", act, routed_g, preferred_element_type=jnp.float32).astype(
        jnp.bfloat16
    )
    term = jnp.einsum("secf,efd->secd", d_pre_gate, w_gate, preferred_element_type=jnp.float32)
    term = term + jnp.einsum("secf,efd->secd", d_pre_up, w_up, preferred_element_type=jnp.float32)
    moved = lax.all_to_all(term, "expert", split_axis=0, concat_axis=0, tiled=True)
    home = lax.psum_scatter(moved, "etp", scatter_dimension=3, tiled=True)
    width = home.shape[3]
    per_pair = home.reshape(experts * capacity, width)[slot_of].reshape(tok_rows, topk, width)
    d_tokens = jnp.sum(per_pair, 1).astype(jnp.bfloat16)
    return (d_tokens, d_gate, d_up, d_down)


def solution(mesh):
    placed = (
        P("expert", "etp"),
        P("expert", "etp"),
        P("expert", None),
        P("expert", None),
        P("expert", "etp", None),
        P("expert", "etp", None),
        P("expert", "etp", None),
    )
    return jax.shard_map(
        body,
        mesh=mesh,
        in_specs=placed,
        out_specs=(
            P("expert", "etp"),
            P("expert", "etp", None),
            P("expert", "etp", None),
            P("expert", "etp", None),
        ),
        check_vma=False,
    )
```

profile of v0, /device:TPU:0, one launch (start us, length us, event | category | flops | bytes accessed | tf_op | source)
XLA Modules:
  0.0 408.4 jit_solution(15865717688573526822)
XLA Ops:
  10.6 2.4 scatter_custom_fusion.1
  15.6 17.3 %all_gather.7 = bf16[128,2880]{0,1:T(8,128)(2,1)S(1)} all-gather(bf16[128,360]{0,1:T(8,128)(2,1)} %param.7), channel_id=1, replica_groups=mesh['expert'=4,'etp'=8] {'etp'}, dimensions={1}, use_global_device_ids=true | all-gather | bytes 829440 | tf_op jit(solution)/shard_map/all_gather | solution.py:28
  33.3 5.0 %gather_fusion.2 = bf16[768,2880]{1,0:T(8,128)(2,1)} fusion(bf16[128,2880]{1,0:T(8,128)(2,1)S(1)} %copy.30, s32[1024]{0:T(1024)S(1)} %pad_clamp_fusion.1), kind=kCustom, calls=%fused_computation.2 | custom fusion | bytes 8850432 | tf_op jit(solution)/shard_map/gather | solution.py:32
  38.2 4.8 %broadcast_select_fusion = bf16[4,2,96,2880]{3,2,1,0:T(8,128)(2,1)} fusion(bf16[4,2,96,2880]{3,2,1,0:T(8,128)(2,1)} %bitcast.68, pred[4,2,96]{2,1,0:T(4,128)(4,1)S(1)} %broadcast_in_dim.38), kind=kLoop, calls=%fused_computation.13 | loop fusion | flops 2211840 | bytes 8848128 | tf_op jit(solution)/shard_map/jit(_where)/select_n | solution.py:32
  43.0 5.0 %all-to-all-start.1 = ((bf16[4,2,96,2880]{3,2,1,0:T(8,128)(2,1)}), bf16[4,2,96,2880]{3,2,1,0:T(8,128)(2,1)}, u32[]{:S(2)}, u32[]{:S(2)}) async-start(bf16[4,2,96,2880]{3,2,1,0:T(8,128)(2,1)} %broadcast_select_fusion), calls=%async_computation.1 | async-start | bytes 9043968 | tf_op jit(solution)/shard_map/all_to_all | solution.py:41
  48.1 15.5 %all_gather.6 = bf16[128,2880]{0,1:T(8,128)(2,1)S(1)} all-gather(bf16[128,360]{0,1:T(8,128)(2,1)S(1)} %copy-done), channel_id=1, replica_groups=mesh['expert'=4,'etp'=8] {'etp'}, dimensions={1}, use_global_device_ids=true | all-gather | bytes 829440 | tf_op jit(solution)/shard_map/all_gather | solution.py:29
  64.0 4.9 %gather_fusion.1 = bf16[768,2880]{1,0:T(8,128)(2,1)} fusion(bf16[128,2880]{1,0:T(8,128)(2,1)S(1)} %copy.28, s32[1024]{0:T(1024)S(1)} %pad_clamp_fusion.1), kind=kCustom, calls=%fused_computation.1 | custom fusion | bytes 8850432 | tf_op jit(solution)/shard_map/gather | solution.py:34
  69.2 5.0 %gather_fusion = f32[768]{0:T(1024)S(1)} fusion(f32[512]{0:T(512)S(1)} %reshape.91, s32[1024]{0:T(1024)S(1)} %pad_clamp_fusion.2), kind=kCustom, calls=%fused_computation | custom fusion | bytes 9216 | tf_op jit(solution)/shard_map/gather | solution.py:26
  74.2 6.8 %fusion.1 = bf16[4,2,96,2880]{3,2,1,0:T(8,128)(2,1)} fusion(bf16[4,2,96,2880]{3,2,1,0:T(8,128)(2,1)} %bitcast.67, f32[4,2,96]{2,1,0:T(2,128)S(1)} %mul.59, pred[4,2,96]{2,1,0:T(4,128)(4,1)S(1)} %broadcast_in_dim.38), kind=kLoop, calls=%fused_computation.8 | loop fusion | flops 8847360 | bytes 8851200 | tf_op jit(solution)/shard_map/convert_element_type | solution.py:36
  81.1 18.8 %all-to-all-done.1 = bf16[4,2,96,2880]{3,2,1,0:T(8,128)(2,1)} async-done(((bf16[4,2,96,2880]{3,2,1,0:T(8,128)(2,1)}), bf16[4,2,96,2880]{3,2,1,0:T(8,128)(2,1)}, u32[]{:S(2)}, u32[]{:S(2)}) %all-to-all-start.1) | async-done | bytes 4423712 | tf_op jit(solution)/shard_map/all_to_all | solution.py:41
  99.8 5.0 %all-to-all-start = ((bf16[4,2,96,2880]{3,2,1,0:T(8,128)(2,1)}), bf16[4,2,96,2880]{3,2,1,0:T(8,128)(2,1)}, u32[]{:S(2)}, u32[]{:S(2)}) async-start(bf16[4,2,96,2880]{3,2,1,0:T(8,128)(2,1)} %fusion.1), calls=%async_computation | async-start | bytes 9043968 | tf_op jit(solution)/shard_map/all_to_all | solution.py:42
  105.0 6.1 %fusion.22 = f32[4,2,96,360]{3,2,0,1:T(8,128)S(1)} fusion(bf16[2,360,2880]{2,1,0:T(8,128)(2,1)} %param.11, bf16[4,2,96,2880]{3,2,1,0:T(8,128)(2,1)} %all-to-all-done.1), kind=kOutput, calls=%fused_computation.30 | convolution fusion | flops 1592524800 | bytes 9676800 | tf_op jit(solution)/shard_map/secd,efd->secf/dot_general | solution.py:44
  111.1 7.6 %fusion.32 = f32[4,2,96,360]{3,2,0,1:T(8,128)} fusion(bf16[2,360,2880]{2,1,0:T(8,128)(2,1)} %param.12, bf16[4,2,96,2880]{3,2,1,0:T(8,128)(2,1)} %all-to-all-done.1), kind=kOutput, calls=%fused_computation.32 | convolution fusion | flops 1592801280 | bytes 9676800 | tf_op jit(solution)/shard_map/secd,efd->secf/dot_general | solution.py:45
  118.7 37.0 %all-to-all-done = bf16[4,2,96,2880]{3,2,1,0:T(8,128)(2,1)} async-done(((bf16[4,2,96,2880]{3,2,1,0:T(8,128)(2,1)}), bf16[4,2,96,2880]{3,2,1,0:T(8,128)(2,1)}, u32[]{:S(2)}, u32[]{:S(2)}) %all-to-all-start) | async-done | bytes 4423712 | tf_op jit(solution)/shard_map/all_to_all | solution.py:42
  155.7 6.7 %multiply_convert_fusion.1 = (bf16[4,2,96,360]{3,2,0,1:T(8,128)(2,1)S(1)}, bf16[4,2,96,360]{3,2,0,1:T(8,128)(2,1)S(1)}) fusion(f32[4,2,96,360]{3,2,0,1:T(8,128)S(1)} %fusion.22, f32[4,2,96,360]{3,2,0,1:T(8,128)} %fusion.32, bf16[2,360,2880]{2,1,0:T(8,128)(2,1)} %param.13, bf16[4,2,96,2880]{3,2,1,0:T(8,128)(2,1)} %all-to-all-done), kind=kOutput, calls=%fused_computation.34 | convolution fusion | flops 1596395520 | bytes 11888640 | tf_op jit(solution)/shard_map/secd,efd->secf/dot_general | solution.py:46
  162.4 4.4 %fusion.2 = f32[2,4,96,2880]{3,2,1,0:T(8,128)S(1)} fusion(bf16[4,2,96,360]{3,2,0,1:T(8,128)(2,1)S(1)} %get-tuple-element.9, bf16[2,360,2880]{2,1,0:T(8,128)(2,1)} %param.11), kind=kOutput, calls=%fused_computation.14 | convolution fusion | flops 1592524800 | bytes 13547520 | tf_op jit(solution)/shard_map/secf,efd->secd/dot_general | solution.py:63
  166.7 4.4 %add_bitcast_fusion = f32[4,2,96,2880]{3,2,0,1:T(8,128)S(1)} fusion(f32[2,4,96,2880]{3,2,1,0:T(8,128)S(1)} %fusion.2, bf16[4,2,96,360]{3,2,0,1:T(8,128)(2,1)S(1)} %get-tuple-element.8, bf16[2,360,2880]{2,1,0:T(8,128)(2,1)} %param.12), kind=kOutput, calls=%fused_computation.9 | convolution fusion | flops 1594736640 | bytes 22394880 | tf_op jit(solution)/shard_map/secf,efd->secd/dot_general | solution.py:64
  171.8 103.2 %all_to_all.15 = f32[4,2,96,2880]{3,2,1,0:T(8,128)} all-to-all(f32[4,2,96,2880]{3,2,1,0:T(8,128)S(1)} %copy.33), channel_id=1, replica_groups=mesh['expert'=4,'etp'=8] {'expert'}, dimensions={0} | all-to-all | bytes 17694720 | tf_op jit(solution)/shard_map/all_to_all | solution.py:65
  275.0 13.0 %copy.46 = f32[4,2,96,2880]{2,0,1,3:T(4,128)} copy(f32[4,2,96,2880]{3,2,1,0:T(8,128)} %all_to_all.15) | data formatting | bytes 17694720
  288.0 13.5 %reshape.152 = f32[2880,768]{1,0:T(8,128)} reshape(f32[2880,2,4,96]{3,2,1,0:T(4,128)} %bitcast.66) | data formatting | bytes 17694720
  301.6 7.0 %bitcast_convert_fusion.1 = bf16[2,360,2880]{2,1,0:T(8,128)(2,1)} fusion(bf16[4,2,96,360]{3,2,0,1:T(8,128)(2,1)S(1)} %get-tuple-element.8, bf16[4,2,96,2880]{3,2,1,0:T(8,128)(2,1)} %all-to-all-done.1), kind=kOutput, calls=%fused_computation.11 | convolution fusion | flops 1594598400 | bytes 9123840 | tf_op jit(solution)/shard_map/secf,secd->efd/dot_general | solution.py:57
  308.6 7.0 %bitcast_convert_fusion.2 = bf16[2,360,2880]{2,1,0:T(8,128)(2,1)} fusion(bf16[4,2,96,360]{3,2,0,1:T(8,128)(2,1)S(1)} %get-tuple-element.9, bf16[4,2,96,2880]{3,2,1,0:T(8,128)(2,1)} %all-to-all-done.1), kind=kOutput, calls=%fused_computation.12 | convolution fusion | flops 1594598400 | bytes 9123840 | tf_op jit(solution)/shard_map/secf,secd->efd/dot_general | solution.py:54
  315.5 6.9 %bitcast_convert_fusion = bf16[2,360,2880]{2,1,0:T(8,128)(2,1)} fusion(bf16[4,2,96,2880]{3,2,1,0:T(8,128)(2,1)} %all-to-all-done, f32[4,2,96,360]{3,2,0,1:T(8,128)S(1)} %copy-done.4, f32[4,2,96,360]{3,2,0,1:T(8,128)S(1)} %copy-done.3), kind=kOutput, calls=%fused_computation.10 | convolution fusion | flops 1596533760 | bytes 10782720 | tf_op jit(solution)/shard_map/secf,secd->efd/dot_general | solution.py:60
  322.4 72.9 %reduce-scatter.4.cloned.1.call-done = f32[360,768]{1,0:T(8,128)} async-done(((f32[2880,768]{1,0:T(8,128)}), f32[360,768]{1,0:T(8,128)}) %reduce-scatter.4.cloned.1.call-update) | async-done | bytes 1105936
  (47 shorter events, 14.1 us)
Async XLA Ops:
  43.0 5.1 %copy-start = (bf16[128,360]{0,1:T(8,128)(2,1)S(1)}, bf16[128,360]{0,1:T(8,128)(2,1)}, u32[]{:S(2)}) copy-start(bf16[128,360]{0,1:T(8,128)(2,1)} %param.8) | copy-start | bytes 276484
  43.0 56.8 %all-to-all-start.1 = ((bf16[4,2,96,2880]{3,2,1,0:T(8,128)(2,1)}), bf16[4,2,96,2880]{3,2,1,0:T(8,128)(2,1)}, u32[]{:S(2)}, u32[]{:S(2)}) async-start(bf16[4,2,96,2880]{3,2,1,0:T(8,128)(2,1)} %broadcast_select_fusion), calls=%async_computation.1 | async-start | bytes 9043968 | tf_op jit(solution)/shard_map/all_to_all | solution.py:41
  64.0 4.9 %copy-start.1 = (f32[128,4]{0,1:T(4,128)S(1)}, f32[128,4]{0,1:T(4,128)}, u32[]{:S(2)}) copy-start(f32[128,4]{0,1:T(4,128)} %param.9) | copy-start | bytes 6148
  99.8 55.9 %all-to-all-start = ((bf16[4,2,96,2880]{3,2,1,0:T(8,128)(2,1)}), bf16[4,2,96,2880]{3,2,1,0:T(8,128)(2,1)}, u32[]{:S(2)}, u32[]{:S(2)}) async-start(bf16[4,2,96,2880]{3,2,1,0:T(8,128)(2,1)} %fusion.1), calls=%async_computation | async-start | bytes 9043968 | tf_op jit(solution)/shard_map/all_to_all | solution.py:42
  104.8 290.5 %reduce-scatter.4.cloned.1.call-start = ((), (), s32[]{:S(2)}) async-start(), calls=%async_computation.4 | async-start | bytes 9953280
  111.1 44.6 %copy-start.2 = (f32[4,2,96,360]{3,2,0,1:T(8,128)}, f32[4,2,96,360]{3,2,0,1:T(8,128)S(1)}, u32[]{:S(2)}) copy-start(f32[4,2,96,360]{3,2,0,1:T(8,128)S(1)} %fusion.22) | copy-start | bytes 3317764
  308.6 7.0 %copy-start.3 = (f32[4,2,96,360]{3,2,0,1:T(8,128)S(1)}, f32[4,2,96,360]{3,2,0,1:T(8,128)}, u32[]{:S(2)}) copy-start(f32[4,2,96,360]{3,2,0,1:T(8,128)} %copy-done.2) | copy-start | bytes 3317764
  308.6 7.0 %copy-start.4 = (f32[4,2,96,360]{3,2,0,1:T(8,128)S(1)}, f32[4,2,96,360]{3,2,0,1:T(8,128)}, u32[]{:S(2)}) copy-start(f32[4,2,96,360]{3,2,0,1:T(8,128)} %fusion.32) | copy-start | bytes 3317764
Sparse Core Ops, SparseCore 0:
  301.7 93.5 reduce-scatter.3
where the time goes:
time: 410 us; the launch traced here: 408 us
  blocking collectives  136 us (33%)
  waiting for transfers between devices  129 us (31%)
  local copies, waits for them, and re-layouts  55.2 us (13%)
  matrix products  49.9 us (12%)
  between operations  14.3 us (3%)
  other arithmetic  14.1 us (3%)
  starting transfers between devices  10.3 us (3%)
    all_to_all x1, blocking collectives, body(): lax.all_to_all(term, 'expert', split_axis=0, concat_axis=0, tiled=True)  103 us
    unnamed x2, waiting for transfers between devices  72.9 us
    all_to_all x1, waiting for transfers between devices, body(): lax.all_to_all(send_g, 'expert', split_axis=0, concat_axis=0, tiled=True)  37 us
    unnamed x16, local copies, waits for them, and re-layouts  30.6 us
    all_to_all x1, waiting for transfers between devices, body(): lax.all_to_all(send_x, 'expert', split_axis=0, concat_axis=0, tiled=True)  18.8 us
    all_gather x1, blocking collectives, body(): lax.all_gather(tokens, 'etp', axis=1, tiled=True)  17.3 us
    all_gather x1, blocking collectives, body(): lax.all_gather(grad_out, 'etp', axis=1, tiled=True)  15.5 us
  transfers between devices with their start and end apart: 3, of which 3 were waited for; matrix products, arithmetic and copies ran while one was open for 13% of the time, Pallas kernels for 0%

commit v1 on v0

v1 whole, which is shorter than its diff:
```python
import jax
import jax.numpy as jnp
from jax import lax
from jax.sharding import Mesh
from jax.sharding import PartitionSpec as P

BF16, F32 = jnp.bfloat16, jnp.float32


def xor_send(a, axis, s):
    return lax.ppermute(a, axis, [(i, i ^ s) for i in range(lax.axis_size(axis))])


def gather_columns(own):
    rings = lax.all_gather(own, "ring", axis=0)
    blocks = [rings] + [
        xor_send(rings, "expert", s) for s in range(1, lax.axis_size("expert"))
    ]
    half = jnp.concatenate(blocks, -1)
    other = xor_send(half, "core", 1)
    first = lax.axis_index("core") == 0
    both = jnp.where(first, jnp.stack([half, other], 1), jnp.stack([other, half], 1))
    return both.reshape(-1, both.shape[-1])


def sum_home(part, rows):
    rings, groups = lax.axis_size("ring"), lax.axis_size("expert")
    core, ring = lax.axis_index("core"), lax.axis_index("ring")
    part = part.reshape(rings, 2, -1, part.shape[-1])
    keep = lax.dynamic_index_in_dim(part, core, 1, False)
    give = lax.dynamic_index_in_dim(part, 1 - core, 1, False).astype(BF16)
    chip = keep + xor_send(give, "core", 1).astype(F32)
    chip_b = chip.astype(BF16)
    mine = chip[..., :rows]
    for s in range(1, groups):
        mine = mine + xor_send(chip_b[..., s * rows : (s + 1) * rows], "expert", s).astype(F32)
    mine_b = mine.astype(BF16)
    home = lax.dynamic_index_in_dim(mine, ring, 0, False)
    for s in range(1, rings):
        home = home + xor_send(
            lax.dynamic_index_in_dim(mine_b, ring ^ s, 0, False), "ring", s
        ).astype(F32)
    return home.astype(BF16)


def body(tokens, grad_out, gates, routes, w_gate, w_up, w_down):
    groups = lax.axis_size("expert")
    local = w_gate.shape[0]
    rows = tokens.shape[0]
    group = lax.axis_index("expert")

    ids = jnp.arange(groups * local, dtype=jnp.int32)
    named = routes[None] == ids[:, None, None]
    weight = jnp.sum(jnp.where(named, gates[None], 0.0), -1)
    weight = weight.reshape(groups, local, rows)
    coef = [lax.dynamic_index_in_dim(weight, group, 0, False)]
    for s in range(1, groups):
        coef.append(xor_send(lax.dynamic_index_in_dim(weight, group ^ s, 0, False), "expert", s))
    coef = jnp.concatenate(coef, -1)[:, None, :]

    x = gather_columns(tokens.T)
    g = gather_columns(grad_out.T)

    def to_hidden(w, a):
        return jnp.einsum("efd,dt->eft", w, a, preferred_element_type=F32)

    pre_gate = to_hidden(w_gate, x)
    pre_up = to_hidden(w_up, x)
    d_act = to_hidden(w_down, g) * coef
    sig = jax.nn.sigmoid(1.702 * pre_gate)
    glu = pre_gate * sig
    act = (glu * (pre_up + 1.0) * coef).astype(BF16)
    d_pre_gate = (d_act * (pre_up + 1.0) * (sig + 1.702 * pre_gate * sig * (1.0 - sig))).astype(BF16)
    d_pre_up = (d_act * glu).astype(BF16)

    term = jnp.einsum("efd,eft->dt", w_gate, d_pre_gate, preferred_element_type=F32)
    term = term + jnp.einsum("efd,eft->dt", w_up, d_pre_up, preferred_element_type=F32)
    d_tokens = sum_home(term, rows).T

    def to_weight(a, b):
        return jnp.einsum("eft,dt->efd", a, b, preferred_element_type=F32).astype(BF16)

    return d_tokens, to_weight(d_pre_gate, x), to_weight(d_pre_up, x), to_weight(act, g)


def solution(mesh):
    groups, shards = mesh.shape["expert"], mesh.shape["etp"]
    split = Mesh(mesh.devices.reshape(groups, shards // 2, 2), ("expert", "ring", "core"))
    etp = ("ring", "core")
    hidden = P("expert", etp, None)
    return jax.shard_map(
        body,
        mesh=split,
        in_specs=(P("expert", etp), P("expert", etp), P("expert", None), P("expert", None), hidden, hidden, hidden),
        out_specs=(P("expert", etp), hidden, hidden, hidden),
        check_vma=False,
    )
```

time: 410 us -> 124 us (0.30)
  blocking collectives: 136 us -> 31.7 us
  waiting for transfers between devices: 129 us -> 25.8 us
  local copies, waits for them, and re-layouts: 55.2 us -> 5.48 us
  matrix products: 49.9 us -> 32.3 us
  between operations: 14.3 us -> 0.94 us
  starting transfers between devices: 10.3 us -> 18.5 us
  other arithmetic: 14.1 us -> 9.29 us
    all_to_all x1 -> x0, blocking collectives: 103 us -> none  [body(): lax.all_to_all(term, 'expert', split_axis=0, concat_axis=0, tiled=True)]
    unnamed x2 -> x0, waiting for transfers between devices: 72.9 us -> none
    all_to_all x2 -> x0, waiting for transfers between devices: 55.8 us -> none  [the longest x1 37 us: body(): lax.all_to_all(send_g, 'expert', split_axis=0, concat_axis=0, tiled=True)]
    unnamed x16 -> x34, local copies, waits for them, and re-layouts: 30.6 us -> 3.42 us
    ppermute x0 -> x18, waiting for transfers between devices: none -> 25.8 us  [xor_send(): lax.ppermute(a, axis, [(i, i ^ s) for i in range(lax.axis_size(axis))])]
    ppermute x0 -> x18, starting transfers between devices: none -> 18.5 us  [xor_send(): lax.ppermute(a, axis, [(i, i ^ s) for i in range(lax.axis_size(axis))])]
    dot_general x8, matrix products: 49.9 us -> 32.3 us  [the longest x3 16.7 us: to_weight(): jnp.einsum('eft,dt->efd', a, b, preferred_element_type=F32).astype(BF16)]
    gather x4 -> x0, local copies, waits for them, and re-layouts: 16.5 us -> none  [the longest x1 5.01 us: body(): weight_of = gates.reshape(-1)[owner]]
  transfers between devices with their start and end apart: 3 -> 18, of which waited for: 3 -> 9; matrix products, arithmetic and copies ran while one was open for 13% -> 16% of each run, Pallas kernels for 0% -> 0%
where the time goes in v1:
time: 124 us
  matrix products  32.3 us (26%)
  blocking collectives  31.7 us (26%)
  waiting for transfers between devices  25.8 us (21%)
  starting transfers between devices  18.5 us (15%)
  other arithmetic  9.29 us (7%)
  local copies, waits for them, and re-layouts  5.48 us (4%)
    all_gather x2, blocking collectives, gather_columns(): rings = lax.all_gather(own, 'ring', axis=0)  31.7 us
    ppermute x18, waiting for transfers between devices, xor_send(): lax.ppermute(a, axis, [(i, i ^ s) for i in range(lax.axis_size(axis))])  25.8 us
    ppermute x18, starting transfers between devices, xor_send(): lax.ppermute(a, axis, [(i, i ^ s) for i in range(lax.axis_size(axis))])  18.5 us
    dot_general x3, matrix products, to_weight(): jnp.einsum('eft,dt->efd', a, b, preferred_element_type=F32).astype(BF16)  16.7 us
    dot_general x3, matrix products, to_hidden(): return jnp.einsum('efd,dt->eft', w, a, preferred_element_type=F32)  10.3 us
    select_n x1, other arithmetic, gather_columns(): jnp.where(first, jnp.stack([half, other], 1), jnp.stack([other, half], 1))  3.66 us
    unnamed x34, local copies, waits for them, and re-layouts  3.42 us
    dot_general x1, matrix products, body(): jnp.einsum('efd,eft->dt', w_up, d_pre_up, preferred_element_type=F32)  2.73 us
  transfers between devices with their start and end apart: 18, of which 9 were waited for; matrix products, arithmetic and copies ran while one was open for 16% of the time, Pallas kernels for 0%

profile of v1, /device:TPU:0, one launch (start us, length us, event | category | flops | bytes accessed | tf_op | source)
XLA Modules:
  0.0 124.1 jit_solution(1122426161669049733)
XLA Ops:
  0.6 16.3 %all-gather = bf16[1440,128]{1,0:T(8,128)(2,1)S(1)} all-gather(bf16[360,128]{1,0:T(8,128)(2,1)} %bitcast.118), channel_id=2, replica_groups=mesh['expert'=4,'ring'=4,'core'=2] {'ring'}, dimensions={0}, use_global_device_ids=true | all-gather | bytes 460800 | tf_op jit(solution)/shard_map/all_gather | solution.py:15
  16.9 2.4 %collective-permute-start.2 = (bf16[4,360,128]{2,1,0:T(8,128)(2,1)S(1)}, bf16[4,360,128]{2,1,0:T(8,128)(2,1)S(1)}, u32[]{:S(2)}, u32[]{:S(2)}) collective-permute-start(bf16[4,360,128]{2,1,0:T(8,128)(2,1)S(1)} %bitcast.114), channel_id=1, source_target_pairs={{0,24},{8,16},{16,8},{24,0},{1,25},{9,17},{17,9},{25,1},{2,26},{10... | collective-permute-start | bytes 1105928 | tf_op jit(solution)/shard_map/ppermute | solution.py:11
  20.4 15.4 %all-gather.1 = bf16[1440,128]{1,0:T(8,128)(2,1)S(1)} all-gather(bf16[360,128]{1,0:T(8,128)(2,1)} %bitcast.119), channel_id=3, replica_groups=mesh['expert'=4,'ring'=4,'core'=2] {'ring'}, dimensions={0}, use_global_device_ids=true | all-gather | bytes 460800 | tf_op jit(solution)/shard_map/all_gather | solution.py:15
  35.9 2.4 %collective-permute-start.9 = (bf16[4,360,128]{2,1,0:T(8,128)(2,1)S(1)}, bf16[4,360,128]{2,1,0:T(8,128)(2,1)S(1)}, u32[]{:S(2)}, u32[]{:S(2)}) collective-permute-start(bf16[4,360,128]{2,1,0:T(8,128)(2,1)S(1)} %bitcast.110), channel_id=1, source_target_pairs={{0,24},{8,16},{16,8},{24,0},{1,25},{9,17},{17,9},{25,1},{2,26},{10... | collective-permute-start | bytes 1105928 | tf_op jit(solution)/shard_map/ppermute | solution.py:11
  40.7 5.6 %collective-permute-done.9 = bf16[4,360,128]{2,1,0:T(8,128)(2,1)S(1)} collective-permute-done((bf16[4,360,128]{2,1,0:T(8,128)(2,1)S(1)}, bf16[4,360,128]{2,1,0:T(8,128)(2,1)S(1)}, u32[]{:S(2)}, u32[]{:S(2)}) %collective-permute-start.9) | collective-permute-done | bytes 368672 | tf_op jit(solution)/shard_map/ppermute | solution.py:11
  46.3 3.8 %collective-permute-done.8 = bf16[4,360,128]{2,1,0:T(8,128)(2,1)S(1)} collective-permute-done((bf16[4,360,128]{2,1,0:T(8,128)(2,1)S(1)}, bf16[4,360,128]{2,1,0:T(8,128)(2,1)S(1)}, u32[]{:S(2)}, u32[]{:S(2)}) %collective-permute-start.8) | collective-permute-done | bytes 368672 | tf_op jit(solution)/shard_map/ppermute | solution.py:11
  51.7 1.6 %collective-permute-start.6 = (f32[2,128]{1,0:T(2,128)S(1)}, f32[2,128]{1,0:T(2,128)S(1)}, u32[]{:S(2)}, u32[]{:S(2)}) collective-permute-start(f32[2,128]{1,0:T(2,128)S(1)} %get-tuple-element.21), channel_id=1, source_target_pairs={{0,24},{8,16},{16,8},{24,0},{1,25},{9,17},{17,9},{25,1},{2,26},{10... | collective-permute-start | bytes 3080 | tf_op jit(solution)/shard_map/ppermute | solution.py:11
  58.3 3.7 %maximum_select_fusion = (bf16[4,2,360,512]{3,2,0,1:T(8,128)(2,1)S(1)}, bf16[4,2,360,512]{3,2,0,1:T(8,128)(2,1)S(1)}) fusion(bf16[4,1,360,512]{3,2,0,1:T(8,128)(2,1)} %bitcast.3, bf16[4,1,360,512]{3,2,0,1:T(8,128)(2,1)S(1)} %get-tuple-element.15, pred[]{:T(512)S(6)} %eq.8, bf16[4,1,360,512]{3,2,0,1:T(8,128)(2,1)S(1)} %get-tuple-element.13, ...), kind=kLoop, calls=%fused_computation.4 | loop fusion | flops 8847360 | bytes 11796481 | tf_op jit(solution)/shard_map/jit(_where)/select_n | solution.py:22
  62.2 4.8 %fusion.27 = f32[512,2,360]{0,2,1:T(8,128)S(1)} fusion(bf16[2880,512,1]{1,0,2:T(8,128)(2,1)S(1)} %bitcast.104, bf16[2,360,2880]{2,1,0:T(8,128)(2,1)} %param.11), kind=kOutput, calls=%fused_computation.54 | convolution fusion | flops 2123366400 | bytes 8570880 | tf_op jit(solution)/shard_map/efd,dt->eft/dot_general | solution.py:65
  67.1 2.4 %fusion.26 = f32[512,2,360]{0,2,1:T(8,128)S(1)} fusion(bf16[2880,512,1]{1,0,2:T(8,128)(2,1)S(1)} %bitcast.105, bf16[2,360,2880]{2,1,0:T(8,128)(2,1)S(1)} %bitcast.103), kind=kOutput, calls=%fused_computation.53 | convolution fusion | flops 2123366400 | bytes 8570880 | tf_op jit(solution)/shard_map/efd,dt->eft/dot_general | solution.py:65
  70.7 3.0 %multiply_convert_fusion = (bf16[2,360,512]{2,1,0:T(8,128)(2,1)S(1)}, bf16[2,360,512]{2,1,0:T(8,128)(2,1)S(1)}) fusion(f32[512,2,360]{0,2,1:T(8,128)S(1)} %fusion.27, f32[512,2,360]{0,2,1:T(8,128)S(1)} %fusion.26, f32[2,512]{1,0:T(2,128)S(1)} %pad_maximum_fusion.2, bf16[2880,512,1]{1,0,2:T(8,128)(2,1)S(1)} %bitcast.108, bf16[2,360,2880]{2,1,0:T(8,128)(2,1)S(1)} %bitcast.122), kind=kOutput, calls=%fused_computation.20 | convolution fusion | flops 2129264640 | bytes 11524096 | tf_op jit(solution)/shard_map/efd,dt->eft/dot_general | solution.py:65
  73.8 2.6 %fusion.28 = f32[512,2880,1]{0,1,2:T(8,128)S(1)} fusion(bf16[2,360,512]{2,1,0:T(8,128)(2,1)S(1)} %get-tuple-element.9, bf16[2,360,2880]{2,1,0:T(8,128)(2,1)S(1)} %bitcast.124), kind=kOutput, calls=%fused_computation.55 | convolution fusion | flops 2123366400 | bytes 10782720 | tf_op jit(solution)/shard_map/efd,eft->dt/dot_general | solution.py:76
  76.4 2.7 %bitcast_add_fusion = f32[512,2880]{0,1:T(8,128)S(1)} fusion(f32[512,2880,1]{0,1,2:T(8,128)S(1)} %fusion.28, bf16[2,360,512]{2,1,0:T(8,128)(2,1)S(1)} %get-tuple-element.8, bf16[2,360,2880]{2,1,0:T(8,128)(2,1)S(1)} %bitcast.103), kind=kOutput, calls=%fused_computation | convolution fusion | flops 2124840960 | bytes 16680960 | tf_op jit(solution)/shard_map/efd,eft->dt/dot_general | solution.py:77
  79.1 2.5 %copy-done = f32[512,2880]{0,1:T(8,128)} copy-done((f32[512,2880]{0,1:T(8,128)}, f32[512,2880]{0,1:T(8,128)S(1)}, u32[]{:S(2)}) %copy-start) | copy-done | bytes 5898264
  83.0 7.7 %convolution_convert_fusion = bf16[2,360,2880]{2,1,0:T(8,128)(2,1)} fusion(bf16[2880,512,1]{1,0,2:T(8,128)(2,1)} %bitcast.109, f32[512,2,360]{0,2,1:T(8,128)} %copy-done.10, f32[2,512]{1,0:T(2,128)S(1)} %pad_maximum_fusion.2, f32[512,2,360]{0,2,1:T(8,128)} %copy-done.9), kind=kOutput, calls=%fused_computation.1 | convolution fusion | flops 2128757760 | bytes 10049536 | tf_op jit(solution)/shard_map/eft,dt->efd/dot_general | solution.py:81
  90.7 2.1 %fusion.24 = (bf16[4,360,512]{2,1,0:T(8,128)(2,1)S(1)}, f32[4,360,512]{2,1,0:T(8,128)S(1)}) fusion(bf16[4,360,512]{2,1,0:T(8,128)(2,1)} %collective-permute-done.11, f32[4,2,360,512]{3,2,1,0:T(8,128)S(1)} %bitcast.101, s32[]{:T(128)S(6)} %select_n.68), kind=kLoop, calls=%fused_computation.51 | loop fusion | flops 2211840 | bytes 8847364 | tf_op jit(solution)/shard_map/convert_element_type | solution.py:33
  95.0 1.5 %collective-permute-start.12 = (bf16[4,360,128]{2,1,0:T(8,128)(2,1)S(1)}, bf16[4,360,128]{2,1,0:T(8,128)(2,1)S(1)}, u32[]{:S(2)}, u32[]{:S(2)}) collective-permute-start(bf16[4,360,128]{2,1,0:T(8,128)(2,1)S(1)} %get-tuple-element.10), channel_id=1, source_target_pairs={{0,8},{8,0},{16,24},{24,16},{1,9},{9,1},{17,25},{25,17},{2,10},{10... | collective-permute-start | bytes 1105928 | tf_op jit(solution)/shard_map/ppermute | solution.py:11
  96.5 4.5 %convolution_convert_fusion.2 = bf16[2,360,2880]{2,1,0:T(8,128)(2,1)} fusion(bf16[2,360,512]{2,1,0:T(8,128)(2,1)S(1)} %copy-done.8, bf16[2880,512,1]{1,0,2:T(8,128)(2,1)S(1)} %bitcast.106), kind=kOutput, calls=%fused_computation.3 | convolution fusion | flops 2125440000 | bytes 7833600 | tf_op jit(solution)/shard_map/eft,dt->efd/dot_general | solution.py:81
  101.0 4.3 %collective-permute-done.14 = bf16[4,360,128]{2,1,0:T(8,128)(2,1)S(1)} collective-permute-done((bf16[4,360,128]{2,1,0:T(8,128)(2,1)S(1)}, bf16[4,360,128]{2,1,0:T(8,128)(2,1)S(1)}, u32[]{:S(2)}, u32[]{:S(2)}) %collective-permute-start.14) | collective-permute-done | bytes 368672 | tf_op jit(solution)/shard_map/ppermute | solution.py:11
  105.3 7.5 %collective-permute-done.13 = bf16[4,360,128]{2,1,0:T(8,128)(2,1)S(1)} collective-permute-done((bf16[4,360,128]{2,1,0:T(8,128)(2,1)S(1)}, bf16[4,360,128]{2,1,0:T(8,128)(2,1)S(1)}, u32[]{:S(2)}, u32[]{:S(2)}) %collective-permute-start.13) | collective-permute-done | bytes 368672 | tf_op jit(solution)/shard_map/ppermute | solution.py:11
  113.0 2.4 %collective-permute-start.17 = (bf16[360,128]{1,0:T(8,128)(2,1)S(1)}, bf16[360,128]{1,0:T(8,128)(2,1)S(1)}, u32[]{:S(2)}, u32[]{:S(2)}) collective-permute-start(bf16[360,128]{1,0:T(8,128)(2,1)S(1)} %get-tuple-element.18), channel_id=1, source_target_pairs={{0,6},{2,4},{4,2},{6,0},{1,7},{3,5},{5,3},{7,1},{8,14},{10,12},{12... | collective-permute-start | bytes 276488 | tf_op jit(solution)/shard_map/ppermute | solution.py:11
  115.4 2.1 %collective-permute-start.15 = (bf16[360,128]{1,0:T(8,128)(2,1)S(1)}, bf16[360,128]{1,0:T(8,128)(2,1)S(1)}, u32[]{:S(2)}, u32[]{:S(2)}) collective-permute-start(bf16[360,128]{1,0:T(8,128)(2,1)S(1)} %get-tuple-element.17), channel_id=1, source_target_pairs={{0,2},{2,0},{4,6},{6,4},{1,3},{3,1},{5,7},{7,5},{8,10},{10,8},{12,... | collective-permute-start | bytes 276488 | tf_op jit(solution)/shard_map/ppermute | solution.py:11
  117.5 4.5 %convolution_convert_fusion.1 = bf16[2,360,2880]{2,1,0:T(8,128)(2,1)} fusion(bf16[2,360,512]{2,1,0:T(8,128)(2,1)S(1)} %copy-done.4, bf16[2880,512,1]{1,0,2:T(8,128)(2,1)S(1)} %bitcast.107), kind=kOutput, calls=%fused_computation.2 | convolution fusion | flops 2125440000 | bytes 7833600 | tf_op jit(solution)/shard_map/eft,dt->efd/dot_general | solution.py:81
  122.0 1.4 %collective-permute-done.16 = bf16[360,128]{1,0:T(8,128)(2,1)S(1)} collective-permute-done((bf16[360,128]{1,0:T(8,128)(2,1)S(1)}, bf16[360,128]{1,0:T(8,128)(2,1)S(1)}, u32[]{:S(2)}, u32[]{:S(2)}) %collective-permute-start.16) | collective-permute-done | bytes 92192 | tf_op jit(solution)/shard_map/ppermute | solution.py:11
  (73 shorter events, 15.8 us)
Async XLA Ops:
  16.9 21.9 %collective-permute-start.2 = (bf16[4,360,128]{2,1,0:T(8,128)(2,1)S(1)}, bf16[4,360,128]{2,1,0:T(8,128)(2,1)S(1)}, u32[]{:S(2)}, u32[]{:S(2)}) collective-permute-start(bf16[4,360,128]{2,1,0:T(8,128)(2,1)S(1)} %bitcast.114), channel_id=1, source_target_pairs={{0,24},{8,16},{16,8},{24,0},{1,25},{9,17},{17,9},{25,1},{2,26},{10... | collective-permute-start | bytes 1105928 | tf_op jit(solution)/shard_map/ppermute | solution.py:11
  19.4 20.0 %collective-permute-start.1 = (bf16[4,360,128]{2,1,0:T(8,128)(2,1)S(1)}, bf16[4,360,128]{2,1,0:T(8,128)(2,1)S(1)}, u32[]{:S(2)}, u32[]{:S(2)}) collective-permute-start(bf16[4,360,128]{2,1,0:T(8,128)(2,1)S(1)} %bitcast.115), channel_id=1, source_target_pairs={{0,16},{8,24},{16,0},{24,8},{1,17},{9,25},{17,1},{25,9},{2,18},{10... | collective-permute-start | bytes 1105928 | tf_op jit(solution)/shard_map/ppermute | solution.py:11
  19.9 19.5 %collective-permute-start = (bf16[4,360,128]{2,1,0:T(8,128)(2,1)S(1)}, bf16[4,360,128]{2,1,0:T(8,128)(2,1)S(1)}, u32[]{:S(2)}, u32[]{:S(2)}) collective-permute-start(bf16[4,360,128]{2,1,0:T(8,128)(2,1)S(1)} %bitcast.116), channel_id=1, source_target_pairs={{0,8},{8,0},{16,24},{24,16},{1,9},{9,1},{17,25},{25,17},{2,10},{10... | collective-permute-start | bytes 1105928 | tf_op jit(solution)/shard_map/ppermute | solution.py:11
  35.9 10.5 %collective-permute-start.9 = (bf16[4,360,128]{2,1,0:T(8,128)(2,1)S(1)}, bf16[4,360,128]{2,1,0:T(8,128)(2,1)S(1)}, u32[]{:S(2)}, u32[]{:S(2)}) collective-permute-start(bf16[4,360,128]{2,1,0:T(8,128)(2,1)S(1)} %bitcast.110), channel_id=1, source_target_pairs={{0,24},{8,16},{16,8},{24,0},{1,25},{9,17},{17,9},{25,1},{2,26},{10... | collective-permute-start | bytes 1105928 | tf_op jit(solution)/shard_map/ppermute | solution.py:11
  38.3 11.8 %collective-permute-start.8 = (bf16[4,360,128]{2,1,0:T(8,128)(2,1)S(1)}, bf16[4,360,128]{2,1,0:T(8,128)(2,1)S(1)}, u32[]{:S(2)}, u32[]{:S(2)}) collective-permute-start(bf16[4,360,128]{2,1,0:T(8,128)(2,1)S(1)} %bitcast.111), channel_id=1, source_target_pairs={{0,16},{8,24},{16,0},{24,8},{1,17},{9,25},{17,1},{25,9},{2,18},{10... | collective-permute-start | bytes 1105928 | tf_op jit(solution)/shard_map/ppermute | solution.py:11
  38.8 11.5 %collective-permute-start.7 = (bf16[4,360,128]{2,1,0:T(8,128)(2,1)S(1)}, bf16[4,360,128]{2,1,0:T(8,128)(2,1)S(1)}, u32[]{:S(2)}, u32[]{:S(2)}) collective-permute-start(bf16[4,360,128]{2,1,0:T(8,128)(2,1)S(1)} %bitcast.112), channel_id=1, source_target_pairs={{0,8},{8,0},{16,24},{24,16},{1,9},{9,1},{17,25},{25,17},{2,10},{10... | collective-permute-start | bytes 1105928 | tf_op jit(solution)/shard_map/ppermute | solution.py:11
  40.7 10.9 %copy-start.5 = (f32[128,4]{0,1:T(4,128)S(1)}, f32[128,4]{0,1:T(4,128)}, u32[]{:S(2)}) copy-start(f32[128,4]{0,1:T(4,128)} %param.9) | copy-start | bytes 6148
  40.7 10.9 %copy-start.6 = (s32[128,4]{0,1:T(4,128)S(1)}, s32[128,4]{0,1:T(4,128)}, u32[]{:S(2)}) copy-start(s32[128,4]{0,1:T(4,128)} %param.10) | copy-start | bytes 6148
  40.7 17.6 %collective-permute-start.3 = (bf16[4,360,512]{2,1,0:T(8,128)(2,1)}, bf16[4,360,512]{2,1,0:T(8,128)(2,1)}, u32[]{:S(2)}, u32[]{:S(2)}) collective-permute-start(bf16[4,360,512]{2,1,0:T(8,128)(2,1)} %get-tuple-element.16), channel_id=1, source_target_pairs={{0,1},{1,0},{2,3},{3,2},{4,5},{5,4},{6,7},{7,6},{8,9},{9,8},{10,11... | collective-permute-start | bytes 4423688 | tf_op jit(solution)/shard_map/ppermute | solution.py:11
  51.6 6.7 %collective-permute-start.10 = (bf16[4,360,512]{2,1,0:T(8,128)(2,1)}, bf16[4,360,512]{2,1,0:T(8,128)(2,1)}, u32[]{:S(2)}, u32[]{:S(2)}) collective-permute-start(bf16[4,360,512]{2,1,0:T(8,128)(2,1)} %get-tuple-element.14), channel_id=1, source_target_pairs={{0,1},{1,0},{2,3},{3,2},{4,5},{5,4},{6,7},{7,6},{8,9},{9,8},{10,11... | collective-permute-start | bytes 4423688 | tf_op jit(solution)/shard_map/ppermute | solution.py:11
  51.7 4.5 %collective-permute-start.6 = (f32[2,128]{1,0:T(2,128)S(1)}, f32[2,128]{1,0:T(2,128)S(1)}, u32[]{:S(2)}, u32[]{:S(2)}) collective-permute-start(f32[2,128]{1,0:T(2,128)S(1)} %get-tuple-element.21), channel_id=1, source_target_pairs={{0,24},{8,16},{16,8},{24,0},{1,25},{9,17},{17,9},{25,1},{2,26},{10... | collective-permute-start | bytes 3080 | tf_op jit(solution)/shard_map/ppermute | solution.py:11
  53.3 3.6 %collective-permute-start.5 = (f32[2,128]{1,0:T(2,128)S(1)}, f32[2,128]{1,0:T(2,128)S(1)}, u32[]{:S(2)}, u32[]{:S(2)}) collective-permute-start(f32[2,128]{1,0:T(2,128)S(1)} %get-tuple-element.22), channel_id=1, source_target_pairs={{0,16},{8,24},{16,0},{24,8},{1,17},{9,25},{17,1},{25,9},{2,18},{10... | collective-permute-start | bytes 3080 | tf_op jit(solution)/shard_map/ppermute | solution.py:11
  54.7 3.6 %collective-permute-start.4 = (f32[2,128]{1,0:T(2,128)S(1)}, f32[2,128]{1,0:T(2,128)S(1)}, u32[]{:S(2)}, u32[]{:S(2)}) collective-permute-start(f32[2,128]{1,0:T(2,128)S(1)} %get-tuple-element.23), channel_id=1, source_target_pairs={{0,8},{8,0},{16,24},{24,16},{1,9},{9,1},{17,25},{25,17},{2,10},{10... | collective-permute-start | bytes 3080 | tf_op jit(solution)/shard_map/ppermute | solution.py:11
  62.2 8.4 %slice-start.2 = ((s8[4239360]{0:T(1024)(128)(4,1)}), s8[4194304]{0:T(1024)(128)(4,1)S(1)}, s32[]{:S(2)}) async-start(s8[4239360]{0:T(1024)(128)(4,1)} %bitcast.121), calls=%async_computation.2 | async-start | bytes 8388608
  83.0 7.7 %collective-permute-start.11 = (bf16[4,360,512]{2,1,0:T(8,128)(2,1)}, bf16[4,360,512]{2,1,0:T(8,128)(2,1)}, u32[]{:S(2)}, u32[]{:S(2)}) collective-permute-start(bf16[4,360,512]{2,1,0:T(8,128)(2,1)} %fusion), channel_id=1, source_target_pairs={{0,1},{1,0},{2,3},{3,2},{4,5},{5,4},{6,7},{7,6},{8,9},{9,8},{10,11... | collective-permute-start | bytes 4423688 | tf_op jit(solution)/shard_map/ppermute | solution.py:11
  83.0 7.7 %copy-start.1 = (f32[512,2880]{0,1:T(8,128)S(1)}, f32[512,2880]{0,1:T(8,128)}, u32[]{:S(2)}) copy-start(f32[512,2880]{0,1:T(8,128)} %copy-done) | copy-start | bytes 17694724
  90.7 5.8 %copy-start.8 = (bf16[2,360,512]{2,1,0:T(8,128)(2,1)S(1)}, bf16[2,360,512]{2,1,0:T(8,128)(2,1)}, u32[]{:S(2)}) copy-start(bf16[2,360,512]{2,1,0:T(8,128)(2,1)} %copy-done.7) | copy-start | bytes 2211844
  92.9 12.4 %collective-permute-start.14 = (bf16[4,360,128]{2,1,0:T(8,128)(2,1)S(1)}, bf16[4,360,128]{2,1,0:T(8,128)(2,1)S(1)}, u32[]{:S(2)}, u32[]{:S(2)}) collective-permute-start(bf16[4,360,128]{2,1,0:T(8,128)(2,1)S(1)} %get-tuple-element.11), channel_id=1, source_target_pairs={{0,24},{8,16},{16,8},{24,0},{1,25},{9,17},{17,9},{25,1},{2,26},{10... | collective-permute-start | bytes 1105928 | tf_op jit(solution)/shard_map/ppermute | solution.py:11
  94.3 18.5 %collective-permute-start.13 = (bf16[4,360,128]{2,1,0:T(8,128)(2,1)S(1)}, bf16[4,360,128]{2,1,0:T(8,128)(2,1)S(1)}, u32[]{:S(2)}, u32[]{:S(2)}) collective-permute-start(bf16[4,360,128]{2,1,0:T(8,128)(2,1)S(1)} %get-tuple-element.12), channel_id=1, source_target_pairs={{0,16},{8,24},{16,0},{24,8},{1,17},{9,25},{17,1},{25,9},{2,18},{10... | collective-permute-start | bytes 1105928 | tf_op jit(solution)/shard_map/ppermute | solution.py:11
  95.0 17.8 %collective-permute-start.12 = (bf16[4,360,128]{2,1,0:T(8,128)(2,1)S(1)}, bf16[4,360,128]{2,1,0:T(8,128)(2,1)S(1)}, u32[]{:S(2)}, u32[]{:S(2)}) collective-permute-start(bf16[4,360,128]{2,1,0:T(8,128)(2,1)S(1)} %get-tuple-element.10), channel_id=1, source_target_pairs={{0,8},{8,0},{16,24},{24,16},{1,9},{9,1},{17,25},{25,17},{2,10},{10... | collective-permute-start | bytes 1105928 | tf_op jit(solution)/shard_map/ppermute | solution.py:11
  101.0 16.5 %copy-start.4 = (bf16[2,360,512]{2,1,0:T(8,128)(2,1)S(1)}, bf16[2,360,512]{2,1,0:T(8,128)(2,1)}, u32[]{:S(2)}) copy-start(bf16[2,360,512]{2,1,0:T(8,128)(2,1)} %copy-done.3) | copy-start | bytes 2211844
  113.0 9.0 %collective-permute-start.17 = (bf16[360,128]{1,0:T(8,128)(2,1)S(1)}, bf16[360,128]{1,0:T(8,128)(2,1)S(1)}, u32[]{:S(2)}, u32[]{:S(2)}) collective-permute-start(bf16[360,128]{1,0:T(8,128)(2,1)S(1)} %get-tuple-element.18), channel_id=1, source_target_pairs={{0,6},{2,4},{4,2},{6,0},{1,7},{3,5},{5,3},{7,1},{8,14},{10,12},{12... | collective-permute-start | bytes 276488 | tf_op jit(solution)/shard_map/ppermute | solution.py:11
  115.4 8.1 %collective-permute-start.16 = (bf16[360,128]{1,0:T(8,128)(2,1)S(1)}, bf16[360,128]{1,0:T(8,128)(2,1)S(1)}, u32[]{:S(2)}, u32[]{:S(2)}) collective-permute-start(bf16[360,128]{1,0:T(8,128)(2,1)S(1)} %get-tuple-element.19), channel_id=1, source_target_pairs={{0,4},{2,6},{4,0},{6,2},{1,5},{3,7},{5,1},{7,3},{8,12},{10,14},{12... | collective-permute-start | bytes 276488 | tf_op jit(solution)/shard_map/ppermute | solution.py:11
  115.4 8.1 %collective-permute-start.15 = (bf16[360,128]{1,0:T(8,128)(2,1)S(1)}, bf16[360,128]{1,0:T(8,128)(2,1)S(1)}, u32[]{:S(2)}, u32[]{:S(2)}) collective-permute-start(bf16[360,128]{1,0:T(8,128)(2,1)S(1)} %get-tuple-element.17), channel_id=1, source_target_pairs={{0,2},{2,0},{4,6},{6,4},{1,3},{3,1},{5,7},{7,5},{8,10},{10,8},{12,... | collective-permute-start | bytes 276488 | tf_op jit(solution)/shard_map/ppermute | solution.py:11
  (11 other events, 36.4 us)

commit v2 on v1

v2 whole, which is shorter than its diff:
```python
import jax
import jax.numpy as jnp
from jax import lax
from jax.sharding import Mesh
from jax.sharding import PartitionSpec as P

BF16, F32 = jnp.bfloat16, jnp.float32


def xor_send(a, axis, s):
    return lax.ppermute(a, axis, [(i, i ^ s) for i in range(lax.axis_size(axis))])


def ring_order(pieces):
    ring, bit = lax.axis_index("ring"), 1
    while bit < len(pieces):
        swap = (ring & bit) > 0
        pieces = [jnp.where(swap, pieces[i ^ bit], pieces[i]) for i in range(len(pieces))]
        bit *= 2
    return jnp.stack(pieces)


def ring_gather(own):
    return [own] + [xor_send(own, "ring", s) for s in range(1, lax.axis_size("ring"))]


def plane_gather(a):
    return [a] + [xor_send(a, "expert", s) for s in range(1, lax.axis_size("expert"))]


def both_cores(half):
    other = xor_send(half, "core", 1)
    first = lax.axis_index("core") == 0
    both = jnp.where(first, jnp.stack([half, other], 1), jnp.stack([other, half], 1))
    return both.reshape(-1, both.shape[-1])


def at(a, i):
    return lax.dynamic_index_in_dim(a, i, 0, False)


def swap_sum(part):
    core = lax.axis_index("core")
    part = part.reshape(lax.axis_size("ring"), 2, -1, part.shape[-1])
    keep = lax.dynamic_index_in_dim(part, core, 1, False)
    give = lax.dynamic_index_in_dim(part, 1 - core, 1, False)
    return keep, xor_send(give, "core", 1)


def plane_sum(keep, other, rows):
    chip = keep.astype(F32) + other.astype(F32)
    far = chip[:, :, rows:].astype(BF16)
    arrived = [
        xor_send(far[:, :, (s - 1) * rows : s * rows], "expert", s)
        for s in range(1, lax.axis_size("expert"))
    ]
    return chip[:, :, :rows], arrived


def ring_sum(mine):
    ring = lax.axis_index("ring")
    mine_b = mine.astype(BF16)
    home = at(mine, ring)
    for s in range(1, lax.axis_size("ring")):
        home = home + xor_send(at(mine_b, ring ^ s), "ring", s).astype(F32)
    return home.astype(BF16)


def body(tokens, grad_out, gates, routes, w_gate, w_up, w_down):
    groups = lax.axis_size("expert")
    local = w_gate.shape[0]
    rows = tokens.shape[0]
    group = lax.axis_index("expert")

    ids = jnp.arange(groups * local, dtype=jnp.int32)
    named = routes[None] == ids[:, None, None]
    weight = jnp.sum(jnp.where(named, gates[None], 0.0), -1)
    weight = weight.reshape(groups, local, rows)
    coef = [at(weight, group)]
    for s in range(1, groups):
        coef.append(xor_send(at(weight, group ^ s), "expert", s))

    def to_hidden(w, a):
        return jnp.einsum("efd,dt->eft", w, a, preferred_element_type=F32)

    x_own, g_own = tokens.T, grad_out.T
    x_ring = ring_order(ring_gather(x_own))
    x_ring, coef, g_own = lax.optimization_barrier((x_ring, coef, g_own))
    x_blocks = plane_gather(x_ring)
    g_ring = lax.all_gather(g_own, "ring", axis=0)
    x_blocks, g_ring = lax.optimization_barrier((x_blocks, g_ring))
    g_blocks = plane_gather(g_ring)
    x = both_cores(jnp.concatenate(x_blocks, -1))
    coef = jnp.concatenate(coef, -1)[:, None, :]
    pre_gate = to_hidden(w_gate, x)
    pre_up = to_hidden(w_up, x)
    sig = jax.nn.sigmoid(1.702 * pre_gate)
    glu = pre_gate * sig
    act = (glu * (pre_up + 1.0) * coef).astype(BF16)
    slope = (pre_up + 1.0) * (sig + 1.702 * pre_gate * sig * (1.0 - sig))
    g_blocks, act, glu, slope = lax.optimization_barrier((g_blocks, act, glu, slope))
    g = both_cores(jnp.concatenate(g_blocks, -1))

    d_act = to_hidden(w_down, g) * coef
    d_pre_gate = (d_act * slope).astype(BF16)
    d_pre_up = (d_act * glu).astype(BF16)

    def to_weight(a, b):
        return jnp.einsum("eft,dt->efd", a, b, preferred_element_type=F32).astype(BF16)

    term = jnp.einsum("efd,eft->dt", w_gate, d_pre_gate, preferred_element_type=F32)
    term = term + jnp.einsum("efd,eft->dt", w_up, d_pre_up, preferred_element_type=F32)
    keep, other = swap_sum(term.astype(BF16))
    keep, other, act, d_pre_gate, d_pre_up = lax.optimization_barrier((keep, other, act, d_pre_gate, d_pre_up))
    own, arrived = plane_sum(keep, other, rows)
    d_gate, d_up, d_down = to_weight(d_pre_gate, x), to_weight(d_pre_up, x), to_weight(act, g)
    own, arrived, d_gate, d_up, d_down = lax.optimization_barrier((own, arrived, d_gate, d_up, d_down))
    for a in arrived:
        own = own + a.astype(F32)
    return ring_sum(own).T, d_gate, d_up, d_down


def solution(mesh):
    groups, shards = mesh.shape["expert"], mesh.shape["etp"]
    split = Mesh(mesh.devices.reshape(groups, shards // 2, 2), ("expert", "ring", "core"))
    etp = ("ring", "core")
    hidden = P("expert", etp, None)
    return jax.shard_map(
        body,
        mesh=split,
        in_specs=(P("expert", etp), P("expert", etp), P("expert", None), P("expert", None), hidden, hidden, hidden),
        out_specs=(P("expert", etp), hidden, hidden, hidden),
        check_vma=False,
    )
```

time: 124 us -> 108 us (0.87)
  blocking collectives: 31.7 us -> 16.1 us
  starting transfers between devices: 18.5 us -> 25.9 us
  other arithmetic: 9.29 us -> 4.38 us
  waiting for transfers between devices: 25.8 us -> 21.2 us
  matrix products: 32.3 us -> 36.6 us
  local copies, waits for them, and re-layouts: 5.48 us -> 2.48 us
    all_gather x2 -> x1, blocking collectives: 31.7 us -> 16.1 us  [body(): g_ring = lax.all_gather(g_own, 'ring', axis=0)]
    dot_general x3, matrix products: 10.3 us -> 17.8 us  [to_hidden(): return jnp.einsum('efd,dt->eft', w, a, preferred_element_type=F32)]
    ppermute x18 -> x21, starting transfers between devices: 18.5 us -> 25.9 us  [xor_send(): lax.ppermute(a, axis, [(i, i ^ s) for i in range(lax.axis_size(axis))])]
    ppermute x18 -> x21, waiting for transfers between devices: 25.8 us -> 21.2 us  [xor_send(): lax.ppermute(a, axis, [(i, i ^ s) for i in range(lax.axis_size(axis))])]
    dot_general x3, matrix products: 16.7 us -> 13.6 us  [to_weight(): jnp.einsum('eft,dt->efd', a, b, preferred_element_type=F32).astype(BF16)]
    unnamed x34 -> x36, local copies, waits for them, and re-layouts: 3.42 us -> 0.57 us
    select_n x1 -> x2, other arithmetic: 3.66 us -> 1.15 us  [both_cores(): jnp.where(first, jnp.stack([half, other], 1), jnp.stack([other, half], 1))]
    convert_element_type x2 -> x1, other arithmetic: 2.26 us -> 0.2 us  [ring_sum(): mine_b = mine.astype(BF16)]
  transfers between devices with their start and end apart: 18 -> 21, of which waited for: 9 -> 8; matrix products, arithmetic and copies ran while one was open for 16% -> 25% of each run, Pallas kernels for 0% -> 0%
where the time goes in v2:
time: 108 us
  matrix products  36.6 us (34%)
  starting transfers between devices  25.9 us (24%)
  waiting for transfers between devices  21.2 us (20%)
  blocking collectives  16.1 us (15%)
  other arithmetic  4.38 us (4%)
  local copies, waits for them, and re-layouts  2.48 us (2%)
    ppermute x21, starting transfers between devices, xor_send(): lax.ppermute(a, axis, [(i, i ^ s) for i in range(lax.axis_size(axis))])  25.9 us
    ppermute x21, waiting for transfers between devices, xor_send(): lax.ppermute(a, axis, [(i, i ^ s) for i in range(lax.axis_size(axis))])  21.2 us
    dot_general x3, matrix products, to_hidden(): return jnp.einsum('efd,dt->eft', w, a, preferred_element_type=F32)  17.8 us
    all_gather x1, blocking collectives, body(): g_ring = lax.all_gather(g_own, 'ring', axis=0)  16.1 us
    dot_general x3, matrix products, to_weight(): jnp.einsum('eft,dt->efd', a, b, preferred_element_type=F32).astype(BF16)  13.6 us
    dot_general x1, matrix products, body(): jnp.einsum('efd,eft->dt', w_up, d_pre_up, preferred_element_type=F32)  2.62 us
    dot_general x1, matrix products, body(): jnp.einsum('efd,eft->dt', w_gate, d_pre_gate, preferred_element_type=F32)  2.62 us
  transfers between devices with their start and end apart: 21, of which 8 were waited for; matrix products, arithmetic and copies ran while one was open for 25% of the time, Pallas kernels for 0%

profile of v2, /device:TPU:0, one launch (start us, length us, event | category | flops | bytes accessed | tf_op | source)
XLA Modules:
  0.0 107.7 jit_solution(14208860797423952505)
XLA Ops:
  0.6 5.1 %collective-permute-start = (bf16[360,128]{1,0:T(8,128)(2,1)}, bf16[360,128]{1,0:T(8,128)(2,1)S(1)}, u32[]{:S(2)}, u32[]{:S(2)}) collective-permute-start(bf16[360,128]{1,0:T(8,128)(2,1)} %bitcast.119), channel_id=1, source_target_pairs={{0,6},{2,4},{4,2},{6,0},{1,7},{3,5},{5,3},{7,1},{8,14},{10,12},{12... | collective-permute-start | bytes 276488 | tf_op jit(solution)/shard_map/ppermute | solution.py:11
  7.1 1.7 %collective-permute-start.3 = (f32[2,128]{1,0:T(2,128)S(1)}, f32[2,128]{1,0:T(2,128)S(1)}, u32[]{:S(2)}, u32[]{:S(2)}) collective-permute-start(f32[2,128]{1,0:T(2,128)S(1)} %get-tuple-element.87), channel_id=1, source_target_pairs={{0,8},{8,0},{16,24},{24,16},{1,9},{9,1},{17,25},{25,17},{2,10},{10... | collective-permute-start | bytes 3080 | tf_op jit(solution)/shard_map/ppermute | solution.py:11
  8.8 1.5 %collective-permute-start.4 = (f32[2,128]{1,0:T(2,128)S(1)}, f32[2,128]{1,0:T(2,128)S(1)}, u32[]{:S(2)}, u32[]{:S(2)}) collective-permute-start(f32[2,128]{1,0:T(2,128)S(1)} %get-tuple-element.86), channel_id=1, source_target_pairs={{0,16},{8,24},{16,0},{24,8},{1,17},{9,25},{17,1},{25,9},{2,18},{10... | collective-permute-start | bytes 3080 | tf_op jit(solution)/shard_map/ppermute | solution.py:11
  10.3 1.6 %collective-permute-start.5 = (f32[2,128]{1,0:T(2,128)S(1)}, f32[2,128]{1,0:T(2,128)S(1)}, u32[]{:S(2)}, u32[]{:S(2)}) collective-permute-start(f32[2,128]{1,0:T(2,128)S(1)} %get-tuple-element.85), channel_id=1, source_target_pairs={{0,24},{8,16},{16,8},{24,0},{1,25},{9,17},{17,9},{25,1},{2,26},{10... | collective-permute-start | bytes 3080 | tf_op jit(solution)/shard_map/ppermute | solution.py:11
  11.9 1.8 %collective-permute-done.1 = bf16[360,128]{1,0:T(8,128)(2,1)S(1)} collective-permute-done((bf16[360,128]{1,0:T(8,128)(2,1)}, bf16[360,128]{1,0:T(8,128)(2,1)S(1)}, u32[]{:S(2)}, u32[]{:S(2)}) %collective-permute-start.1) | collective-permute-done | bytes 92192 | tf_op jit(solution)/shard_map/ppermute | solution.py:11
  14.8 1.5 %collective-permute-start.6 = (bf16[4,360,128]{2,1,0:T(8,128)(2,1)S(1)}, bf16[4,360,128]{2,1,0:T(8,128)(2,1)S(1)}, u32[]{:S(2)}, u32[]{:S(2)}) collective-permute-start(bf16[4,360,128]{2,1,0:T(8,128)(2,1)S(1)} %pad_maximum_fusion), channel_id=1, source_target_pairs={{0,8},{8,0},{16,24},{24,16},{1,9},{9,1},{17,25},{25,17},{2,10},{10... | collective-permute-start | bytes 1105928 | tf_op jit(solution)/shard_map/ppermute | solution.py:11
  18.3 16.1 %all-gather = bf16[1440,128]{1,0:T(8,128)(2,1)S(1)} all-gather(bf16[360,128]{1,0:T(8,128)(2,1)} %bitcast.118), channel_id=2, replica_groups=mesh['expert'=4,'ring'=4,'core'=2] {'ring'}, dimensions={0}, use_global_device_ids=true | all-gather | bytes 460800 | tf_op jit(solution)/shard_map/all_gather | solution.py:90
  34.9 1.6 %collective-permute-start.9 = (bf16[4,360,128]{2,1,0:T(8,128)(2,1)S(1)}, bf16[4,360,128]{2,1,0:T(8,128)(2,1)S(1)}, u32[]{:S(2)}, u32[]{:S(2)}) collective-permute-start(bf16[4,360,128]{2,1,0:T(8,128)(2,1)S(1)} %bitcast.112), channel_id=1, source_target_pairs={{0,8},{8,0},{16,24},{24,16},{1,9},{9,1},{17,25},{25,17},{2,10},{10... | collective-permute-start | bytes 1105928 | tf_op jit(solution)/shard_map/ppermute | solution.py:11
  36.5 1.5 %collective-permute-start.10 = (bf16[4,360,128]{2,1,0:T(8,128)(2,1)S(1)}, bf16[4,360,128]{2,1,0:T(8,128)(2,1)S(1)}, u32[]{:S(2)}, u32[]{:S(2)}) collective-permute-start(bf16[4,360,128]{2,1,0:T(8,128)(2,1)S(1)} %bitcast.113), channel_id=1, source_target_pairs={{0,16},{8,24},{16,0},{24,8},{1,17},{9,25},{17,1},{25,9},{2,18},{10... | collective-permute-start | bytes 1105928 | tf_op jit(solution)/shard_map/ppermute | solution.py:11
  39.0 6.0 %fusion.14 = f32[512,2,360]{0,2,1:T(8,128)S(1)} fusion(bf16[2880,512,1]{1,0,2:T(8,128)(2,1)S(1)} %bitcast.104, bf16[2,360,2880]{2,1,0:T(8,128)(2,1)} %param.12), kind=kOutput, calls=%fused_computation.60 | convolution fusion | flops 2123366400 | bytes 8570880 | tf_op jit(solution)/shard_map/efd,dt->eft/dot_general | solution.py:84
  45.0 4.9 %bitcast_multiply_fusion.1 = (f32[2,360,512]{2,1,0:T(8,128)}, bf16[2,360,512]{2,1,0:T(8,128)(2,1)}, f32[2,360,512]{2,1,0:T(8,128)}) fusion(f32[512,2,360]{0,2,1:T(8,128)S(1)} %fusion.14, f32[2,512]{1,0:T(2,128)S(1)} %pad_maximum_fusion.1, bf16[2880,512,1]{1,0,2:T(8,128)(2,1)S(1)} %bitcast.105, bf16[2,360,2880]{2,1,0:T(8,128)(2,1)S(1)} %bitcast.124), kind=kOutput, calls=%fused_computation.9 | convolution fusion | flops 2128527360 | bytes 12261376 | tf_op jit(solution)/shard_map/efd,dt->eft/dot_general | solution.py:84
  49.9 5.1 %collective-permute-done.10 = bf16[4,360,128]{2,1,0:T(8,128)(2,1)S(1)} collective-permute-done((bf16[4,360,128]{2,1,0:T(8,128)(2,1)S(1)}, bf16[4,360,128]{2,1,0:T(8,128)(2,1)S(1)}, u32[]{:S(2)}, u32[]{:S(2)}) %collective-permute-start.10) | collective-permute-done | bytes 368672 | tf_op jit(solution)/shard_map/ppermute | solution.py:11
  55.5 3.3 %collective-permute-done.13 = bf16[4,360,512]{2,1,0:T(8,128)(2,1)S(1)} collective-permute-done((bf16[4,360,512]{2,1,0:T(8,128)(2,1)S(1)}, bf16[4,360,512]{2,1,0:T(8,128)(2,1)S(1)}, u32[]{:S(2)}, u32[]{:S(2)}) %collective-permute-start.13) | collective-permute-done | bytes 1474592 | tf_op jit(solution)/shard_map/ppermute | solution.py:11
  59.4 6.9 %multiply_convert_fusion = (bf16[2,360,512]{2,1,0:T(8,128)(2,1)S(1)}, bf16[2,360,512]{2,1,0:T(8,128)(2,1)S(1)}) fusion(f32[2,360,512]{2,1,0:T(8,128)} %get-tuple-element.50, f32[2,360,512]{2,1,0:T(8,128)} %get-tuple-element.49, f32[2,512]{1,0:T(2,128)S(1)} %pad_maximum_fusion.1, bf16[2880,512,1]{1,0,2:T(8,128)(2,1)S(1)} %bitcast.108, ...), kind=kOutput, calls=%fused_computation.17 | convolution fusion | flops 2125209600 | bytes 11524096 | tf_op jit(solution)/shard_map/efd,dt->eft/dot_general | solution.py:84
  66.4 2.6 %fusion.15 = f32[512,2880,1]{0,1,2:T(8,128)S(1)} fusion(bf16[2,360,512]{2,1,0:T(8,128)(2,1)S(1)} %get-tuple-element.54, bf16[2,360,2880]{2,1,0:T(8,128)(2,1)S(1)} %bitcast.126), kind=kOutput, calls=%fused_computation.61 | convolution fusion | flops 2123366400 | bytes 10782720 | tf_op jit(solution)/shard_map/efd,eft->dt/dot_general | solution.py:111
  69.1 2.6 %fusion = bf16[512,2880]{0,1:T(8,128)(2,1)S(1)} fusion(f32[512,2880,1]{0,1,2:T(8,128)S(1)} %fusion.15, bf16[2,360,512]{2,1,0:T(8,128)(2,1)S(1)} %get-tuple-element.55, bf16[2,360,2880]{2,1,0:T(8,128)(2,1)S(1)} %bitcast.128), kind=kOutput, calls=%fused_computation.1 | convolution fusion | flops 2126315520 | bytes 13731840 | tf_op jit(solution)/shard_map/efd,eft->dt/dot_general | solution.py:112
  73.2 3.4 %collective-permute-done.14 = bf16[4,360,512]{2,1,0:T(8,128)(2,1)S(1)} collective-permute-done((bf16[4,360,512]{2,1,0:T(8,128)(2,1)}, bf16[4,360,512]{2,1,0:T(8,128)(2,1)S(1)}, u32[]{:S(2)}, u32[]{:S(2)}) %collective-permute-start.14) | collective-permute-done | bytes 1474592 | tf_op jit(solution)/shard_map/ppermute | solution.py:11
  81.1 4.5 %convolution_convert_fusion.2 = bf16[2,360,2880]{2,1,0:T(8,128)(2,1)} fusion(bf16[2,360,512]{2,1,0:T(8,128)(2,1)S(1)} %copy-done.5, bf16[2880,512,1]{1,0,2:T(8,128)(2,1)S(1)} %bitcast.106), kind=kOutput, calls=%fused_computation.4 | convolution fusion | flops 2125440000 | bytes 7833600 | tf_op jit(solution)/shard_map/eft,dt->efd/dot_general | solution.py:109
  85.6 4.5 %convolution_convert_fusion.1 = bf16[2,360,2880]{2,1,0:T(8,128)(2,1)} fusion(bf16[2,360,512]{2,1,0:T(8,128)(2,1)S(1)} %copy-done.7, bf16[2880,512,1]{1,0,2:T(8,128)(2,1)S(1)} %bitcast.107), kind=kOutput, calls=%fused_computation.3 | convolution fusion | flops 2125440000 | bytes 7833600 | tf_op jit(solution)/shard_map/eft,dt->efd/dot_general | solution.py:109
  90.1 4.5 %convolution_convert_fusion = bf16[2,360,2880]{2,1,0:T(8,128)(2,1)} fusion(bf16[2,360,512]{2,1,0:T(8,128)(2,1)S(1)} %copy-done.8, bf16[2880,512,1]{1,0,2:T(8,128)(2,1)S(1)} %bitcast.109), kind=kOutput, calls=%fused_computation.2 | convolution fusion | flops 2125440000 | bytes 7833600 | tf_op jit(solution)/shard_map/eft,dt->efd/dot_general | solution.py:109
  95.4 1.6 %collective-permute-done.17 = bf16[4,360,128]{2,1,0:T(8,128)(2,1)S(1)} collective-permute-done((bf16[4,360,128]{2,1,0:T(8,128)(2,1)S(1)}, bf16[4,360,128]{2,1,0:T(8,128)(2,1)S(1)}, u32[]{:S(2)}, u32[]{:S(2)}) %collective-permute-start.17) | collective-permute-done | bytes 368672 | tf_op jit(solution)/shard_map/ppermute | solution.py:11
  98.8 3.0 %collective-permute-start.18 = (bf16[360,128]{1,0:T(8,128)(2,1)S(1)}, bf16[360,128]{1,0:T(8,128)(2,1)S(1)}, u32[]{:S(2)}, u32[]{:S(2)}) collective-permute-start(bf16[360,128]{1,0:T(8,128)(2,1)S(1)} %get-tuple-element.78), channel_id=1, source_target_pairs={{0,2},{2,0},{4,6},{6,4},{1,3},{3,1},{5,7},{7,5},{8,10},{10,8},{12,... | collective-permute-start | bytes 276488 | tf_op jit(solution)/shard_map/ppermute | solution.py:11
  101.8 3.2 %collective-permute-done.20 = bf16[360,128]{1,0:T(8,128)(2,1)S(1)} collective-permute-done((bf16[360,128]{1,0:T(8,128)(2,1)S(1)}, bf16[360,128]{1,0:T(8,128)(2,1)S(1)}, u32[]{:S(2)}, u32[]{:S(2)}) %collective-permute-start.20) | collective-permute-done | bytes 92192 | tf_op jit(solution)/shard_map/ppermute | solution.py:11
  104.9 2.1 %collective-permute-done.19 = bf16[360,128]{1,0:T(8,128)(2,1)S(1)} collective-permute-done((bf16[360,128]{1,0:T(8,128)(2,1)S(1)}, bf16[360,128]{1,0:T(8,128)(2,1)S(1)}, u32[]{:S(2)}, u32[]{:S(2)}) %collective-permute-start.19) | collective-permute-done | bytes 92192 | tf_op jit(solution)/shard_map/ppermute | solution.py:11
  (82 shorter events, 16.1 us)
Async XLA Ops:
  0.6 9.7 %collective-permute-start = (bf16[360,128]{1,0:T(8,128)(2,1)}, bf16[360,128]{1,0:T(8,128)(2,1)S(1)}, u32[]{:S(2)}, u32[]{:S(2)}) collective-permute-start(bf16[360,128]{1,0:T(8,128)(2,1)} %bitcast.119), channel_id=1, source_target_pairs={{0,6},{2,4},{4,2},{6,0},{1,7},{3,5},{5,3},{7,1},{8,14},{10,12},{12... | collective-permute-start | bytes 276488 | tf_op jit(solution)/shard_map/ppermute | solution.py:11
  5.7 7.9 %collective-permute-start.1 = (bf16[360,128]{1,0:T(8,128)(2,1)}, bf16[360,128]{1,0:T(8,128)(2,1)S(1)}, u32[]{:S(2)}, u32[]{:S(2)}) collective-permute-start(bf16[360,128]{1,0:T(8,128)(2,1)} %bitcast.120), channel_id=1, source_target_pairs={{0,4},{2,6},{4,0},{6,2},{1,5},{3,7},{5,1},{7,3},{8,12},{10,14},{12... | collective-permute-start | bytes 276488 | tf_op jit(solution)/shard_map/ppermute | solution.py:11
  5.7 7.9 %collective-permute-start.2 = (bf16[360,128]{1,0:T(8,128)(2,1)}, bf16[360,128]{1,0:T(8,128)(2,1)S(1)}, u32[]{:S(2)}, u32[]{:S(2)}) collective-permute-start(bf16[360,128]{1,0:T(8,128)(2,1)} %bitcast.121), channel_id=1, source_target_pairs={{0,2},{2,0},{4,6},{6,4},{1,3},{3,1},{5,7},{7,5},{8,10},{10,8},{12,... | collective-permute-start | bytes 276488 | tf_op jit(solution)/shard_map/ppermute | solution.py:11
  7.1 7.6 %collective-permute-start.3 = (f32[2,128]{1,0:T(2,128)S(1)}, f32[2,128]{1,0:T(2,128)S(1)}, u32[]{:S(2)}, u32[]{:S(2)}) collective-permute-start(f32[2,128]{1,0:T(2,128)S(1)} %get-tuple-element.87), channel_id=1, source_target_pairs={{0,8},{8,0},{16,24},{24,16},{1,9},{9,1},{17,25},{25,17},{2,10},{10... | collective-permute-start | bytes 3080 | tf_op jit(solution)/shard_map/ppermute | solution.py:11
  8.8 6.0 %collective-permute-start.4 = (f32[2,128]{1,0:T(2,128)S(1)}, f32[2,128]{1,0:T(2,128)S(1)}, u32[]{:S(2)}, u32[]{:S(2)}) collective-permute-start(f32[2,128]{1,0:T(2,128)S(1)} %get-tuple-element.86), channel_id=1, source_target_pairs={{0,16},{8,24},{16,0},{24,8},{1,17},{9,25},{17,1},{25,9},{2,18},{10... | collective-permute-start | bytes 3080 | tf_op jit(solution)/shard_map/ppermute | solution.py:11
  10.3 4.5 %collective-permute-start.5 = (f32[2,128]{1,0:T(2,128)S(1)}, f32[2,128]{1,0:T(2,128)S(1)}, u32[]{:S(2)}, u32[]{:S(2)}) collective-permute-start(f32[2,128]{1,0:T(2,128)S(1)} %get-tuple-element.85), channel_id=1, source_target_pairs={{0,24},{8,16},{16,8},{24,0},{1,25},{9,17},{17,9},{25,1},{2,26},{10... | collective-permute-start | bytes 3080 | tf_op jit(solution)/shard_map/ppermute | solution.py:11
  14.8 19.6 %collective-permute-start.6 = (bf16[4,360,128]{2,1,0:T(8,128)(2,1)S(1)}, bf16[4,360,128]{2,1,0:T(8,128)(2,1)S(1)}, u32[]{:S(2)}, u32[]{:S(2)}) collective-permute-start(bf16[4,360,128]{2,1,0:T(8,128)(2,1)S(1)} %pad_maximum_fusion), channel_id=1, source_target_pairs={{0,8},{8,0},{16,24},{24,16},{1,9},{9,1},{17,25},{25,17},{2,10},{10... | collective-permute-start | bytes 1105928 | tf_op jit(solution)/shard_map/ppermute | solution.py:11
  16.3 18.1 %collective-permute-start.7 = (bf16[4,360,128]{2,1,0:T(8,128)(2,1)S(1)}, bf16[4,360,128]{2,1,0:T(8,128)(2,1)S(1)}, u32[]{:S(2)}, u32[]{:S(2)}) collective-permute-start(bf16[4,360,128]{2,1,0:T(8,128)(2,1)S(1)} %pad_maximum_fusion), channel_id=1, source_target_pairs={{0,16},{8,24},{16,0},{24,8},{1,17},{9,25},{17,1},{25,9},{2,18},{10... | collective-permute-start | bytes 1105928 | tf_op jit(solution)/shard_map/ppermute | solution.py:11
  17.9 16.6 %collective-permute-start.8 = (bf16[4,360,128]{2,1,0:T(8,128)(2,1)S(1)}, bf16[4,360,128]{2,1,0:T(8,128)(2,1)S(1)}, u32[]{:S(2)}, u32[]{:S(2)}) collective-permute-start(bf16[4,360,128]{2,1,0:T(8,128)(2,1)S(1)} %pad_maximum_fusion), channel_id=1, source_target_pairs={{0,24},{8,16},{16,8},{24,0},{1,25},{9,17},{17,9},{25,1},{2,26},{10... | collective-permute-start | bytes 1105928 | tf_op jit(solution)/shard_map/ppermute | solution.py:11
  34.8 3.7 %collective-permute-start.12 = (bf16[4,360,512]{2,1,0:T(8,128)(2,1)S(1)}, bf16[4,360,512]{2,1,0:T(8,128)(2,1)S(1)}, u32[]{:S(2)}, u32[]{:S(2)}) collective-permute-start(bf16[4,360,512]{2,1,0:T(8,128)(2,1)S(1)} %constant_dynamic-update-slice_fusion), channel_id=1, source_target_pairs={{0,1},{1,0},{2,3},{3,2},{4,5},{5,4},{6,7},{7,6},{8,9},{9,8},{10,11... | collective-permute-start | bytes 4423688 | tf_op jit(solution)/shard_map/ppermute | solution.py:11
  34.9 15.0 %collective-permute-start.9 = (bf16[4,360,128]{2,1,0:T(8,128)(2,1)S(1)}, bf16[4,360,128]{2,1,0:T(8,128)(2,1)S(1)}, u32[]{:S(2)}, u32[]{:S(2)}) collective-permute-start(bf16[4,360,128]{2,1,0:T(8,128)(2,1)S(1)} %bitcast.112), channel_id=1, source_target_pairs={{0,8},{8,0},{16,24},{24,16},{1,9},{9,1},{17,25},{25,17},{2,10},{10... | collective-permute-start | bytes 1105928 | tf_op jit(solution)/shard_map/ppermute | solution.py:11
  36.5 18.5 %collective-permute-start.10 = (bf16[4,360,128]{2,1,0:T(8,128)(2,1)S(1)}, bf16[4,360,128]{2,1,0:T(8,128)(2,1)S(1)}, u32[]{:S(2)}, u32[]{:S(2)}) collective-permute-start(bf16[4,360,128]{2,1,0:T(8,128)(2,1)S(1)} %bitcast.113), channel_id=1, source_target_pairs={{0,16},{8,24},{16,0},{24,8},{1,17},{9,25},{17,1},{25,9},{2,18},{10... | collective-permute-start | bytes 1105928 | tf_op jit(solution)/shard_map/ppermute | solution.py:11
  38.0 17.0 %collective-permute-start.11 = (bf16[4,360,128]{2,1,0:T(8,128)(2,1)S(1)}, bf16[4,360,128]{2,1,0:T(8,128)(2,1)S(1)}, u32[]{:S(2)}, u32[]{:S(2)}) collective-permute-start(bf16[4,360,128]{2,1,0:T(8,128)(2,1)S(1)} %bitcast.114), channel_id=1, source_target_pairs={{0,24},{8,16},{16,8},{24,0},{1,25},{9,17},{17,9},{25,1},{2,26},{10... | collective-permute-start | bytes 1105928 | tf_op jit(solution)/shard_map/ppermute | solution.py:11
  55.4 3.3 %collective-permute-start.13 = (bf16[4,360,512]{2,1,0:T(8,128)(2,1)S(1)}, bf16[4,360,512]{2,1,0:T(8,128)(2,1)S(1)}, u32[]{:S(2)}, u32[]{:S(2)}) collective-permute-start(bf16[4,360,512]{2,1,0:T(8,128)(2,1)S(1)} %constant_dynamic-update-slice_fusion.4), channel_id=1, source_target_pairs={{0,1},{1,0},{2,3},{3,2},{4,5},{5,4},{6,7},{7,6},{8,9},{9,8},{10,11... | collective-permute-start | bytes 4423688 | tf_op jit(solution)/shard_map/ppermute | solution.py:11
  58.7 7.7 %slice-start.2 = ((s8[4239360]{0:T(1024)(128)(4,1)}), s8[4194304]{0:T(1024)(128)(4,1)S(1)}, s32[]{:S(2)}) async-start(s8[4239360]{0:T(1024)(128)(4,1)} %bitcast.125), calls=%async_computation.2 | async-start | bytes 8388608
  58.7 10.4 %slice-start.4 = ((s8[4239360]{0:T(1024)(128)(4,1)}), s8[4194304]{0:T(1024)(128)(4,1)S(1)}, s32[]{:S(2)}) async-start(s8[4239360]{0:T(1024)(128)(4,1)} %bitcast.127), calls=%async_computation.4 | async-start | bytes 8388608
  59.4 9.7 %slice-start.5 = ((s8[4239360]{0:T(1024)(128)(4,1)}), s8[45056]{0:T(1024)(128)(4,1)S(1)}, s32[]{:S(2)}) async-start(s8[4239360]{0:T(1024)(128)(4,1)} %bitcast.127), calls=%async_computation.5 | async-start | bytes 90112
  73.1 3.5 %collective-permute-start.14 = (bf16[4,360,512]{2,1,0:T(8,128)(2,1)}, bf16[4,360,512]{2,1,0:T(8,128)(2,1)S(1)}, u32[]{:S(2)}, u32[]{:S(2)}) collective-permute-start(bf16[4,360,512]{2,1,0:T(8,128)(2,1)} %get-tuple-element.68), channel_id=1, source_target_pairs={{0,1},{1,0},{2,3},{3,2},{4,5},{5,4},{6,7},{7,6},{8,9},{9,8},{10,11... | collective-permute-start | bytes 4423688 | tf_op jit(solution)/shard_map/ppermute | solution.py:11
  77.5 17.1 %collective-permute-start.15 = (bf16[4,360,128]{2,1,0:T(8,128)(2,1)S(1)}, bf16[4,360,128]{2,1,0:T(8,128)(2,1)S(1)}, u32[]{:S(2)}, u32[]{:S(2)}) collective-permute-start(bf16[4,360,128]{2,1,0:T(8,128)(2,1)S(1)} %get-tuple-element.74), channel_id=1, source_target_pairs={{0,8},{8,0},{16,24},{24,16},{1,9},{9,1},{17,25},{25,17},{2,10},{10... | collective-permute-start | bytes 1105928 | tf_op jit(solution)/shard_map/ppermute | solution.py:11
  78.8 16.6 %collective-permute-start.16 = (bf16[4,360,128]{2,1,0:T(8,128)(2,1)S(1)}, bf16[4,360,128]{2,1,0:T(8,128)(2,1)S(1)}, u32[]{:S(2)}, u32[]{:S(2)}) collective-permute-start(bf16[4,360,128]{2,1,0:T(8,128)(2,1)S(1)} %get-tuple-element.73), channel_id=1, source_target_pairs={{0,16},{8,24},{16,0},{24,8},{1,17},{9,25},{17,1},{25,9},{2,18},{10... | collective-permute-start | bytes 1105928 | tf_op jit(solution)/shard_map/ppermute | solution.py:11
  79.6 17.4 %collective-permute-start.17 = (bf16[4,360,128]{2,1,0:T(8,128)(2,1)S(1)}, bf16[4,360,128]{2,1,0:T(8,128)(2,1)S(1)}, u32[]{:S(2)}, u32[]{:S(2)}) collective-permute-start(bf16[4,360,128]{2,1,0:T(8,128)(2,1)S(1)} %get-tuple-element.72), channel_id=1, source_target_pairs={{0,24},{8,16},{16,8},{24,0},{1,25},{9,17},{17,9},{25,1},{2,26},{10... | collective-permute-start | bytes 1105928 | tf_op jit(solution)/shard_map/ppermute | solution.py:11
  97.3 7.6 %collective-permute-start.20 = (bf16[360,128]{1,0:T(8,128)(2,1)S(1)}, bf16[360,128]{1,0:T(8,128)(2,1)S(1)}, u32[]{:S(2)}, u32[]{:S(2)}) collective-permute-start(bf16[360,128]{1,0:T(8,128)(2,1)S(1)} %get-tuple-element.79), channel_id=1, source_target_pairs={{0,6},{2,4},{4,2},{6,0},{1,7},{3,5},{5,3},{7,1},{8,14},{10,12},{12... | collective-permute-start | bytes 276488 | tf_op jit(solution)/shard_map/ppermute | solution.py:11
  98.8 8.2 %collective-permute-start.19 = (bf16[360,128]{1,0:T(8,128)(2,1)S(1)}, bf16[360,128]{1,0:T(8,128)(2,1)S(1)}, u32[]{:S(2)}, u32[]{:S(2)}) collective-permute-start(bf16[360,128]{1,0:T(8,128)(2,1)S(1)} %get-tuple-element.80), channel_id=1, source_target_pairs={{0,4},{2,6},{4,0},{6,2},{1,5},{3,7},{5,1},{7,3},{8,12},{10,14},{12... | collective-permute-start | bytes 276488 | tf_op jit(solution)/shard_map/ppermute | solution.py:11
  98.8 8.2 %collective-permute-start.18 = (bf16[360,128]{1,0:T(8,128)(2,1)S(1)}, bf16[360,128]{1,0:T(8,128)(2,1)S(1)}, u32[]{:S(2)}, u32[]{:S(2)}) collective-permute-start(bf16[360,128]{1,0:T(8,128)(2,1)S(1)} %get-tuple-element.78), channel_id=1, source_target_pairs={{0,2},{2,0},{4,6},{6,4},{1,3},{3,1},{5,7},{7,5},{8,10},{10,8},{12,... | collective-permute-start | bytes 276488 | tf_op jit(solution)/shard_map/ppermute | solution.py:11
  (12 other events, 60.6 us)

commit v3 on v2

--- a/solution.py
+++ b/solution.py
@@ -11,8 +11,9 @@
     return lax.ppermute(a, axis, [(i, i ^ s) for i in range(lax.axis_size(axis))])
 
 
-def ring_order(pieces):
+def ring_order(stack):
     ring, bit = lax.axis_index("ring"), 1
+    pieces = [stack[i] for i in range(stack.shape[0])]
     while bit < len(pieces):
         swap = (ring & bit) > 0
         pieces = [jnp.where(swap, pieces[i ^ bit], pieces[i]) for i in range(len(pieces))]
@@ -30,6 +31,8 @@
 
 def both_cores(half):
     other = xor_send(half, "core", 1)
+    half, other = lax.optimization_barrier((ring_order(half), other))
+    other = ring_order(other)
     first = lax.axis_index("core") == 0
     both = jnp.where(first, jnp.stack([half, other], 1), jnp.stack([other, half], 1))
     return both.reshape(-1, both.shape[-1])
@@ -69,37 +72,55 @@
 def body(tokens, grad_out, gates, routes, w_gate, w_up, w_down):
     groups = lax.axis_size("expert")
     local = w_gate.shape[0]
-    rows = tokens.shape[0]
+    width, rows = tokens.shape[1], tokens.shape[0]
     group = lax.axis_index("expert")
 
     ids = jnp.arange(groups * local, dtype=jnp.int32)
     named = routes[None] == ids[:, None, None]
     weight = jnp.sum(jnp.where(named, gates[None], 0.0), -1)
-    weight = weight.reshape(groups, local, rows)
-    coef = [at(weight, group)]
-    for s in range(1, groups):
-        coef.append(xor_send(at(weight, group ^ s), "expert", s))
+    parts, left = [], weight
+    for _ in range(3):
+        part = lax.reduce_precision(left, 8, 7)
+        parts.append(part.astype(BF16))
+        left = left - part
 
     def to_hidden(w, a):
         return jnp.einsum("efd,dt->eft", w, a, preferred_element_type=F32)
 
     x_own, g_own = tokens.T, grad_out.T
-    x_ring = ring_order(ring_gather(x_own))
-    x_ring, coef, g_own = lax.optimization_barrier((x_ring, coef, g_own))
-    x_blocks = plane_gather(x_ring)
-    g_ring = lax.all_gather(g_own, "ring", axis=0)
-    x_blocks, g_ring = lax.optimization_barrier((x_blocks, g_ring))
-    g_blocks = plane_gather(g_ring)
-    x = both_cores(jnp.concatenate(x_blocks, -1))
-    coef = jnp.concatenate(coef, -1)[:, None, :]
+    x_ring = ring_gather(x_own)
+    early = plane_gather(jnp.concatenate([x_own, g_own] + parts, 0))
+    early, g_first = lax.optimization_barrier((early, g_own))
+    g_ring = ring_gather(g_first)
+
+    def next_places(near):
+        return xor_send(jnp.stack(near[1:]), "ring", 1)
+
+    def all_places(near, nearer, ring_own, rest):
+        rows = [jnp.concatenate(near, -1)]
+        rows.append(jnp.concatenate([ring_own[1]] + [nearer[s] for s in range(groups - 1)], -1))
+        rest = jnp.concatenate(rest, -1)
+        return jnp.stack(rows + [rest[i] for i in range(rest.shape[0])])
+
+    x_near = [a[:width] for a in early]
+    g_near = [a[width : 2 * width] for a in early]
+    x_next = next_places(x_near)
+    x_ring = lax.optimization_barrier(x_ring)
+    x_rest = plane_gather(jnp.stack(x_ring[2:]))
+    g_ring, g_near, _, _ = lax.optimization_barrier((g_ring, g_near, x_rest, x_next))
+    g_next = next_places(g_near)
+    g_rest = plane_gather(jnp.stack(g_ring[2:]))
+    x = both_cores(all_places(x_near, x_next, x_ring, x_rest))
+    coef = jnp.concatenate([a[2 * width :] for a in early], -1).reshape(3, groups * local, -1).astype(F32)
+    coef = lax.dynamic_slice_in_dim(coef[0] + coef[1] + coef[2], group * local, local, 0)[:, None, :]
     pre_gate = to_hidden(w_gate, x)
     pre_up = to_hidden(w_up, x)
     sig = jax.nn.sigmoid(1.702 * pre_gate)
     glu = pre_gate * sig
     act = (glu * (pre_up + 1.0) * coef).astype(BF16)
     slope = (pre_up + 1.0) * (sig + 1.702 * pre_gate * sig * (1.0 - sig))
-    g_blocks, act, glu, slope = lax.optimization_barrier((g_blocks, act, glu, slope))
-    g = both_cores(jnp.concatenate(g_blocks, -1))
+    g_rest, g_next, act, glu, slope = lax.optimization_barrier((g_rest, g_next, act, glu, slope))
+    g = both_cores(all_places(g_near, g_next, g_ring, g_rest))
 
     d_act = to_hidden(w_down, g) * coef
     d_pre_gate = (d_act * slope).astype(BF16)

time: 108 us -> 106 us (0.981)
  blocking collectives: 16.1 us -> 0 us
  starting transfers between devices: 25.9 us -> 34.2 us
  matrix products: 36.6 us -> 28.5 us
  other arithmetic: 4.38 us -> 9.87 us
  local copies, waits for them, and re-layouts: 2.48 us -> 7.58 us
  waiting for transfers between devices: 21.2 us -> 24.2 us
    all_gather x1 -> x0, blocking collectives: 16.1 us -> none  [body(): g_ring = lax.all_gather(g_own, 'ring', axis=0)]
    dot_general x3, matrix products: 17.8 us -> 9.33 us  [to_hidden(): return jnp.einsum('efd,dt->eft', w, a, preferred_element_type=F32)]
    ppermute x21 -> x26, starting transfers between devices: 25.9 us -> 34.2 us  [xor_send(): lax.ppermute(a, axis, [(i, i ^ s) for i in range(lax.axis_size(axis))])]
    unnamed x36 -> x47, local copies, waits for them, and re-layouts: 0.57 us -> 5.31 us
    select_n x0 -> x10, other arithmetic: none -> 3.37 us  [ring_order(): jnp.where(swap, pieces[i ^ bit], pieces[i])]
    ppermute x21 -> x26, waiting for transfers between devices: 21.2 us -> 24.2 us  [xor_send(): lax.ppermute(a, axis, [(i, i ^ s) for i in range(lax.axis_size(axis))])]
    another operation x1 -> x13, other arithmetic: 0.59 us -> 2.64 us  [the longest x6 1.6 us: all_places(): return jnp.stack(rows + [rest[i] for i in range(rest.shape[0])])]
  transfers between devices with their start and end apart: 21 -> 26, of which waited for: 8 -> 11; matrix products, arithmetic and copies ran while one was open for 25% -> 25% of each run, Pallas kernels for 0% -> 0%
where the time goes in v3:
time: 106 us
  starting transfers between devices  34.2 us (32%)
  matrix products  28.5 us (27%)
  waiting for transfers between devices  24.2 us (23%)
  other arithmetic  9.87 us (9%)
  local copies, waits for them, and re-layouts  7.58 us (7%)
  between operations  1.24 us (1%)
    ppermute x26, starting transfers between devices, xor_send(): lax.ppermute(a, axis, [(i, i ^ s) for i in range(lax.axis_size(axis))])  34.2 us
    ppermute x26, waiting for transfers between devices, xor_send(): lax.ppermute(a, axis, [(i, i ^ s) for i in range(lax.axis_size(axis))])  24.2 us
    dot_general x3, matrix products, to_weight(): jnp.einsum('eft,dt->efd', a, b, preferred_element_type=F32).astype(BF16)  13.8 us
    dot_general x3, matrix products, to_hidden(): return jnp.einsum('efd,dt->eft', w, a, preferred_element_type=F32)  9.33 us
    unnamed x47, local copies, waits for them, and re-layouts  5.31 us
    select_n x10, other arithmetic, ring_order(): jnp.where(swap, pieces[i ^ bit], pieces[i])  3.37 us
    dot_general x1, matrix products, body(): jnp.einsum('efd,eft->dt', w_up, d_pre_up, preferred_element_type=F32)  2.72 us
    dot_general x1, matrix products, body(): jnp.einsum('efd,eft->dt', w_gate, d_pre_gate, preferred_element_type=F32)  2.64 us
  transfers between devices with their start and end apart: 26, of which 11 were waited for; matrix products, arithmetic and copies ran while one was open for 25% of the time, Pallas kernels for 0%

profile of v3, /device:TPU:0, one launch (start us, length us, event | category | flops | bytes accessed | tf_op | source)
XLA Modules:
  0.0 105.6 jit_solution(2908648138758263276)
XLA Ops:
  0.6 3.1 %collective-permute-start.6 = (bf16[360,128]{1,0:T(8,128)(2,1)}, bf16[360,128]{1,0:T(8,128)(2,1)S(1)}, u32[]{:S(2)}, u32[]{:S(2)}) collective-permute-start(bf16[360,128]{1,0:T(8,128)(2,1)} %bitcast.165), channel_id=1, source_target_pairs={{0,2},{2,0},{4,6},{6,4},{1,3},{3,1},{5,7},{7,5},{8,10},{10,8},{12,... | collective-permute-start | bytes 276488 | tf_op jit(solution)/shard_map/ppermute | solution.py:11
  3.7 2.6 %collective-permute-start.7 = (bf16[360,128]{1,0:T(8,128)(2,1)}, bf16[360,128]{1,0:T(8,128)(2,1)S(1)}, u32[]{:S(2)}, u32[]{:S(2)}) collective-permute-start(bf16[360,128]{1,0:T(8,128)(2,1)} %bitcast.166), channel_id=1, source_target_pairs={{0,4},{2,6},{4,0},{6,2},{1,5},{3,7},{5,1},{7,3},{8,12},{10,14},{12... | collective-permute-start | bytes 276488 | tf_op jit(solution)/shard_map/ppermute | solution.py:11
  8.9 1.7 %collective-permute-start = (bf16[744,128]{1,0:T(8,128)(2,1)S(1)}, bf16[744,128]{1,0:T(8,128)(2,1)S(1)}, u32[]{:S(2)}, u32[]{:S(2)}) collective-permute-start(bf16[744,128]{1,0:T(8,128)(2,1)S(1)} %constant_dynamic-update-slice_fusion), channel_id=1, source_target_pairs={{0,8},{8,0},{16,24},{24,16},{1,9},{9,1},{17,25},{25,17},{2,10},{10... | collective-permute-start | bytes 571400 | tf_op jit(solution)/shard_map/ppermute | solution.py:11
  17.0 2.3 %collective-permute-start.11 = (bf16[2,360,128]{2,1,0:T(8,128)(2,1)S(1)}, bf16[2,360,128]{2,1,0:T(8,128)(2,1)S(1)}, u32[]{:S(2)}, u32[]{:S(2)}) collective-permute-start(bf16[2,360,128]{2,1,0:T(8,128)(2,1)S(1)} %pad_maximum_fusion.10), channel_id=1, source_target_pairs={{0,24},{8,16},{16,8},{24,0},{1,25},{9,17},{17,9},{25,1},{2,26},{10... | collective-permute-start | bytes 552968 | tf_op jit(solution)/shard_map/ppermute | solution.py:11
  19.3 2.4 %collective-permute-done.1 = bf16[744,128]{1,0:T(8,128)(2,1)S(1)} collective-permute-done((bf16[744,128]{1,0:T(8,128)(2,1)S(1)}, bf16[744,128]{1,0:T(8,128)(2,1)S(1)}, u32[]{:S(2)}, u32[]{:S(2)}) %collective-permute-start.1) | collective-permute-done | bytes 190496 | tf_op jit(solution)/shard_map/ppermute | solution.py:11
  24.7 2.1 %collective-permute-start.4 = (bf16[360,128]{1,0:T(8,128)(2,1)S(1)}, bf16[360,128]{1,0:T(8,128)(2,1)S(1)}, u32[]{:S(2)}, u32[]{:S(2)}) collective-permute-start(bf16[360,128]{1,0:T(8,128)(2,1)S(1)} %bitcast.169), channel_id=1, source_target_pairs={{0,4},{2,6},{4,0},{6,2},{1,5},{3,7},{5,1},{7,3},{8,12},{10,14},{12... | collective-permute-start | bytes 276488 | tf_op jit(solution)/shard_map/ppermute | solution.py:11
  28.2 3.5 %collective-permute-start.5 = (bf16[360,128]{1,0:T(8,128)(2,1)S(1)}, bf16[360,128]{1,0:T(8,128)(2,1)S(1)}, u32[]{:S(2)}, u32[]{:S(2)}) collective-permute-start(bf16[360,128]{1,0:T(8,128)(2,1)S(1)} %bitcast.170), channel_id=1, source_target_pairs={{0,6},{2,4},{4,2},{6,0},{1,7},{3,5},{5,3},{7,1},{8,14},{10,12},{12... | collective-permute-start | bytes 276488 | tf_op jit(solution)/shard_map/ppermute | solution.py:11
  31.9 3.5 %collective-permute-done.5 = bf16[360,128]{1,0:T(8,128)(2,1)S(1)} collective-permute-done((bf16[360,128]{1,0:T(8,128)(2,1)S(1)}, bf16[360,128]{1,0:T(8,128)(2,1)S(1)}, u32[]{:S(2)}, u32[]{:S(2)}) %collective-permute-start.5) | collective-permute-done | bytes 92192 | tf_op jit(solution)/shard_map/ppermute | solution.py:11
  37.4 2.0 %collective-permute-start.15 = (bf16[2,360,128]{2,1,0:T(8,128)(2,1)S(1)}, bf16[2,360,128]{2,1,0:T(8,128)(2,1)S(1)}, u32[]{:S(2)}, u32[]{:S(2)}) collective-permute-start(bf16[2,360,128]{2,1,0:T(8,128)(2,1)S(1)} %pad_maximum_fusion.11), channel_id=1, source_target_pairs={{0,24},{8,16},{16,8},{24,0},{1,25},{9,17},{17,9},{25,1},{2,26},{10... | collective-permute-start | bytes 552968 | tf_op jit(solution)/shard_map/ppermute | solution.py:11
  41.5 2.2 %slice-done.6 = s8[4194304]{0:T(1024)(128)(4,1)S(1)} async-done(((s8[4239360]{0:T(1024)(128)(4,1)}), s8[4194304]{0:T(1024)(128)(4,1)S(1)}, s32[]{:S(2)}) %slice-start.6) | async-done | bytes 4194328
  43.7 2.4 %fusion.17 = f32[512,2,360]{0,2,1:T(8,128)S(1)} fusion(bf16[2880,512,1]{1,0,2:T(8,128)(2,1)S(1)} %bitcast.145, bf16[2,360,2880]{2,1,0:T(8,128)(2,1)S(1)} %bitcast.180), kind=kOutput, calls=%fused_computation.118 | convolution fusion | flops 2123366400 | bytes 8570880 | tf_op jit(solution)/shard_map/efd,dt->eft/dot_general | solution.py:88
  46.2 4.5 %bitcast_multiply_fusion.1 = (f32[2,360,512]{2,1,0:T(8,128)S(1)}, bf16[2,360,512]{2,1,0:T(8,128)(2,1)}, f32[2,360,512]{2,1,0:T(8,128)}) fusion(f32[512,2,360]{0,2,1:T(8,128)S(1)} %fusion.17, f32[2,512]{1,0:T(2,128)S(1)} %dynamic-slice_add_fusion, bf16[2880,512,1]{1,0,2:T(8,128)(2,1)S(1)} %bitcast.146, bf16[2,360,2880]{2,1,0:T(8,128)(2,1)S(1)} %bitcast.176), kind=kOutput, calls=%fused_computation.15 | convolution fusion | flops 2128527360 | bytes 12261376 | tf_op jit(solution)/shard_map/efd,dt->eft/dot_general | solution.py:88
  53.4 2.5 %collective-permute-done.18 = bf16[4,360,512]{2,1,0:T(8,128)(2,1)} collective-permute-done((bf16[4,360,512]{2,1,0:T(8,128)(2,1)}, bf16[4,360,512]{2,1,0:T(8,128)(2,1)}, u32[]{:S(2)}, u32[]{:S(2)}) %collective-permute-start.18) | collective-permute-done | bytes 1474592 | tf_op jit(solution)/shard_map/ppermute | solution.py:11
  59.5 2.4 %bitcast_multiply_fusion = f32[2,360,512]{2,1,0:T(8,128)S(1)} fusion(bf16[2880,512,1]{1,0,2:T(8,128)(2,1)S(1)} %bitcast.149, bf16[2,360,2880]{2,1,0:T(8,128)(2,1)S(1)} %bitcast.174, f32[2,512]{1,0:T(2,128)S(1)} %dynamic-slice_add_fusion), kind=kOutput, calls=%fused_computation.14 | convolution fusion | flops 2123735040 | bytes 8574976 | tf_op jit(solution)/shard_map/efd,dt->eft/dot_general | solution.py:88
  62.7 2.6 %fusion.18 = f32[512,2880,1]{0,1,2:T(8,128)S(1)} fusion(bf16[2,360,512]{2,1,0:T(8,128)(2,1)S(1)} %get-tuple-element.72, bf16[2,360,2880]{2,1,0:T(8,128)(2,1)S(1)} %bitcast.178), kind=kOutput, calls=%fused_computation.119 | convolution fusion | flops 2123366400 | bytes 10782720 | tf_op jit(solution)/shard_map/efd,eft->dt/dot_general | solution.py:132
  65.4 2.7 %fusion = bf16[512,2880]{0,1:T(8,128)(2,1)S(1)} fusion(f32[512,2880,1]{0,1,2:T(8,128)S(1)} %fusion.18, bf16[2,360,512]{2,1,0:T(8,128)(2,1)S(1)} %get-tuple-element.73, bf16[2,360,2880]{2,1,0:T(8,128)(2,1)S(1)} %bitcast.182), kind=kOutput, calls=%fused_computation.1 | convolution fusion | flops 2126315520 | bytes 13731840 | tf_op jit(solution)/shard_map/efd,eft->dt/dot_general | solution.py:133
  69.6 3.3 %collective-permute-done.19 = bf16[4,360,512]{2,1,0:T(8,128)(2,1)S(1)} collective-permute-done((bf16[4,360,512]{2,1,0:T(8,128)(2,1)}, bf16[4,360,512]{2,1,0:T(8,128)(2,1)S(1)}, u32[]{:S(2)}, u32[]{:S(2)}) %collective-permute-start.19) | collective-permute-done | bytes 1474592 | tf_op jit(solution)/shard_map/ppermute | solution.py:11
  73.8 1.7 %collective-permute-start.20 = (bf16[4,360,128]{2,1,0:T(8,128)(2,1)S(1)}, bf16[4,360,128]{2,1,0:T(8,128)(2,1)S(1)}, u32[]{:S(2)}, u32[]{:S(2)}) collective-permute-start(bf16[4,360,128]{2,1,0:T(8,128)(2,1)S(1)} %get-tuple-element.92), channel_id=1, source_target_pairs={{0,8},{8,0},{16,24},{24,16},{1,9},{9,1},{17,25},{25,17},{2,10},{10... | collective-permute-start | bytes 1105928 | tf_op jit(solution)/shard_map/ppermute | solution.py:11
  77.4 4.5 %convolution_convert_fusion.2 = bf16[2,360,2880]{2,1,0:T(8,128)(2,1)} fusion(bf16[2,360,512]{2,1,0:T(8,128)(2,1)S(1)} %copy-done.8, bf16[2880,512,1]{1,0,2:T(8,128)(2,1)S(1)} %bitcast.147), kind=kOutput, calls=%fused_computation.4 | convolution fusion | flops 2125440000 | bytes 7833600 | tf_op jit(solution)/shard_map/eft,dt->efd/dot_general | solution.py:130
  81.9 4.7 %convolution_convert_fusion.1 = bf16[2,360,2880]{2,1,0:T(8,128)(2,1)} fusion(bf16[2,360,512]{2,1,0:T(8,128)(2,1)S(1)} %copy-done.6, bf16[2880,512,1]{1,0,2:T(8,128)(2,1)S(1)} %bitcast.148), kind=kOutput, calls=%fused_computation.3 | convolution fusion | flops 2125440000 | bytes 7833600 | tf_op jit(solution)/shard_map/eft,dt->efd/dot_general | solution.py:130
  86.7 4.5 %convolution_convert_fusion = bf16[2,360,2880]{2,1,0:T(8,128)(2,1)} fusion(bf16[2,360,512]{2,1,0:T(8,128)(2,1)S(1)} %copy-done.10, bf16[2880,512,1]{1,0,2:T(8,128)(2,1)S(1)} %bitcast.150), kind=kOutput, calls=%fused_computation.2 | convolution fusion | flops 2125440000 | bytes 7833600 | tf_op jit(solution)/shard_map/eft,dt->efd/dot_general | solution.py:130
  94.1 2.2 %collective-permute-start.25 = (bf16[360,128]{1,0:T(8,128)(2,1)S(1)}, bf16[360,128]{1,0:T(8,128)(2,1)S(1)}, u32[]{:S(2)}, u32[]{:S(2)}) collective-permute-start(bf16[360,128]{1,0:T(8,128)(2,1)S(1)} %get-tuple-element.105), channel_id=1, source_target_pairs={{0,6},{2,4},{4,2},{6,0},{1,7},{3,5},{5,3},{7,1},{8,14},{10,12},{12... | collective-permute-start | bytes 276488 | tf_op jit(solution)/shard_map/ppermute | solution.py:11
  98.6 2.9 %collective-permute-done.25 = bf16[360,128]{1,0:T(8,128)(2,1)S(1)} collective-permute-done((bf16[360,128]{1,0:T(8,128)(2,1)S(1)}, bf16[360,128]{1,0:T(8,128)(2,1)S(1)}, u32[]{:S(2)}, u32[]{:S(2)}) %collective-permute-start.25) | collective-permute-done | bytes 92192 | tf_op jit(solution)/shard_map/ppermute | solution.py:11
  101.5 3.4 %collective-permute-done.24 = bf16[360,128]{1,0:T(8,128)(2,1)S(1)} collective-permute-done((bf16[360,128]{1,0:T(8,128)(2,1)S(1)}, bf16[360,128]{1,0:T(8,128)(2,1)S(1)}, u32[]{:S(2)}, u32[]{:S(2)}) %collective-permute-start.24) | collective-permute-done | bytes 92192 | tf_op jit(solution)/shard_map/ppermute | solution.py:11
  (141 shorter events, 34.4 us)
Async XLA Ops:
  0.6 11.6 %collective-permute-start.6 = (bf16[360,128]{1,0:T(8,128)(2,1)}, bf16[360,128]{1,0:T(8,128)(2,1)S(1)}, u32[]{:S(2)}, u32[]{:S(2)}) collective-permute-start(bf16[360,128]{1,0:T(8,128)(2,1)} %bitcast.165), channel_id=1, source_target_pairs={{0,2},{2,0},{4,6},{6,4},{1,3},{3,1},{5,7},{7,5},{8,10},{10,8},{12,... | collective-permute-start | bytes 276488 | tf_op jit(solution)/shard_map/ppermute | solution.py:11
  3.7 10.2 %collective-permute-start.7 = (bf16[360,128]{1,0:T(8,128)(2,1)}, bf16[360,128]{1,0:T(8,128)(2,1)S(1)}, u32[]{:S(2)}, u32[]{:S(2)}) collective-permute-start(bf16[360,128]{1,0:T(8,128)(2,1)} %bitcast.166), channel_id=1, source_target_pairs={{0,4},{2,6},{4,0},{6,2},{1,5},{3,7},{5,1},{7,3},{8,12},{10,14},{12... | collective-permute-start | bytes 276488 | tf_op jit(solution)/shard_map/ppermute | solution.py:11
  6.3 7.6 %collective-permute-start.8 = (bf16[360,128]{1,0:T(8,128)(2,1)}, bf16[360,128]{1,0:T(8,128)(2,1)S(1)}, u32[]{:S(2)}, u32[]{:S(2)}) collective-permute-start(bf16[360,128]{1,0:T(8,128)(2,1)} %bitcast.167), channel_id=1, source_target_pairs={{0,6},{2,4},{4,2},{6,0},{1,7},{3,5},{5,3},{7,1},{8,14},{10,12},{12... | collective-permute-start | bytes 276488 | tf_op jit(solution)/shard_map/ppermute | solution.py:11
  8.9 8.1 %collective-permute-start = (bf16[744,128]{1,0:T(8,128)(2,1)S(1)}, bf16[744,128]{1,0:T(8,128)(2,1)S(1)}, u32[]{:S(2)}, u32[]{:S(2)}) collective-permute-start(bf16[744,128]{1,0:T(8,128)(2,1)S(1)} %constant_dynamic-update-slice_fusion), channel_id=1, source_target_pairs={{0,8},{8,0},{16,24},{24,16},{1,9},{9,1},{17,25},{25,17},{2,10},{10... | collective-permute-start | bytes 571400 | tf_op jit(solution)/shard_map/ppermute | solution.py:11
  10.7 11.1 %collective-permute-start.1 = (bf16[744,128]{1,0:T(8,128)(2,1)S(1)}, bf16[744,128]{1,0:T(8,128)(2,1)S(1)}, u32[]{:S(2)}, u32[]{:S(2)}) collective-permute-start(bf16[744,128]{1,0:T(8,128)(2,1)S(1)} %constant_dynamic-update-slice_fusion), channel_id=1, source_target_pairs={{0,16},{8,24},{16,0},{24,8},{1,17},{9,25},{17,1},{25,9},{2,18},{10... | collective-permute-start | bytes 571400 | tf_op jit(solution)/shard_map/ppermute | solution.py:11
  12.2 9.6 %collective-permute-start.2 = (bf16[744,128]{1,0:T(8,128)(2,1)S(1)}, bf16[744,128]{1,0:T(8,128)(2,1)S(1)}, u32[]{:S(2)}, u32[]{:S(2)}) collective-permute-start(bf16[744,128]{1,0:T(8,128)(2,1)S(1)} %constant_dynamic-update-slice_fusion), channel_id=1, source_target_pairs={{0,24},{8,16},{16,8},{24,0},{1,25},{9,17},{17,9},{25,1},{2,26},{10... | collective-permute-start | bytes 571400 | tf_op jit(solution)/shard_map/ppermute | solution.py:11
  13.9 10.8 %collective-permute-start.9 = (bf16[2,360,128]{2,1,0:T(8,128)(2,1)S(1)}, bf16[2,360,128]{2,1,0:T(8,128)(2,1)S(1)}, u32[]{:S(2)}, u32[]{:S(2)}) collective-permute-start(bf16[2,360,128]{2,1,0:T(8,128)(2,1)S(1)} %pad_maximum_fusion.10), channel_id=1, source_target_pairs={{0,8},{8,0},{16,24},{24,16},{1,9},{9,1},{17,25},{25,17},{2,10},{10... | collective-permute-start | bytes 552968 | tf_op jit(solution)/shard_map/ppermute | solution.py:11
  15.5 12.7 %collective-permute-start.10 = (bf16[2,360,128]{2,1,0:T(8,128)(2,1)S(1)}, bf16[2,360,128]{2,1,0:T(8,128)(2,1)S(1)}, u32[]{:S(2)}, u32[]{:S(2)}) collective-permute-start(bf16[2,360,128]{2,1,0:T(8,128)(2,1)S(1)} %pad_maximum_fusion.10), channel_id=1, source_target_pairs={{0,16},{8,24},{16,0},{24,8},{1,17},{9,25},{17,1},{25,9},{2,18},{10... | collective-permute-start | bytes 552968 | tf_op jit(solution)/shard_map/ppermute | solution.py:11
  17.0 14.7 %collective-permute-start.11 = (bf16[2,360,128]{2,1,0:T(8,128)(2,1)S(1)}, bf16[2,360,128]{2,1,0:T(8,128)(2,1)S(1)}, u32[]{:S(2)}, u32[]{:S(2)}) collective-permute-start(bf16[2,360,128]{2,1,0:T(8,128)(2,1)S(1)} %pad_maximum_fusion.10), channel_id=1, source_target_pairs={{0,24},{8,16},{16,8},{24,0},{1,25},{9,17},{17,9},{25,1},{2,26},{10... | collective-permute-start | bytes 552968 | tf_op jit(solution)/shard_map/ppermute | solution.py:11
  22.0 9.9 %collective-permute-start.3 = (bf16[360,128]{1,0:T(8,128)(2,1)S(1)}, bf16[360,128]{1,0:T(8,128)(2,1)S(1)}, u32[]{:S(2)}, u32[]{:S(2)}) collective-permute-start(bf16[360,128]{1,0:T(8,128)(2,1)S(1)} %bitcast.168), channel_id=1, source_target_pairs={{0,2},{2,0},{4,6},{6,4},{1,3},{3,1},{5,7},{7,5},{8,10},{10,8},{12,... | collective-permute-start | bytes 276488 | tf_op jit(solution)/shard_map/ppermute | solution.py:11
  22.6 12.8 %collective-permute-start.12 = (bf16[3,360,128]{2,1,0:T(8,128)(2,1)S(1)}, bf16[3,360,128]{2,1,0:T(8,128)(2,1)S(1)}, u32[]{:S(2)}, u32[]{:S(2)}) collective-permute-start(bf16[3,360,128]{2,1,0:T(8,128)(2,1)S(1)} %pad_maximum_fusion.8), channel_id=1, source_target_pairs={{0,2},{2,0},{4,6},{6,4},{1,3},{3,1},{5,7},{7,5},{8,10},{10,8},{12,... | collective-permute-start | bytes 829448 | tf_op jit(solution)/shard_map/ppermute | solution.py:11
  24.7 7.2 %collective-permute-start.4 = (bf16[360,128]{1,0:T(8,128)(2,1)S(1)}, bf16[360,128]{1,0:T(8,128)(2,1)S(1)}, u32[]{:S(2)}, u32[]{:S(2)}) collective-permute-start(bf16[360,128]{1,0:T(8,128)(2,1)S(1)} %bitcast.169), channel_id=1, source_target_pairs={{0,4},{2,6},{4,0},{6,2},{1,5},{3,7},{5,1},{7,3},{8,12},{10,14},{12... | collective-permute-start | bytes 276488 | tf_op jit(solution)/shard_map/ppermute | solution.py:11
  28.2 7.1 %collective-permute-start.5 = (bf16[360,128]{1,0:T(8,128)(2,1)S(1)}, bf16[360,128]{1,0:T(8,128)(2,1)S(1)}, u32[]{:S(2)}, u32[]{:S(2)}) collective-permute-start(bf16[360,128]{1,0:T(8,128)(2,1)S(1)} %bitcast.170), channel_id=1, source_target_pairs={{0,6},{2,4},{4,2},{6,0},{1,7},{3,5},{5,3},{7,1},{8,14},{10,12},{12... | collective-permute-start | bytes 276488 | tf_op jit(solution)/shard_map/ppermute | solution.py:11
  35.7 4.9 %collective-permute-start.17 = (bf16[4,360,512]{2,1,0:T(8,128)(2,1)S(1)}, bf16[4,360,512]{2,1,0:T(8,128)(2,1)S(1)}, u32[]{:S(2)}, u32[]{:S(2)}) collective-permute-start(bf16[4,360,512]{2,1,0:T(8,128)(2,1)S(1)} %maximum_maximum_fusion), channel_id=1, source_target_pairs={{0,1},{1,0},{2,3},{3,2},{4,5},{5,4},{6,7},{7,6},{8,9},{9,8},{10,11... | collective-permute-start | bytes 4423688 | tf_op jit(solution)/shard_map/ppermute | solution.py:11
  35.8 14.9 %collective-permute-start.13 = (bf16[2,360,128]{2,1,0:T(8,128)(2,1)S(1)}, bf16[2,360,128]{2,1,0:T(8,128)(2,1)S(1)}, u32[]{:S(2)}, u32[]{:S(2)}) collective-permute-start(bf16[2,360,128]{2,1,0:T(8,128)(2,1)S(1)} %pad_maximum_fusion.11), channel_id=1, source_target_pairs={{0,8},{8,0},{16,24},{24,16},{1,9},{9,1},{17,25},{25,17},{2,10},{10... | collective-permute-start | bytes 552968 | tf_op jit(solution)/shard_map/ppermute | solution.py:11
  36.9 13.8 %collective-permute-start.14 = (bf16[2,360,128]{2,1,0:T(8,128)(2,1)S(1)}, bf16[2,360,128]{2,1,0:T(8,128)(2,1)S(1)}, u32[]{:S(2)}, u32[]{:S(2)}) collective-permute-start(bf16[2,360,128]{2,1,0:T(8,128)(2,1)S(1)} %pad_maximum_fusion.11), channel_id=1, source_target_pairs={{0,16},{8,24},{16,0},{24,8},{1,17},{9,25},{17,1},{25,9},{2,18},{10... | collective-permute-start | bytes 552968 | tf_op jit(solution)/shard_map/ppermute | solution.py:11
  37.4 13.3 %collective-permute-start.15 = (bf16[2,360,128]{2,1,0:T(8,128)(2,1)S(1)}, bf16[2,360,128]{2,1,0:T(8,128)(2,1)S(1)}, u32[]{:S(2)}, u32[]{:S(2)}) collective-permute-start(bf16[2,360,128]{2,1,0:T(8,128)(2,1)S(1)} %pad_maximum_fusion.11), channel_id=1, source_target_pairs={{0,24},{8,16},{16,8},{24,0},{1,25},{9,17},{17,9},{25,1},{2,26},{10... | collective-permute-start | bytes 552968 | tf_op jit(solution)/shard_map/ppermute | solution.py:11
  39.3 11.3 %collective-permute-start.16 = (bf16[3,360,128]{2,1,0:T(8,128)(2,1)S(1)}, bf16[3,360,128]{2,1,0:T(8,128)(2,1)S(1)}, u32[]{:S(2)}, u32[]{:S(2)}) collective-permute-start(bf16[3,360,128]{2,1,0:T(8,128)(2,1)S(1)} %pad_maximum_fusion.9), channel_id=1, source_target_pairs={{0,2},{2,0},{4,6},{6,4},{1,3},{3,1},{5,7},{7,5},{8,10},{10,8},{12,... | collective-permute-start | bytes 829448 | tf_op jit(solution)/shard_map/ppermute | solution.py:11
  73.8 17.4 %collective-permute-start.20 = (bf16[4,360,128]{2,1,0:T(8,128)(2,1)S(1)}, bf16[4,360,128]{2,1,0:T(8,128)(2,1)S(1)}, u32[]{:S(2)}, u32[]{:S(2)}) collective-permute-start(bf16[4,360,128]{2,1,0:T(8,128)(2,1)S(1)} %get-tuple-element.92), channel_id=1, source_target_pairs={{0,8},{8,0},{16,24},{24,16},{1,9},{9,1},{17,25},{25,17},{2,10},{10... | collective-permute-start | bytes 1105928 | tf_op jit(solution)/shard_map/ppermute | solution.py:11
  75.5 17.1 %collective-permute-start.21 = (bf16[4,360,128]{2,1,0:T(8,128)(2,1)S(1)}, bf16[4,360,128]{2,1,0:T(8,128)(2,1)S(1)}, u32[]{:S(2)}, u32[]{:S(2)}) collective-permute-start(bf16[4,360,128]{2,1,0:T(8,128)(2,1)S(1)} %get-tuple-element.91), channel_id=1, source_target_pairs={{0,16},{8,24},{16,0},{24,8},{1,17},{9,25},{17,1},{25,9},{2,18},{10... | collective-permute-start | bytes 1105928 | tf_op jit(solution)/shard_map/ppermute | solution.py:11
  76.9 17.0 %collective-permute-start.22 = (bf16[4,360,128]{2,1,0:T(8,128)(2,1)S(1)}, bf16[4,360,128]{2,1,0:T(8,128)(2,1)S(1)}, u32[]{:S(2)}, u32[]{:S(2)}) collective-permute-start(bf16[4,360,128]{2,1,0:T(8,128)(2,1)S(1)} %get-tuple-element.90), channel_id=1, source_target_pairs={{0,24},{8,16},{16,8},{24,0},{1,25},{9,17},{17,9},{25,1},{2,26},{10... | collective-permute-start | bytes 1105928 | tf_op jit(solution)/shard_map/ppermute | solution.py:11
  94.1 7.4 %collective-permute-start.25 = (bf16[360,128]{1,0:T(8,128)(2,1)S(1)}, bf16[360,128]{1,0:T(8,128)(2,1)S(1)}, u32[]{:S(2)}, u32[]{:S(2)}) collective-permute-start(bf16[360,128]{1,0:T(8,128)(2,1)S(1)} %get-tuple-element.105), channel_id=1, source_target_pairs={{0,6},{2,4},{4,2},{6,0},{1,7},{3,5},{5,3},{7,1},{8,14},{10,12},{12... | collective-permute-start | bytes 276488 | tf_op jit(solution)/shard_map/ppermute | solution.py:11
  96.3 8.6 %collective-permute-start.24 = (bf16[360,128]{1,0:T(8,128)(2,1)S(1)}, bf16[360,128]{1,0:T(8,128)(2,1)S(1)}, u32[]{:S(2)}, u32[]{:S(2)}) collective-permute-start(bf16[360,128]{1,0:T(8,128)(2,1)S(1)} %get-tuple-element.106), channel_id=1, source_target_pairs={{0,4},{2,6},{4,0},{6,2},{1,5},{3,7},{5,1},{7,3},{8,12},{10,14},{12... | collective-permute-start | bytes 276488 | tf_op jit(solution)/shard_map/ppermute | solution.py:11
  97.0 8.0 %collective-permute-start.23 = (bf16[360,128]{1,0:T(8,128)(2,1)S(1)}, bf16[360,128]{1,0:T(8,128)(2,1)S(1)}, u32[]{:S(2)}, u32[]{:S(2)}) collective-permute-start(bf16[360,128]{1,0:T(8,128)(2,1)S(1)} %get-tuple-element.104), channel_id=1, source_target_pairs={{0,2},{2,0},{4,6},{6,4},{1,3},{3,1},{5,7},{7,5},{8,10},{10,8},{12,... | collective-permute-start | bytes 276488 | tf_op jit(solution)/shard_map/ppermute | solution.py:11
  (23 other events, 98.2 us)

commit v4 on v3

--- a/solution.py
+++ b/solution.py
@@ -22,11 +22,13 @@
 
 
 def ring_gather(own):
-    return [own] + [xor_send(own, "ring", s) for s in range(1, lax.axis_size("ring"))]
+    sent = [xor_send(own, "ring", s) for s in range(lax.axis_size("ring") - 1, 0, -1)]
+    return [own] + sent[::-1]
 
 
 def plane_gather(a):
-    return [a] + [xor_send(a, "expert", s) for s in range(1, lax.axis_size("expert"))]
+    sent = [xor_send(a, "expert", s) for s in range(lax.axis_size("expert") - 1, 0, -1)]
+    return [a] + sent[::-1]
 
 
 def both_cores(half):
@@ -50,23 +52,17 @@
     return keep, xor_send(give, "core", 1)
 
 
-def plane_sum(keep, other, rows):
-    chip = keep.astype(F32) + other.astype(F32)
-    far = chip[:, :, rows:].astype(BF16)
-    arrived = [
-        xor_send(far[:, :, (s - 1) * rows : s * rows], "expert", s)
-        for s in range(1, lax.axis_size("expert"))
+def plane_out(a, rows):
+    return [
+        xor_send(a[..., s * rows : (s + 1) * rows], "expert", s)
+        for s in range(lax.axis_size("expert") - 1, 0, -1)
     ]
-    return chip[:, :, :rows], arrived
 
 
-def ring_sum(mine):
-    ring = lax.axis_index("ring")
-    mine_b = mine.astype(BF16)
-    home = at(mine, ring)
-    for s in range(1, lax.axis_size("ring")):
-        home = home + xor_send(at(mine_b, ring ^ s), "ring", s).astype(F32)
-    return home.astype(BF16)
+def add_all(first, others):
+    for a in others:
+        first = first + a.astype(F32)
+    return first
 
 
 def body(tokens, grad_out, gates, routes, w_gate, w_up, w_down):
@@ -107,7 +103,7 @@
     x_next = next_places(x_near)
     x_ring = lax.optimization_barrier(x_ring)
     x_rest = plane_gather(jnp.stack(x_ring[2:]))
-    g_ring, g_near, _, _ = lax.optimization_barrier((g_ring, g_near, x_rest, x_next))
+    x_rest, x_next, g_ring, g_near = lax.optimization_barrier((x_rest, x_next, g_ring, g_near))
     g_next = next_places(g_near)
     g_rest = plane_gather(jnp.stack(g_ring[2:]))
     x = both_cores(all_places(x_near, x_next, x_ring, x_rest))
@@ -133,12 +129,27 @@
     term = term + jnp.einsum("efd,eft->dt", w_up, d_pre_up, preferred_element_type=F32)
     keep, other = swap_sum(term.astype(BF16))
     keep, other, act, d_pre_gate, d_pre_up = lax.optimization_barrier((keep, other, act, d_pre_gate, d_pre_up))
-    own, arrived = plane_sum(keep, other, rows)
-    d_gate, d_up, d_down = to_weight(d_pre_gate, x), to_weight(d_pre_up, x), to_weight(act, g)
-    own, arrived, d_gate, d_up, d_down = lax.optimization_barrier((own, arrived, d_gate, d_up, d_down))
-    for a in arrived:
-        own = own + a.astype(F32)
-    return ring_sum(own).T, d_gate, d_up, d_down
+    ring, rings = lax.axis_index("ring"), lax.axis_size("ring")
+
+    def chip(s):
+        return at(keep, ring ^ s).astype(F32) + at(other, ring ^ s).astype(F32)
+
+    far = jnp.stack([chip(s) for s in range(2, rings)])
+    far_in = plane_out(far.astype(BF16), rows)
+    near_in = xor_send(chip(1).astype(BF16), "ring", 1)
+    far_own, near = far[:, :, :rows], chip(0)
+    d_gate, d_up = to_weight(d_pre_gate, x), to_weight(d_pre_up, x)
+    far_own, far_in, near, near_in, d_gate, d_up, act = lax.optimization_barrier(
+        (far_own, far_in, near, near_in, d_gate, d_up, act)
+    )
+    far_sum = add_all(far_own, far_in).astype(BF16)
+    near = near + near_in.astype(F32)
+    arrived = [xor_send(far_sum[s - 2], "ring", s) for s in range(rings - 1, 1, -1)]
+    arrived += plane_out(near.astype(BF16), rows)
+    own = near[:, :rows]
+    d_down = to_weight(act, g)
+    own, arrived, d_down = lax.optimization_barrier((own, arrived, d_down))
+    return add_all(own, arrived).astype(BF16).T, d_gate, d_up, d_down
 
 
 def solution(mesh):

time: 106 us -> 103 us (0.972)
  waiting for transfers between devices: 24.2 us -> 19 us
  starting transfers between devices: 34.2 us -> 36.7 us
    ppermute x26 -> x29, waiting for transfers between devices: 24.2 us -> 19 us  [xor_send(): lax.ppermute(a, axis, [(i, i ^ s) for i in range(lax.axis_size(axis))])]
    ppermute x26 -> x29, starting transfers between devices: 34.2 us -> 36.7 us  [xor_send(): lax.ppermute(a, axis, [(i, i ^ s) for i in range(lax.axis_size(axis))])]
    unnamed x47 -> x50, local copies, waits for them, and re-layouts: 5.31 us -> 5.4 us
  transfers between devices with their start and end apart: 26 -> 29, of which waited for: 11 -> 8; matrix products, arithmetic and copies ran while one was open for 25% -> 26% of each run, Pallas kernels for 0% -> 0%
where the time goes in v4:
time: 103 us
  starting transfers between devices  36.7 us (36%)
  matrix products  28.5 us (28%)
  waiting for transfers between devices  19 us (18%)
  other arithmetic  9.87 us (10%)
  local copies, waits for them, and re-layouts  7.58 us (7%)
  between operations  1.35 us (1%)
    ppermute x29, starting transfers between devices, xor_send(): lax.ppermute(a, axis, [(i, i ^ s) for i in range(lax.axis_size(axis))])  36.7 us
    ppermute x29, waiting for transfers between devices, xor_send(): lax.ppermute(a, axis, [(i, i ^ s) for i in range(lax.axis_size(axis))])  19 us
    dot_general x3, matrix products, to_weight(): jnp.einsum('eft,dt->efd', a, b, preferred_element_type=F32).astype(BF16)  13.8 us
    dot_general x3, matrix products, to_hidden(): return jnp.einsum('efd,dt->eft', w, a, preferred_element_type=F32)  9.32 us
    unnamed x50, local copies, waits for them, and re-layouts  5.4 us
    select_n x10, other arithmetic, ring_order(): jnp.where(swap, pieces[i ^ bit], pieces[i])  3.37 us
    dot_general x1, matrix products, body(): jnp.einsum('efd,eft->dt', w_up, d_pre_up, preferred_element_type=F32)  2.72 us
    dot_general x1, matrix products, body(): jnp.einsum('efd,eft->dt', w_gate, d_pre_gate, preferred_element_type=F32)  2.64 us
  transfers between devices with their start and end apart: 29, of which 8 were waited for; matrix products, arithmetic and copies ran while one was open for 26% of the time, Pallas kernels for 0%

profile of v4, /device:TPU:0, one launch (start us, length us, event | category | flops | bytes accessed | tf_op | source)
XLA Modules:
  0.0 103.0 jit_solution(6185393954666409312)
XLA Ops:
  0.6 5.1 %collective-permute-start.2 = (bf16[360,128]{1,0:T(8,128)(2,1)}, bf16[360,128]{1,0:T(8,128)(2,1)S(1)}, u32[]{:S(2)}, u32[]{:S(2)}) collective-permute-start(bf16[360,128]{1,0:T(8,128)(2,1)} %bitcast.151), channel_id=1, source_target_pairs={{0,6},{2,4},{4,2},{6,0},{1,7},{3,5},{5,3},{7,1},{8,14},{10,12},{12... | collective-permute-start | bytes 276488 | tf_op jit(solution)/shard_map/ppermute | solution.py:11
  9.0 2.7 %collective-permute-start.8 = (bf16[744,128]{1,0:T(8,128)(2,1)S(1)}, bf16[744,128]{1,0:T(8,128)(2,1)S(1)}, u32[]{:S(2)}, u32[]{:S(2)}) collective-permute-start(bf16[744,128]{1,0:T(8,128)(2,1)S(1)} %constant_dynamic-update-slice_fusion), channel_id=1, source_target_pairs={{0,24},{8,16},{16,8},{24,0},{1,25},{9,17},{17,9},{25,1},{2,26},{10... | collective-permute-start | bytes 571400 | tf_op jit(solution)/shard_map/ppermute | solution.py:11
  13.7 2.5 %collective-permute-start.5 = (bf16[2,360,128]{2,1,0:T(8,128)(2,1)S(1)}, bf16[2,360,128]{2,1,0:T(8,128)(2,1)S(1)}, u32[]{:S(2)}, u32[]{:S(2)}) collective-permute-start(bf16[2,360,128]{2,1,0:T(8,128)(2,1)S(1)} %pad_maximum_fusion.11), channel_id=1, source_target_pairs={{0,24},{8,16},{16,8},{24,0},{1,25},{9,17},{17,9},{25,1},{2,26},{10... | collective-permute-start | bytes 552968 | tf_op jit(solution)/shard_map/ppermute | solution.py:11
  17.5 1.8 %collective-permute-start.3 = (bf16[2,360,128]{2,1,0:T(8,128)(2,1)S(1)}, bf16[2,360,128]{2,1,0:T(8,128)(2,1)S(1)}, u32[]{:S(2)}, u32[]{:S(2)}) collective-permute-start(bf16[2,360,128]{2,1,0:T(8,128)(2,1)S(1)} %pad_maximum_fusion.11), channel_id=1, source_target_pairs={{0,8},{8,0},{16,24},{24,16},{1,9},{9,1},{17,25},{25,17},{2,10},{10... | collective-permute-start | bytes 552968 | tf_op jit(solution)/shard_map/ppermute | solution.py:11
  19.3 4.0 %collective-permute-done.7 = bf16[744,128]{1,0:T(8,128)(2,1)S(1)} collective-permute-done((bf16[744,128]{1,0:T(8,128)(2,1)S(1)}, bf16[744,128]{1,0:T(8,128)(2,1)S(1)}, u32[]{:S(2)}, u32[]{:S(2)}) %collective-permute-start.7) | collective-permute-done | bytes 190496 | tf_op jit(solution)/shard_map/ppermute | solution.py:11
  24.9 2.5 %collective-permute-start.12 = (bf16[360,128]{1,0:T(8,128)(2,1)S(1)}, bf16[360,128]{1,0:T(8,128)(2,1)S(1)}, u32[]{:S(2)}, u32[]{:S(2)}) collective-permute-start(bf16[360,128]{1,0:T(8,128)(2,1)S(1)} %bitcast.154), channel_id=1, source_target_pairs={{0,6},{2,4},{4,2},{6,0},{1,7},{3,5},{5,3},{7,1},{8,14},{10,12},{12... | collective-permute-start | bytes 276488 | tf_op jit(solution)/shard_map/ppermute | solution.py:11
  28.0 1.6 %collective-permute-start.10 = (bf16[360,128]{1,0:T(8,128)(2,1)S(1)}, bf16[360,128]{1,0:T(8,128)(2,1)S(1)}, u32[]{:S(2)}, u32[]{:S(2)}) collective-permute-start(bf16[360,128]{1,0:T(8,128)(2,1)S(1)} %bitcast.156), channel_id=1, source_target_pairs={{0,2},{2,0},{4,6},{6,4},{1,3},{3,1},{5,7},{7,5},{8,10},{10,8},{12,... | collective-permute-start | bytes 276488 | tf_op jit(solution)/shard_map/ppermute | solution.py:11
  29.7 5.7 %collective-permute-done.12 = bf16[360,128]{1,0:T(8,128)(2,1)S(1)} collective-permute-done((bf16[360,128]{1,0:T(8,128)(2,1)S(1)}, bf16[360,128]{1,0:T(8,128)(2,1)S(1)}, u32[]{:S(2)}, u32[]{:S(2)}) %collective-permute-start.12) | collective-permute-done | bytes 92192 | tf_op jit(solution)/shard_map/ppermute | solution.py:11
  36.7 1.5 %collective-permute-start.15 = (bf16[2,360,128]{2,1,0:T(8,128)(2,1)S(1)}, bf16[2,360,128]{2,1,0:T(8,128)(2,1)S(1)}, u32[]{:S(2)}, u32[]{:S(2)}) collective-permute-start(bf16[2,360,128]{2,1,0:T(8,128)(2,1)S(1)} %pad_maximum_fusion.12), channel_id=1, source_target_pairs={{0,24},{8,16},{16,8},{24,0},{1,25},{9,17},{17,9},{25,1},{2,26},{10... | collective-permute-start | bytes 552968 | tf_op jit(solution)/shard_map/ppermute | solution.py:11
  38.2 1.8 %collective-permute-start.14 = (bf16[2,360,128]{2,1,0:T(8,128)(2,1)S(1)}, bf16[2,360,128]{2,1,0:T(8,128)(2,1)S(1)}, u32[]{:S(2)}, u32[]{:S(2)}) collective-permute-start(bf16[2,360,128]{2,1,0:T(8,128)(2,1)S(1)} %pad_maximum_fusion.12), channel_id=1, source_target_pairs={{0,16},{8,24},{16,0},{24,8},{1,17},{9,25},{17,1},{25,9},{2,18},{10... | collective-permute-start | bytes 552968 | tf_op jit(solution)/shard_map/ppermute | solution.py:11
  43.6 2.2 %slice-done.6 = s8[4194304]{0:T(1024)(128)(4,1)S(1)} async-done(((s8[4239360]{0:T(1024)(128)(4,1)}), s8[4194304]{0:T(1024)(128)(4,1)S(1)}, s32[]{:S(2)}) %slice-start.6) | async-done | bytes 4194328
  45.8 2.4 %fusion.17 = f32[512,2,360]{0,2,1:T(8,128)S(1)} fusion(bf16[2880,512,1]{1,0,2:T(8,128)(2,1)S(1)} %bitcast.137, bf16[2,360,2880]{2,1,0:T(8,128)(2,1)S(1)} %bitcast.168), kind=kOutput, calls=%fused_computation.127 | convolution fusion | flops 2123366400 | bytes 8570880 | tf_op jit(solution)/shard_map/efd,dt->eft/dot_general | solution.py:84
  48.2 4.4 %bitcast_multiply_fusion.1 = (f32[2,360,512]{2,1,0:T(8,128)S(1)}, bf16[2,360,512]{2,1,0:T(8,128)(2,1)}, f32[2,360,512]{2,1,0:T(8,128)}) fusion(f32[512,2,360]{0,2,1:T(8,128)S(1)} %fusion.17, f32[2,512]{1,0:T(2,128)S(1)} %dynamic-slice_add_fusion, bf16[2880,512,1]{1,0,2:T(8,128)(2,1)S(1)} %bitcast.138, bf16[2,360,2880]{2,1,0:T(8,128)(2,1)S(1)} %bitcast.164), kind=kOutput, calls=%fused_computation.18 | convolution fusion | flops 2128527360 | bytes 12261376 | tf_op jit(solution)/shard_map/efd,dt->eft/dot_general | solution.py:84
  55.4 2.5 %collective-permute-done.18 = bf16[4,360,512]{2,1,0:T(8,128)(2,1)} collective-permute-done((bf16[4,360,512]{2,1,0:T(8,128)(2,1)}, bf16[4,360,512]{2,1,0:T(8,128)(2,1)}, u32[]{:S(2)}, u32[]{:S(2)}) %collective-permute-start.18) | collective-permute-done | bytes 1474592 | tf_op jit(solution)/shard_map/ppermute | solution.py:11
  61.6 2.4 %bitcast_multiply_fusion = f32[2,360,512]{2,1,0:T(8,128)S(1)} fusion(bf16[2880,512,1]{1,0,2:T(8,128)(2,1)S(1)} %bitcast.141, bf16[2,360,2880]{2,1,0:T(8,128)(2,1)S(1)} %bitcast.162, f32[2,512]{1,0:T(2,128)S(1)} %dynamic-slice_add_fusion), kind=kOutput, calls=%fused_computation.17 | convolution fusion | flops 2123735040 | bytes 8574976 | tf_op jit(solution)/shard_map/efd,dt->eft/dot_general | solution.py:84
  64.7 2.6 %fusion.18 = f32[512,2880,1]{0,1,2:T(8,128)S(1)} fusion(bf16[2,360,512]{2,1,0:T(8,128)(2,1)S(1)} %get-tuple-element.91, bf16[2,360,2880]{2,1,0:T(8,128)(2,1)S(1)} %bitcast.166), kind=kOutput, calls=%fused_computation.128 | convolution fusion | flops 2123366400 | bytes 10782720 | tf_op jit(solution)/shard_map/efd,eft->dt/dot_general | solution.py:128
  67.4 2.7 %fusion = bf16[512,2880]{0,1:T(8,128)(2,1)S(1)} fusion(f32[512,2880,1]{0,1,2:T(8,128)S(1)} %fusion.18, bf16[2,360,512]{2,1,0:T(8,128)(2,1)S(1)} %get-tuple-element.92, bf16[2,360,2880]{2,1,0:T(8,128)(2,1)S(1)} %bitcast.170), kind=kOutput, calls=%fused_computation.1 | convolution fusion | flops 2126315520 | bytes 13731840 | tf_op jit(solution)/shard_map/efd,eft->dt/dot_general | solution.py:129
  71.6 3.3 %collective-permute-done.19 = bf16[4,360,512]{2,1,0:T(8,128)(2,1)S(1)} collective-permute-done((bf16[4,360,512]{2,1,0:T(8,128)(2,1)}, bf16[4,360,512]{2,1,0:T(8,128)(2,1)S(1)}, u32[]{:S(2)}, u32[]{:S(2)}) %collective-permute-start.19) | collective-permute-done | bytes 1474592 | tf_op jit(solution)/shard_map/ppermute | solution.py:11
  75.6 2.1 %collective-permute-start.22 = (bf16[2,360,128]{2,1,0:T(8,128)(2,1)S(1)}, bf16[2,360,128]{2,1,0:T(8,128)(2,1)S(1)}, u32[]{:S(2)}, u32[]{:S(2)}) collective-permute-start(bf16[2,360,128]{2,1,0:T(8,128)(2,1)S(1)} %get-tuple-element.131), channel_id=1, source_target_pairs={{0,8},{8,0},{16,24},{24,16},{1,9},{9,1},{17,25},{25,17},{2,10},{10... | collective-permute-start | bytes 552968 | tf_op jit(solution)/shard_map/ppermute | solution.py:11
  80.0 4.5 %convolution_convert_fusion.2 = bf16[2,360,2880]{2,1,0:T(8,128)(2,1)} fusion(bf16[2,360,512]{2,1,0:T(8,128)(2,1)S(1)} %copy-done.8, bf16[2880,512,1]{1,0,2:T(8,128)(2,1)S(1)} %bitcast.139), kind=kOutput, calls=%fused_computation.4 | convolution fusion | flops 2125440000 | bytes 7833600 | tf_op jit(solution)/shard_map/eft,dt->efd/dot_general | solution.py:126
  84.6 4.8 %convolution_convert_fusion.1 = bf16[2,360,2880]{2,1,0:T(8,128)(2,1)} fusion(bf16[2,360,512]{2,1,0:T(8,128)(2,1)S(1)} %copy-done.6, bf16[2880,512,1]{1,0,2:T(8,128)(2,1)S(1)} %bitcast.140), kind=kOutput, calls=%fused_computation.3 | convolution fusion | flops 2125440000 | bytes 7833600 | tf_op jit(solution)/shard_map/eft,dt->efd/dot_general | solution.py:126
  89.6 1.8 %collective-permute-start.28 = (bf16[360,128]{1,0:T(8,128)(2,1)S(1)}, bf16[360,128]{1,0:T(8,128)(2,1)S(1)}, u32[]{:S(2)}, u32[]{:S(2)}) collective-permute-start(bf16[360,128]{1,0:T(8,128)(2,1)S(1)} %get-tuple-element.134), channel_id=1, source_target_pairs={{0,8},{8,0},{16,24},{24,16},{1,9},{9,1},{17,25},{25,17},{2,10},{10... | collective-permute-start | bytes 276488 | tf_op jit(solution)/shard_map/ppermute | solution.py:11
  93.3 2.5 %collective-permute-start.25 = (bf16[360,128]{1,0:T(8,128)(2,1)S(1)}, bf16[360,128]{1,0:T(8,128)(2,1)S(1)}, u32[]{:S(2)}, u32[]{:S(2)}) collective-permute-start(bf16[360,128]{1,0:T(8,128)(2,1)S(1)} %get-tuple-element.161), channel_id=1, source_target_pairs={{0,4},{2,6},{4,0},{6,2},{1,5},{3,7},{5,1},{7,3},{8,12},{10,14},{12... | collective-permute-start | bytes 276488 | tf_op jit(solution)/shard_map/ppermute | solution.py:11
  97.0 4.5 %convolution_convert_fusion = bf16[2,360,2880]{2,1,0:T(8,128)(2,1)} fusion(bf16[2,360,512]{2,1,0:T(8,128)(2,1)S(1)} %copy-done.10, bf16[2880,512,1]{1,0,2:T(8,128)(2,1)S(1)} %bitcast.142), kind=kOutput, calls=%fused_computation.2 | convolution fusion | flops 2125440000 | bytes 7833600 | tf_op jit(solution)/shard_map/eft,dt->efd/dot_general | solution.py:126
  (154 shorter events, 29.6 us)
Async XLA Ops:
  0.6 11.5 %collective-permute-start.2 = (bf16[360,128]{1,0:T(8,128)(2,1)}, bf16[360,128]{1,0:T(8,128)(2,1)S(1)}, u32[]{:S(2)}, u32[]{:S(2)}) collective-permute-start(bf16[360,128]{1,0:T(8,128)(2,1)} %bitcast.151), channel_id=1, source_target_pairs={{0,6},{2,4},{4,2},{6,0},{1,7},{3,5},{5,3},{7,1},{8,14},{10,12},{12... | collective-permute-start | bytes 276488 | tf_op jit(solution)/shard_map/ppermute | solution.py:11
  5.7 7.9 %collective-permute-start.1 = (bf16[360,128]{1,0:T(8,128)(2,1)}, bf16[360,128]{1,0:T(8,128)(2,1)S(1)}, u32[]{:S(2)}, u32[]{:S(2)}) collective-permute-start(bf16[360,128]{1,0:T(8,128)(2,1)} %bitcast.152), channel_id=1, source_target_pairs={{0,4},{2,6},{4,0},{6,2},{1,5},{3,7},{5,1},{7,3},{8,12},{10,14},{12... | collective-permute-start | bytes 276488 | tf_op jit(solution)/shard_map/ppermute | solution.py:11
  9.0 8.6 %collective-permute-start.8 = (bf16[744,128]{1,0:T(8,128)(2,1)S(1)}, bf16[744,128]{1,0:T(8,128)(2,1)S(1)}, u32[]{:S(2)}, u32[]{:S(2)}) collective-permute-start(bf16[744,128]{1,0:T(8,128)(2,1)S(1)} %constant_dynamic-update-slice_fusion), channel_id=1, source_target_pairs={{0,24},{8,16},{16,8},{24,0},{1,25},{9,17},{17,9},{25,1},{2,26},{10... | collective-permute-start | bytes 571400 | tf_op jit(solution)/shard_map/ppermute | solution.py:11
  11.6 11.7 %collective-permute-start.7 = (bf16[744,128]{1,0:T(8,128)(2,1)S(1)}, bf16[744,128]{1,0:T(8,128)(2,1)S(1)}, u32[]{:S(2)}, u32[]{:S(2)}) collective-permute-start(bf16[744,128]{1,0:T(8,128)(2,1)S(1)} %constant_dynamic-update-slice_fusion), channel_id=1, source_target_pairs={{0,16},{8,24},{16,0},{24,8},{1,17},{9,25},{17,1},{25,9},{2,18},{10... | collective-permute-start | bytes 571400 | tf_op jit(solution)/shard_map/ppermute | solution.py:11
  12.1 11.2 %collective-permute-start.6 = (bf16[744,128]{1,0:T(8,128)(2,1)S(1)}, bf16[744,128]{1,0:T(8,128)(2,1)S(1)}, u32[]{:S(2)}, u32[]{:S(2)}) collective-permute-start(bf16[744,128]{1,0:T(8,128)(2,1)S(1)} %constant_dynamic-update-slice_fusion), channel_id=1, source_target_pairs={{0,8},{8,0},{16,24},{24,16},{1,9},{9,1},{17,25},{25,17},{2,10},{10... | collective-permute-start | bytes 571400 | tf_op jit(solution)/shard_map/ppermute | solution.py:11
  13.7 13.7 %collective-permute-start.5 = (bf16[2,360,128]{2,1,0:T(8,128)(2,1)S(1)}, bf16[2,360,128]{2,1,0:T(8,128)(2,1)S(1)}, u32[]{:S(2)}, u32[]{:S(2)}) collective-permute-start(bf16[2,360,128]{2,1,0:T(8,128)(2,1)S(1)} %pad_maximum_fusion.11), channel_id=1, source_target_pairs={{0,24},{8,16},{16,8},{24,0},{1,25},{9,17},{17,9},{25,1},{2,26},{10... | collective-permute-start | bytes 552968 | tf_op jit(solution)/shard_map/ppermute | solution.py:11
  16.2 11.8 %collective-permute-start.4 = (bf16[2,360,128]{2,1,0:T(8,128)(2,1)S(1)}, bf16[2,360,128]{2,1,0:T(8,128)(2,1)S(1)}, u32[]{:S(2)}, u32[]{:S(2)}) collective-permute-start(bf16[2,360,128]{2,1,0:T(8,128)(2,1)S(1)} %pad_maximum_fusion.11), channel_id=1, source_target_pairs={{0,16},{8,24},{16,0},{24,8},{1,17},{9,25},{17,1},{25,9},{2,18},{10... | collective-permute-start | bytes 552968 | tf_op jit(solution)/shard_map/ppermute | solution.py:11
  17.5 12.1 %collective-permute-start.3 = (bf16[2,360,128]{2,1,0:T(8,128)(2,1)S(1)}, bf16[2,360,128]{2,1,0:T(8,128)(2,1)S(1)}, u32[]{:S(2)}, u32[]{:S(2)}) collective-permute-start(bf16[2,360,128]{2,1,0:T(8,128)(2,1)S(1)} %pad_maximum_fusion.11), channel_id=1, source_target_pairs={{0,8},{8,0},{16,24},{24,16},{1,9},{9,1},{17,25},{25,17},{2,10},{10... | collective-permute-start | bytes 552968 | tf_op jit(solution)/shard_map/ppermute | solution.py:11
  23.6 12.5 %collective-permute-start.9 = (bf16[3,360,128]{2,1,0:T(8,128)(2,1)S(1)}, bf16[3,360,128]{2,1,0:T(8,128)(2,1)S(1)}, u32[]{:S(2)}, u32[]{:S(2)}) collective-permute-start(bf16[3,360,128]{2,1,0:T(8,128)(2,1)S(1)} %pad_maximum_fusion.9), channel_id=1, source_target_pairs={{0,2},{2,0},{4,6},{6,4},{1,3},{3,1},{5,7},{7,5},{8,10},{10,8},{12,... | collective-permute-start | bytes 829448 | tf_op jit(solution)/shard_map/ppermute | solution.py:11
  24.9 10.5 %collective-permute-start.12 = (bf16[360,128]{1,0:T(8,128)(2,1)S(1)}, bf16[360,128]{1,0:T(8,128)(2,1)S(1)}, u32[]{:S(2)}, u32[]{:S(2)}) collective-permute-start(bf16[360,128]{1,0:T(8,128)(2,1)S(1)} %bitcast.154), channel_id=1, source_target_pairs={{0,6},{2,4},{4,2},{6,0},{1,7},{3,5},{5,3},{7,1},{8,14},{10,12},{12... | collective-permute-start | bytes 276488 | tf_op jit(solution)/shard_map/ppermute | solution.py:11
  27.4 8.0 %collective-permute-start.11 = (bf16[360,128]{1,0:T(8,128)(2,1)S(1)}, bf16[360,128]{1,0:T(8,128)(2,1)S(1)}, u32[]{:S(2)}, u32[]{:S(2)}) collective-permute-start(bf16[360,128]{1,0:T(8,128)(2,1)S(1)} %bitcast.155), channel_id=1, source_target_pairs={{0,4},{2,6},{4,0},{6,2},{1,5},{3,7},{5,1},{7,3},{8,12},{10,14},{12... | collective-permute-start | bytes 276488 | tf_op jit(solution)/shard_map/ppermute | solution.py:11
  28.0 8.1 %collective-permute-start.10 = (bf16[360,128]{1,0:T(8,128)(2,1)S(1)}, bf16[360,128]{1,0:T(8,128)(2,1)S(1)}, u32[]{:S(2)}, u32[]{:S(2)}) collective-permute-start(bf16[360,128]{1,0:T(8,128)(2,1)S(1)} %bitcast.156), channel_id=1, source_target_pairs={{0,2},{2,0},{4,6},{6,4},{1,3},{3,1},{5,7},{7,5},{8,10},{10,8},{12,... | collective-permute-start | bytes 276488 | tf_op jit(solution)/shard_map/ppermute | solution.py:11
  36.7 16.0 %collective-permute-start.15 = (bf16[2,360,128]{2,1,0:T(8,128)(2,1)S(1)}, bf16[2,360,128]{2,1,0:T(8,128)(2,1)S(1)}, u32[]{:S(2)}, u32[]{:S(2)}) collective-permute-start(bf16[2,360,128]{2,1,0:T(8,128)(2,1)S(1)} %pad_maximum_fusion.12), channel_id=1, source_target_pairs={{0,24},{8,16},{16,8},{24,0},{1,25},{9,17},{17,9},{25,1},{2,26},{10... | collective-permute-start | bytes 552968 | tf_op jit(solution)/shard_map/ppermute | solution.py:11
  38.2 14.5 %collective-permute-start.14 = (bf16[2,360,128]{2,1,0:T(8,128)(2,1)S(1)}, bf16[2,360,128]{2,1,0:T(8,128)(2,1)S(1)}, u32[]{:S(2)}, u32[]{:S(2)}) collective-permute-start(bf16[2,360,128]{2,1,0:T(8,128)(2,1)S(1)} %pad_maximum_fusion.12), channel_id=1, source_target_pairs={{0,16},{8,24},{16,0},{24,8},{1,17},{9,25},{17,1},{25,9},{2,18},{10... | collective-permute-start | bytes 552968 | tf_op jit(solution)/shard_map/ppermute | solution.py:11
  40.0 12.7 %collective-permute-start.13 = (bf16[2,360,128]{2,1,0:T(8,128)(2,1)S(1)}, bf16[2,360,128]{2,1,0:T(8,128)(2,1)S(1)}, u32[]{:S(2)}, u32[]{:S(2)}) collective-permute-start(bf16[2,360,128]{2,1,0:T(8,128)(2,1)S(1)} %pad_maximum_fusion.12), channel_id=1, source_target_pairs={{0,8},{8,0},{16,24},{24,16},{1,9},{9,1},{17,25},{25,17},{2,10},{10... | collective-permute-start | bytes 552968 | tf_op jit(solution)/shard_map/ppermute | solution.py:11
  40.3 12.4 %collective-permute-start.16 = (bf16[3,360,128]{2,1,0:T(8,128)(2,1)S(1)}, bf16[3,360,128]{2,1,0:T(8,128)(2,1)S(1)}, u32[]{:S(2)}, u32[]{:S(2)}) collective-permute-start(bf16[3,360,128]{2,1,0:T(8,128)(2,1)S(1)} %pad_maximum_fusion.10), channel_id=1, source_target_pairs={{0,2},{2,0},{4,6},{6,4},{1,3},{3,1},{5,7},{7,5},{8,10},{10,8},{12,... | collective-permute-start | bytes 829448 | tf_op jit(solution)/shard_map/ppermute | solution.py:11
  75.6 13.7 %collective-permute-start.22 = (bf16[2,360,128]{2,1,0:T(8,128)(2,1)S(1)}, bf16[2,360,128]{2,1,0:T(8,128)(2,1)S(1)}, u32[]{:S(2)}, u32[]{:S(2)}) collective-permute-start(bf16[2,360,128]{2,1,0:T(8,128)(2,1)S(1)} %get-tuple-element.131), channel_id=1, source_target_pairs={{0,8},{8,0},{16,24},{24,16},{1,9},{9,1},{17,25},{25,17},{2,10},{10... | collective-permute-start | bytes 552968 | tf_op jit(solution)/shard_map/ppermute | solution.py:11
  77.7 11.7 %collective-permute-start.21 = (bf16[2,360,128]{2,1,0:T(8,128)(2,1)S(1)}, bf16[2,360,128]{2,1,0:T(8,128)(2,1)S(1)}, u32[]{:S(2)}, u32[]{:S(2)}) collective-permute-start(bf16[2,360,128]{2,1,0:T(8,128)(2,1)S(1)} %get-tuple-element.132), channel_id=1, source_target_pairs={{0,16},{8,24},{16,0},{24,8},{1,17},{9,25},{17,1},{25,9},{2,18},{10... | collective-permute-start | bytes 552968 | tf_op jit(solution)/shard_map/ppermute | solution.py:11
  77.8 11.6 %collective-permute-start.20 = (bf16[2,360,128]{2,1,0:T(8,128)(2,1)S(1)}, bf16[2,360,128]{2,1,0:T(8,128)(2,1)S(1)}, u32[]{:S(2)}, u32[]{:S(2)}) collective-permute-start(bf16[2,360,128]{2,1,0:T(8,128)(2,1)S(1)} %get-tuple-element.133), channel_id=1, source_target_pairs={{0,24},{8,16},{16,8},{24,0},{1,25},{9,17},{17,9},{25,1},{2,26},{10... | collective-permute-start | bytes 552968 | tf_op jit(solution)/shard_map/ppermute | solution.py:11
  79.2 10.2 %collective-permute-start.23 = (bf16[360,512]{1,0:T(8,128)(2,1)S(1)}, bf16[360,512]{1,0:T(8,128)(2,1)S(1)}, u32[]{:S(2)}, u32[]{:S(2)}) collective-permute-start(bf16[360,512]{1,0:T(8,128)(2,1)S(1)} %get-tuple-element.112), channel_id=1, source_target_pairs={{0,2},{2,0},{4,6},{6,4},{1,3},{3,1},{5,7},{7,5},{8,10},{10,8},{12,... | collective-permute-start | bytes 1105928 | tf_op jit(solution)/shard_map/ppermute | solution.py:11
  89.6 11.9 %collective-permute-start.28 = (bf16[360,128]{1,0:T(8,128)(2,1)S(1)}, bf16[360,128]{1,0:T(8,128)(2,1)S(1)}, u32[]{:S(2)}, u32[]{:S(2)}) collective-permute-start(bf16[360,128]{1,0:T(8,128)(2,1)S(1)} %get-tuple-element.134), channel_id=1, source_target_pairs={{0,8},{8,0},{16,24},{24,16},{1,9},{9,1},{17,25},{25,17},{2,10},{10... | collective-permute-start | bytes 276488 | tf_op jit(solution)/shard_map/ppermute | solution.py:11
  91.5 10.1 %collective-permute-start.27 = (bf16[360,128]{1,0:T(8,128)(2,1)S(1)}, bf16[360,128]{1,0:T(8,128)(2,1)S(1)}, u32[]{:S(2)}, u32[]{:S(2)}) collective-permute-start(bf16[360,128]{1,0:T(8,128)(2,1)S(1)} %get-tuple-element.135), channel_id=1, source_target_pairs={{0,16},{8,24},{16,0},{24,8},{1,17},{9,25},{17,1},{25,9},{2,18},{10... | collective-permute-start | bytes 276488 | tf_op jit(solution)/shard_map/ppermute | solution.py:11
  91.7 9.9 %collective-permute-start.26 = (bf16[360,128]{1,0:T(8,128)(2,1)S(1)}, bf16[360,128]{1,0:T(8,128)(2,1)S(1)}, u32[]{:S(2)}, u32[]{:S(2)}) collective-permute-start(bf16[360,128]{1,0:T(8,128)(2,1)S(1)} %get-tuple-element.136), channel_id=1, source_target_pairs={{0,24},{8,16},{16,8},{24,0},{1,25},{9,17},{17,9},{25,1},{2,26},{10... | collective-permute-start | bytes 276488 | tf_op jit(solution)/shard_map/ppermute | solution.py:11
  93.3 9.0 %collective-permute-start.25 = (bf16[360,128]{1,0:T(8,128)(2,1)S(1)}, bf16[360,128]{1,0:T(8,128)(2,1)S(1)}, u32[]{:S(2)}, u32[]{:S(2)}) collective-permute-start(bf16[360,128]{1,0:T(8,128)(2,1)S(1)} %get-tuple-element.161), channel_id=1, source_target_pairs={{0,4},{2,6},{4,0},{6,2},{1,5},{3,7},{5,1},{7,3},{8,12},{10,14},{12... | collective-permute-start | bytes 276488 | tf_op jit(solution)/shard_map/ppermute | solution.py:11
  (26 other events, 116.4 us)

commit v5 on v4

--- a/solution.py
+++ b/solution.py
@@ -86,7 +86,7 @@
     x_own, g_own = tokens.T, grad_out.T
     x_ring = ring_gather(x_own)
     early = plane_gather(jnp.concatenate([x_own, g_own] + parts, 0))
-    early, g_first = lax.optimization_barrier((early, g_own))
+    early[1], g_first = lax.optimization_barrier((early[1], g_own))
     g_ring = ring_gather(g_first)
 
     def next_places(near):
@@ -103,7 +103,7 @@
     x_next = next_places(x_near)
     x_ring = lax.optimization_barrier(x_ring)
     x_rest = plane_gather(jnp.stack(x_ring[2:]))
-    x_rest, x_next, g_ring, g_near = lax.optimization_barrier((x_rest, x_next, g_ring, g_near))
+    g_ring, g_near, x_rest[1], x_rest[-1] = lax.optimization_barrier((g_ring, g_near, x_rest[1], x_rest[-1]))
     g_next = next_places(g_near)
     g_rest = plane_gather(jnp.stack(g_ring[2:]))
     x = both_cores(all_places(x_near, x_next, x_ring, x_rest))

time: 103 us -> 101 us (0.981)
  waiting for transfers between devices: 19 us -> 15.6 us
  starting transfers between devices: 36.7 us -> 38.2 us
    ppermute x29, waiting for transfers between devices: 19 us -> 15.6 us  [xor_send(): lax.ppermute(a, axis, [(i, i ^ s) for i in range(lax.axis_size(axis))])]
    ppermute x29, starting transfers between devices: 36.7 us -> 38.2 us  [xor_send(): lax.ppermute(a, axis, [(i, i ^ s) for i in range(lax.axis_size(axis))])]
    unnamed x50 -> x49, local copies, waits for them, and re-layouts: 5.4 us -> 4.88 us
  transfers between devices with their start and end apart: 29 -> 29, of which waited for: 8 -> 8; matrix products, arithmetic and copies ran while one was open for 26% -> 27% of each run, Pallas kernels for 0% -> 0%
where the time goes in v5:
time: 101 us
  starting transfers between devices  38.2 us (38%)
  matrix products  28.5 us (28%)
  waiting for transfers between devices  15.6 us (15%)
  other arithmetic  9.99 us (10%)
  local copies, waits for them, and re-layouts  7.22 us (7%)
  between operations  1.31 us (1%)
    ppermute x29, starting transfers between devices, xor_send(): lax.ppermute(a, axis, [(i, i ^ s) for i in range(lax.axis_size(axis))])  38.2 us
    ppermute x29, waiting for transfers between devices, xor_send(): lax.ppermute(a, axis, [(i, i ^ s) for i in range(lax.axis_size(axis))])  15.6 us
    dot_general x3, matrix products, to_weight(): jnp.einsum('eft,dt->efd', a, b, preferred_element_type=F32).astype(BF16)  13.8 us
    dot_general x3, matrix products, to_hidden(): return jnp.einsum('efd,dt->eft', w, a, preferred_element_type=F32)  9.32 us
    unnamed x49, local copies, waits for them, and re-layouts  4.88 us
    select_n x10, other arithmetic, ring_order(): jnp.where(swap, pieces[i ^ bit], pieces[i])  3.37 us
    dot_general x1, matrix products, body(): jnp.einsum('efd,eft->dt', w_up, d_pre_up, preferred_element_type=F32)  2.72 us
    dot_general x1, matrix products, body(): jnp.einsum('efd,eft->dt', w_gate, d_pre_gate, preferred_element_type=F32)  2.64 us
  transfers between devices with their start and end apart: 29, of which 8 were waited for; matrix products, arithmetic and copies ran while one was open for 27% of the time, Pallas kernels for 0%

profile of v5, /device:TPU:0, one launch (start us, length us, event | category | flops | bytes accessed | tf_op | source)
XLA Modules:
  0.0 100.8 jit_solution(13564143502860818588)
XLA Ops:
  0.6 5.1 %collective-permute-start.8 = (bf16[360,128]{1,0:T(8,128)(2,1)}, bf16[360,128]{1,0:T(8,128)(2,1)S(1)}, u32[]{:S(2)}, u32[]{:S(2)}) collective-permute-start(bf16[360,128]{1,0:T(8,128)(2,1)} %bitcast.132), channel_id=1, source_target_pairs={{0,6},{2,4},{4,2},{6,0},{1,7},{3,5},{5,3},{7,1},{8,14},{10,12},{12... | collective-permute-start | bytes 276488 | tf_op jit(solution)/shard_map/ppermute | solution.py:11
  9.0 1.7 %collective-permute-start = (bf16[744,128]{1,0:T(8,128)(2,1)S(1)}, bf16[744,128]{1,0:T(8,128)(2,1)S(1)}, u32[]{:S(2)}, u32[]{:S(2)}) collective-permute-start(bf16[744,128]{1,0:T(8,128)(2,1)S(1)} %get-tuple-element.100), channel_id=1, source_target_pairs={{0,8},{8,0},{16,24},{24,16},{1,9},{9,1},{17,25},{25,17},{2,10},{10... | collective-permute-start | bytes 571400 | tf_op jit(solution)/shard_map/ppermute | solution.py:11
  13.7 2.5 %collective-permute-start.10 = (bf16[2,360,128]{2,1,0:T(8,128)(2,1)S(1)}, bf16[2,360,128]{2,1,0:T(8,128)(2,1)S(1)}, u32[]{:S(2)}, u32[]{:S(2)}) collective-permute-start(bf16[2,360,128]{2,1,0:T(8,128)(2,1)S(1)} %pad_maximum_fusion.11), channel_id=1, source_target_pairs={{0,24},{8,16},{16,8},{24,0},{1,25},{9,17},{17,9},{25,1},{2,26},{10... | collective-permute-start | bytes 552968 | tf_op jit(solution)/shard_map/ppermute | solution.py:11
  16.8 3.6 %collective-permute-start.3 = (bf16[360,128]{1,0:T(8,128)(2,1)}, bf16[360,128]{1,0:T(8,128)(2,1)S(1)}, u32[]{:S(2)}, u32[]{:S(2)}) collective-permute-start(bf16[360,128]{1,0:T(8,128)(2,1)} %bitcast.140), channel_id=1, source_target_pairs={{0,6},{2,4},{4,2},{6,0},{1,7},{3,5},{5,3},{7,1},{8,14},{10,12},{12... | collective-permute-start | bytes 276488 | tf_op jit(solution)/shard_map/ppermute | solution.py:11
  20.4 1.7 %collective-permute-done.5 = bf16[744,128]{1,0:T(8,128)(2,1)S(1)} collective-permute-done((bf16[744,128]{1,0:T(8,128)(2,1)S(1)}, bf16[744,128]{1,0:T(8,128)(2,1)S(1)}, u32[]{:S(2)}, u32[]{:S(2)}) %collective-permute-start.5) | collective-permute-done | bytes 190496 | tf_op jit(solution)/shard_map/ppermute | solution.py:11
  22.0 2.2 %collective-permute-start.2 = (bf16[360,128]{1,0:T(8,128)(2,1)}, bf16[360,128]{1,0:T(8,128)(2,1)S(1)}, u32[]{:S(2)}, u32[]{:S(2)}) collective-permute-start(bf16[360,128]{1,0:T(8,128)(2,1)} %bitcast.141), channel_id=1, source_target_pairs={{0,4},{2,6},{4,0},{6,2},{1,5},{3,7},{5,1},{7,3},{8,12},{10,14},{12... | collective-permute-start | bytes 276488 | tf_op jit(solution)/shard_map/ppermute | solution.py:11
  25.1 1.6 %collective-permute-start.16 = (bf16[3,360,128]{2,1,0:T(8,128)(2,1)S(1)}, bf16[3,360,128]{2,1,0:T(8,128)(2,1)S(1)}, u32[]{:S(2)}, u32[]{:S(2)}) collective-permute-start(bf16[3,360,128]{2,1,0:T(8,128)(2,1)S(1)} %pad_maximum_fusion.10), channel_id=1, source_target_pairs={{0,2},{2,0},{4,6},{6,4},{1,3},{3,1},{5,7},{7,5},{8,10},{10,8},{12,... | collective-permute-start | bytes 829448 | tf_op jit(solution)/shard_map/ppermute | solution.py:11
  28.5 4.7 %collective-permute-done.1 = bf16[360,128]{1,0:T(8,128)(2,1)S(1)} collective-permute-done((bf16[360,128]{1,0:T(8,128)(2,1)S(1)}, bf16[360,128]{1,0:T(8,128)(2,1)S(1)}, u32[]{:S(2)}, u32[]{:S(2)}) %collective-permute-start.1) | collective-permute-done | bytes 92192 | tf_op jit(solution)/shard_map/ppermute | solution.py:11
  33.2 1.7 %collective-permute-start.13 = (bf16[2,360,128]{2,1,0:T(8,128)(2,1)S(1)}, bf16[2,360,128]{2,1,0:T(8,128)(2,1)S(1)}, u32[]{:S(2)}, u32[]{:S(2)}) collective-permute-start(bf16[2,360,128]{2,1,0:T(8,128)(2,1)S(1)} %pad_maximum_fusion.12), channel_id=1, source_target_pairs={{0,24},{8,16},{16,8},{24,0},{1,25},{9,17},{17,9},{25,1},{2,26},{10... | collective-permute-start | bytes 552968 | tf_op jit(solution)/shard_map/ppermute | solution.py:11
  41.5 1.8 %slice-done.6 = s8[4194304]{0:T(1024)(128)(4,1)S(1)} async-done(((s8[4239360]{0:T(1024)(128)(4,1)}), s8[4194304]{0:T(1024)(128)(4,1)S(1)}, s32[]{:S(2)}) %slice-start.6) | async-done | bytes 4194328
  43.3 2.4 %fusion.17 = f32[512,2,360]{0,2,1:T(8,128)S(1)} fusion(bf16[2880,512,1]{1,0,2:T(8,128)(2,1)S(1)} %bitcast.149, bf16[2,360,2880]{2,1,0:T(8,128)(2,1)S(1)} %bitcast.178), kind=kOutput, calls=%fused_computation.122 | convolution fusion | flops 2123366400 | bytes 8570880 | tf_op jit(solution)/shard_map/efd,dt->eft/dot_general | solution.py:84
  45.8 4.4 %bitcast_multiply_fusion.1 = (f32[2,360,512]{2,1,0:T(8,128)S(1)}, bf16[2,360,512]{2,1,0:T(8,128)(2,1)}, f32[2,360,512]{2,1,0:T(8,128)}) fusion(f32[512,2,360]{0,2,1:T(8,128)S(1)} %fusion.17, f32[2,512]{1,0:T(2,128)S(1)} %dynamic-slice_add_fusion, bf16[2880,512,1]{1,0,2:T(8,128)(2,1)S(1)} %bitcast.150, bf16[2,360,2880]{2,1,0:T(8,128)(2,1)S(1)} %bitcast.174), kind=kOutput, calls=%fused_computation.18 | convolution fusion | flops 2128527360 | bytes 12261376 | tf_op jit(solution)/shard_map/efd,dt->eft/dot_general | solution.py:84
  53.1 2.4 %collective-permute-done.18 = bf16[4,360,512]{2,1,0:T(8,128)(2,1)} collective-permute-done((bf16[4,360,512]{2,1,0:T(8,128)(2,1)}, bf16[4,360,512]{2,1,0:T(8,128)(2,1)}, u32[]{:S(2)}, u32[]{:S(2)}) %collective-permute-start.18) | collective-permute-done | bytes 1474592 | tf_op jit(solution)/shard_map/ppermute | solution.py:11
  59.2 2.4 %bitcast_multiply_fusion = f32[2,360,512]{2,1,0:T(8,128)S(1)} fusion(bf16[2880,512,1]{1,0,2:T(8,128)(2,1)S(1)} %bitcast.153, bf16[2,360,2880]{2,1,0:T(8,128)(2,1)S(1)} %bitcast.172, f32[2,512]{1,0:T(2,128)S(1)} %dynamic-slice_add_fusion), kind=kOutput, calls=%fused_computation.17 | convolution fusion | flops 2123735040 | bytes 8574976 | tf_op jit(solution)/shard_map/efd,dt->eft/dot_general | solution.py:84
  62.3 2.6 %fusion.18 = f32[512,2880,1]{0,1,2:T(8,128)S(1)} fusion(bf16[2,360,512]{2,1,0:T(8,128)(2,1)S(1)} %get-tuple-element.79, bf16[2,360,2880]{2,1,0:T(8,128)(2,1)S(1)} %bitcast.176), kind=kOutput, calls=%fused_computation.123 | convolution fusion | flops 2123366400 | bytes 10782720 | tf_op jit(solution)/shard_map/efd,eft->dt/dot_general | solution.py:128
  65.0 2.7 %fusion = bf16[512,2880]{0,1:T(8,128)(2,1)S(1)} fusion(f32[512,2880,1]{0,1,2:T(8,128)S(1)} %fusion.18, bf16[2,360,512]{2,1,0:T(8,128)(2,1)S(1)} %get-tuple-element.80, bf16[2,360,2880]{2,1,0:T(8,128)(2,1)S(1)} %bitcast.180), kind=kOutput, calls=%fused_computation.1 | convolution fusion | flops 2126315520 | bytes 13731840 | tf_op jit(solution)/shard_map/efd,eft->dt/dot_general | solution.py:129
  69.2 3.3 %collective-permute-done.19 = bf16[4,360,512]{2,1,0:T(8,128)(2,1)S(1)} collective-permute-done((bf16[4,360,512]{2,1,0:T(8,128)(2,1)}, bf16[4,360,512]{2,1,0:T(8,128)(2,1)S(1)}, u32[]{:S(2)}, u32[]{:S(2)}) %collective-permute-start.19) | collective-permute-done | bytes 1474592 | tf_op jit(solution)/shard_map/ppermute | solution.py:11
  73.2 1.6 %collective-permute-start.22 = (bf16[2,360,128]{2,1,0:T(8,128)(2,1)S(1)}, bf16[2,360,128]{2,1,0:T(8,128)(2,1)S(1)}, u32[]{:S(2)}, u32[]{:S(2)}) collective-permute-start(bf16[2,360,128]{2,1,0:T(8,128)(2,1)S(1)} %get-tuple-element.125), channel_id=1, source_target_pairs={{0,8},{8,0},{16,24},{24,16},{1,9},{9,1},{17,25},{25,17},{2,10},{10... | collective-permute-start | bytes 552968 | tf_op jit(solution)/shard_map/ppermute | solution.py:11
  78.0 4.5 %convolution_convert_fusion.2 = bf16[2,360,2880]{2,1,0:T(8,128)(2,1)} fusion(bf16[2,360,512]{2,1,0:T(8,128)(2,1)S(1)} %copy-done.10, bf16[2880,512,1]{1,0,2:T(8,128)(2,1)S(1)} %bitcast.151), kind=kOutput, calls=%fused_computation.4 | convolution fusion | flops 2125440000 | bytes 7833600 | tf_op jit(solution)/shard_map/eft,dt->efd/dot_general | solution.py:126
  82.5 4.8 %convolution_convert_fusion.1 = bf16[2,360,2880]{2,1,0:T(8,128)(2,1)} fusion(bf16[2,360,512]{2,1,0:T(8,128)(2,1)S(1)} %copy-done.8, bf16[2880,512,1]{1,0,2:T(8,128)(2,1)S(1)} %bitcast.152), kind=kOutput, calls=%fused_computation.3 | convolution fusion | flops 2125440000 | bytes 7833600 | tf_op jit(solution)/shard_map/eft,dt->efd/dot_general | solution.py:126
  87.6 1.6 %collective-permute-start.28 = (bf16[360,128]{1,0:T(8,128)(2,1)S(1)}, bf16[360,128]{1,0:T(8,128)(2,1)S(1)}, u32[]{:S(2)}, u32[]{:S(2)}) collective-permute-start(bf16[360,128]{1,0:T(8,128)(2,1)S(1)} %get-tuple-element.128), channel_id=1, source_target_pairs={{0,8},{8,0},{16,24},{24,16},{1,9},{9,1},{17,25},{25,17},{2,10},{10... | collective-permute-start | bytes 276488 | tf_op jit(solution)/shard_map/ppermute | solution.py:11
  89.6 1.5 %collective-permute-start.26 = (bf16[360,128]{1,0:T(8,128)(2,1)S(1)}, bf16[360,128]{1,0:T(8,128)(2,1)S(1)}, u32[]{:S(2)}, u32[]{:S(2)}) collective-permute-start(bf16[360,128]{1,0:T(8,128)(2,1)S(1)} %get-tuple-element.130), channel_id=1, source_target_pairs={{0,24},{8,16},{16,8},{24,0},{1,25},{9,17},{17,9},{25,1},{2,26},{10... | collective-permute-start | bytes 276488 | tf_op jit(solution)/shard_map/ppermute | solution.py:11
  91.3 2.3 %collective-permute-start.25 = (bf16[360,128]{1,0:T(8,128)(2,1)S(1)}, bf16[360,128]{1,0:T(8,128)(2,1)S(1)}, u32[]{:S(2)}, u32[]{:S(2)}) collective-permute-start(bf16[360,128]{1,0:T(8,128)(2,1)S(1)} %get-tuple-element.152), channel_id=1, source_target_pairs={{0,4},{2,6},{4,0},{6,2},{1,5},{3,7},{5,1},{7,3},{8,12},{10,14},{12... | collective-permute-start | bytes 276488 | tf_op jit(solution)/shard_map/ppermute | solution.py:11
  94.5 4.5 %convolution_convert_fusion = bf16[2,360,2880]{2,1,0:T(8,128)(2,1)} fusion(bf16[2,360,512]{2,1,0:T(8,128)(2,1)S(1)} %copy-done.11, bf16[2880,512,1]{1,0,2:T(8,128)(2,1)S(1)} %bitcast.154), kind=kOutput, calls=%fused_computation.2 | convolution fusion | flops 2125440000 | bytes 7833600 | tf_op jit(solution)/shard_map/eft,dt->efd/dot_general | solution.py:126
  (153 shorter events, 31.8 us)
Async XLA Ops:
  0.6 11.5 %collective-permute-start.8 = (bf16[360,128]{1,0:T(8,128)(2,1)}, bf16[360,128]{1,0:T(8,128)(2,1)S(1)}, u32[]{:S(2)}, u32[]{:S(2)}) collective-permute-start(bf16[360,128]{1,0:T(8,128)(2,1)} %bitcast.132), channel_id=1, source_target_pairs={{0,6},{2,4},{4,2},{6,0},{1,7},{3,5},{5,3},{7,1},{8,14},{10,12},{12... | collective-permute-start | bytes 276488 | tf_op jit(solution)/shard_map/ppermute | solution.py:11
  5.8 7.9 %collective-permute-start.7 = (bf16[360,128]{1,0:T(8,128)(2,1)}, bf16[360,128]{1,0:T(8,128)(2,1)S(1)}, u32[]{:S(2)}, u32[]{:S(2)}) collective-permute-start(bf16[360,128]{1,0:T(8,128)(2,1)} %bitcast.133), channel_id=1, source_target_pairs={{0,4},{2,6},{4,0},{6,2},{1,5},{3,7},{5,1},{7,3},{8,12},{10,14},{12... | collective-permute-start | bytes 276488 | tf_op jit(solution)/shard_map/ppermute | solution.py:11
  5.8 7.9 %collective-permute-start.6 = (bf16[360,128]{1,0:T(8,128)(2,1)}, bf16[360,128]{1,0:T(8,128)(2,1)S(1)}, u32[]{:S(2)}, u32[]{:S(2)}) collective-permute-start(bf16[360,128]{1,0:T(8,128)(2,1)} %bitcast.134), channel_id=1, source_target_pairs={{0,2},{2,0},{4,6},{6,4},{1,3},{3,1},{5,7},{7,5},{8,10},{10,8},{12,... | collective-permute-start | bytes 276488 | tf_op jit(solution)/shard_map/ppermute | solution.py:11
  9.0 7.8 %collective-permute-start = (bf16[744,128]{1,0:T(8,128)(2,1)S(1)}, bf16[744,128]{1,0:T(8,128)(2,1)S(1)}, u32[]{:S(2)}, u32[]{:S(2)}) collective-permute-start(bf16[744,128]{1,0:T(8,128)(2,1)S(1)} %get-tuple-element.100), channel_id=1, source_target_pairs={{0,8},{8,0},{16,24},{24,16},{1,9},{9,1},{17,25},{25,17},{2,10},{10... | collective-permute-start | bytes 571400 | tf_op jit(solution)/shard_map/ppermute | solution.py:11
  10.7 11.4 %collective-permute-start.5 = (bf16[744,128]{1,0:T(8,128)(2,1)S(1)}, bf16[744,128]{1,0:T(8,128)(2,1)S(1)}, u32[]{:S(2)}, u32[]{:S(2)}) collective-permute-start(bf16[744,128]{1,0:T(8,128)(2,1)S(1)} %get-tuple-element.100), channel_id=1, source_target_pairs={{0,24},{8,16},{16,8},{24,0},{1,25},{9,17},{17,9},{25,1},{2,26},{10... | collective-permute-start | bytes 571400 | tf_op jit(solution)/shard_map/ppermute | solution.py:11
  12.2 12.8 %collective-permute-start.4 = (bf16[744,128]{1,0:T(8,128)(2,1)S(1)}, bf16[744,128]{1,0:T(8,128)(2,1)S(1)}, u32[]{:S(2)}, u32[]{:S(2)}) collective-permute-start(bf16[744,128]{1,0:T(8,128)(2,1)S(1)} %get-tuple-element.100), channel_id=1, source_target_pairs={{0,16},{8,24},{16,0},{24,8},{1,17},{9,25},{17,1},{25,9},{2,18},{10... | collective-permute-start | bytes 571400 | tf_op jit(solution)/shard_map/ppermute | solution.py:11
  13.7 13.0 %collective-permute-start.10 = (bf16[2,360,128]{2,1,0:T(8,128)(2,1)S(1)}, bf16[2,360,128]{2,1,0:T(8,128)(2,1)S(1)}, u32[]{:S(2)}, u32[]{:S(2)}) collective-permute-start(bf16[2,360,128]{2,1,0:T(8,128)(2,1)S(1)} %pad_maximum_fusion.11), channel_id=1, source_target_pairs={{0,24},{8,16},{16,8},{24,0},{1,25},{9,17},{17,9},{25,1},{2,26},{10... | collective-permute-start | bytes 552968 | tf_op jit(solution)/shard_map/ppermute | solution.py:11
  16.3 11.1 %collective-permute-start.9 = (bf16[2,360,128]{2,1,0:T(8,128)(2,1)S(1)}, bf16[2,360,128]{2,1,0:T(8,128)(2,1)S(1)}, u32[]{:S(2)}, u32[]{:S(2)}) collective-permute-start(bf16[2,360,128]{2,1,0:T(8,128)(2,1)S(1)} %pad_maximum_fusion.11), channel_id=1, source_target_pairs={{0,8},{8,0},{16,24},{24,16},{1,9},{9,1},{17,25},{25,17},{2,10},{10... | collective-permute-start | bytes 552968 | tf_op jit(solution)/shard_map/ppermute | solution.py:11
  16.8 11.7 %collective-permute-start.3 = (bf16[360,128]{1,0:T(8,128)(2,1)}, bf16[360,128]{1,0:T(8,128)(2,1)S(1)}, u32[]{:S(2)}, u32[]{:S(2)}) collective-permute-start(bf16[360,128]{1,0:T(8,128)(2,1)} %bitcast.140), channel_id=1, source_target_pairs={{0,6},{2,4},{4,2},{6,0},{1,7},{3,5},{5,3},{7,1},{8,14},{10,12},{12... | collective-permute-start | bytes 276488 | tf_op jit(solution)/shard_map/ppermute | solution.py:11
  22.0 6.5 %collective-permute-start.2 = (bf16[360,128]{1,0:T(8,128)(2,1)}, bf16[360,128]{1,0:T(8,128)(2,1)S(1)}, u32[]{:S(2)}, u32[]{:S(2)}) collective-permute-start(bf16[360,128]{1,0:T(8,128)(2,1)} %bitcast.141), channel_id=1, source_target_pairs={{0,4},{2,6},{4,0},{6,2},{1,5},{3,7},{5,1},{7,3},{8,12},{10,14},{12... | collective-permute-start | bytes 276488 | tf_op jit(solution)/shard_map/ppermute | solution.py:11
  25.1 11.7 %collective-permute-start.16 = (bf16[3,360,128]{2,1,0:T(8,128)(2,1)S(1)}, bf16[3,360,128]{2,1,0:T(8,128)(2,1)S(1)}, u32[]{:S(2)}, u32[]{:S(2)}) collective-permute-start(bf16[3,360,128]{2,1,0:T(8,128)(2,1)S(1)} %pad_maximum_fusion.10), channel_id=1, source_target_pairs={{0,2},{2,0},{4,6},{6,4},{1,3},{3,1},{5,7},{7,5},{8,10},{10,8},{12,... | collective-permute-start | bytes 829448 | tf_op jit(solution)/shard_map/ppermute | solution.py:11
  27.4 9.6 %collective-permute-start.15 = (bf16[2,360,128]{2,1,0:T(8,128)(2,1)S(1)}, bf16[2,360,128]{2,1,0:T(8,128)(2,1)S(1)}, u32[]{:S(2)}, u32[]{:S(2)}) collective-permute-start(bf16[2,360,128]{2,1,0:T(8,128)(2,1)S(1)} %pad_maximum_fusion.11), channel_id=1, source_target_pairs={{0,16},{8,24},{16,0},{24,8},{1,17},{9,25},{17,1},{25,9},{2,18},{10... | collective-permute-start | bytes 552968 | tf_op jit(solution)/shard_map/ppermute | solution.py:11
  33.2 17.1 %collective-permute-start.13 = (bf16[2,360,128]{2,1,0:T(8,128)(2,1)S(1)}, bf16[2,360,128]{2,1,0:T(8,128)(2,1)S(1)}, u32[]{:S(2)}, u32[]{:S(2)}) collective-permute-start(bf16[2,360,128]{2,1,0:T(8,128)(2,1)S(1)} %pad_maximum_fusion.12), channel_id=1, source_target_pairs={{0,24},{8,16},{16,8},{24,0},{1,25},{9,17},{17,9},{25,1},{2,26},{10... | collective-permute-start | bytes 552968 | tf_op jit(solution)/shard_map/ppermute | solution.py:11
  35.0 15.3 %collective-permute-start.12 = (bf16[2,360,128]{2,1,0:T(8,128)(2,1)S(1)}, bf16[2,360,128]{2,1,0:T(8,128)(2,1)S(1)}, u32[]{:S(2)}, u32[]{:S(2)}) collective-permute-start(bf16[2,360,128]{2,1,0:T(8,128)(2,1)S(1)} %pad_maximum_fusion.12), channel_id=1, source_target_pairs={{0,16},{8,24},{16,0},{24,8},{1,17},{9,25},{17,1},{25,9},{2,18},{10... | collective-permute-start | bytes 552968 | tf_op jit(solution)/shard_map/ppermute | solution.py:11
  36.3 14.0 %collective-permute-start.11 = (bf16[2,360,128]{2,1,0:T(8,128)(2,1)S(1)}, bf16[2,360,128]{2,1,0:T(8,128)(2,1)S(1)}, u32[]{:S(2)}, u32[]{:S(2)}) collective-permute-start(bf16[2,360,128]{2,1,0:T(8,128)(2,1)S(1)} %pad_maximum_fusion.12), channel_id=1, source_target_pairs={{0,8},{8,0},{16,24},{24,16},{1,9},{9,1},{17,25},{25,17},{2,10},{10... | collective-permute-start | bytes 552968 | tf_op jit(solution)/shard_map/ppermute | solution.py:11
  37.2 13.1 %collective-permute-start.14 = (bf16[3,360,128]{2,1,0:T(8,128)(2,1)S(1)}, bf16[3,360,128]{2,1,0:T(8,128)(2,1)S(1)}, u32[]{:S(2)}, u32[]{:S(2)}) collective-permute-start(bf16[3,360,128]{2,1,0:T(8,128)(2,1)S(1)} %pad_maximum_fusion.9), channel_id=1, source_target_pairs={{0,2},{2,0},{4,6},{6,4},{1,3},{3,1},{5,7},{7,5},{8,10},{10,8},{12,... | collective-permute-start | bytes 829448 | tf_op jit(solution)/shard_map/ppermute | solution.py:11
  73.2 14.1 %collective-permute-start.22 = (bf16[2,360,128]{2,1,0:T(8,128)(2,1)S(1)}, bf16[2,360,128]{2,1,0:T(8,128)(2,1)S(1)}, u32[]{:S(2)}, u32[]{:S(2)}) collective-permute-start(bf16[2,360,128]{2,1,0:T(8,128)(2,1)S(1)} %get-tuple-element.125), channel_id=1, source_target_pairs={{0,8},{8,0},{16,24},{24,16},{1,9},{9,1},{17,25},{25,17},{2,10},{10... | collective-permute-start | bytes 552968 | tf_op jit(solution)/shard_map/ppermute | solution.py:11
  74.8 12.5 %collective-permute-start.21 = (bf16[2,360,128]{2,1,0:T(8,128)(2,1)S(1)}, bf16[2,360,128]{2,1,0:T(8,128)(2,1)S(1)}, u32[]{:S(2)}, u32[]{:S(2)}) collective-permute-start(bf16[2,360,128]{2,1,0:T(8,128)(2,1)S(1)} %get-tuple-element.126), channel_id=1, source_target_pairs={{0,16},{8,24},{16,0},{24,8},{1,17},{9,25},{17,1},{25,9},{2,18},{10... | collective-permute-start | bytes 552968 | tf_op jit(solution)/shard_map/ppermute | solution.py:11
  75.5 11.8 %collective-permute-start.20 = (bf16[2,360,128]{2,1,0:T(8,128)(2,1)S(1)}, bf16[2,360,128]{2,1,0:T(8,128)(2,1)S(1)}, u32[]{:S(2)}, u32[]{:S(2)}) collective-permute-start(bf16[2,360,128]{2,1,0:T(8,128)(2,1)S(1)} %get-tuple-element.127), channel_id=1, source_target_pairs={{0,24},{8,16},{16,8},{24,0},{1,25},{9,17},{17,9},{25,1},{2,26},{10... | collective-permute-start | bytes 552968 | tf_op jit(solution)/shard_map/ppermute | solution.py:11
  76.8 10.6 %collective-permute-start.23 = (bf16[360,512]{1,0:T(8,128)(2,1)S(1)}, bf16[360,512]{1,0:T(8,128)(2,1)S(1)}, u32[]{:S(2)}, u32[]{:S(2)}) collective-permute-start(bf16[360,512]{1,0:T(8,128)(2,1)S(1)} %get-tuple-element.106), channel_id=1, source_target_pairs={{0,2},{2,0},{4,6},{6,4},{1,3},{3,1},{5,7},{7,5},{8,10},{10,8},{12,... | collective-permute-start | bytes 1105928 | tf_op jit(solution)/shard_map/ppermute | solution.py:11
  87.6 11.5 %collective-permute-start.28 = (bf16[360,128]{1,0:T(8,128)(2,1)S(1)}, bf16[360,128]{1,0:T(8,128)(2,1)S(1)}, u32[]{:S(2)}, u32[]{:S(2)}) collective-permute-start(bf16[360,128]{1,0:T(8,128)(2,1)S(1)} %get-tuple-element.128), channel_id=1, source_target_pairs={{0,8},{8,0},{16,24},{24,16},{1,9},{9,1},{17,25},{25,17},{2,10},{10... | collective-permute-start | bytes 276488 | tf_op jit(solution)/shard_map/ppermute | solution.py:11
  89.1 9.9 %collective-permute-start.27 = (bf16[360,128]{1,0:T(8,128)(2,1)S(1)}, bf16[360,128]{1,0:T(8,128)(2,1)S(1)}, u32[]{:S(2)}, u32[]{:S(2)}) collective-permute-start(bf16[360,128]{1,0:T(8,128)(2,1)S(1)} %get-tuple-element.129), channel_id=1, source_target_pairs={{0,16},{8,24},{16,0},{24,8},{1,17},{9,25},{17,1},{25,9},{2,18},{10... | collective-permute-start | bytes 276488 | tf_op jit(solution)/shard_map/ppermute | solution.py:11
  89.6 9.4 %collective-permute-start.26 = (bf16[360,128]{1,0:T(8,128)(2,1)S(1)}, bf16[360,128]{1,0:T(8,128)(2,1)S(1)}, u32[]{:S(2)}, u32[]{:S(2)}) collective-permute-start(bf16[360,128]{1,0:T(8,128)(2,1)S(1)} %get-tuple-element.130), channel_id=1, source_target_pairs={{0,24},{8,16},{16,8},{24,0},{1,25},{9,17},{17,9},{25,1},{2,26},{10... | collective-permute-start | bytes 276488 | tf_op jit(solution)/shard_map/ppermute | solution.py:11
  91.3 7.8 %collective-permute-start.25 = (bf16[360,128]{1,0:T(8,128)(2,1)S(1)}, bf16[360,128]{1,0:T(8,128)(2,1)S(1)}, u32[]{:S(2)}, u32[]{:S(2)}) collective-permute-start(bf16[360,128]{1,0:T(8,128)(2,1)S(1)} %get-tuple-element.152), channel_id=1, source_target_pairs={{0,4},{2,6},{4,0},{6,2},{1,5},{3,7},{5,1},{7,3},{8,12},{10,14},{12... | collective-permute-start | bytes 276488 | tf_op jit(solution)/shard_map/ppermute | solution.py:11
  (27 other events, 138.6 us)

commit v6 on v5

--- a/solution.py
+++ b/solution.py
@@ -86,7 +86,7 @@
     x_own, g_own = tokens.T, grad_out.T
     x_ring = ring_gather(x_own)
     early = plane_gather(jnp.concatenate([x_own, g_own] + parts, 0))
-    early[1], g_first = lax.optimization_barrier((early[1], g_own))
+    x_ring[1], g_first = lax.optimization_barrier((x_ring[1], g_own))
     g_ring = ring_gather(g_first)
 
     def next_places(near):

time: 101 us -> 102 us (level)
  starting transfers between devices: 38.2 us -> 39.3 us
    ppermute x29, starting transfers between devices: 38.2 us -> 39.3 us  [xor_send(): lax.ppermute(a, axis, [(i, i ^ s) for i in range(lax.axis_size(axis))])]
  transfers between devices with their start and end apart: 29 -> 29, of which waited for: 8 -> 7; matrix products, arithmetic and copies ran while one was open for 27% -> 27% of each run, Pallas kernels for 0% -> 0%
where the time goes in v6:
time: 102 us
  starting transfers between devices  39.3 us (39%)
  matrix products  28.5 us (28%)
  waiting for transfers between devices  15.3 us (15%)
  other arithmetic  9.98 us (10%)
  local copies, waits for them, and re-layouts  7.22 us (7%)
  between operations  1.31 us (1%)
    ppermute x29, starting transfers between devices, xor_send(): lax.ppermute(a, axis, [(i, i ^ s) for i in range(lax.axis_size(axis))])  39.3 us
    ppermute x29, waiting for transfers between devices, xor_send(): lax.ppermute(a, axis, [(i, i ^ s) for i in range(lax.axis_size(axis))])  15.3 us
    dot_general x3, matrix products, to_weight(): jnp.einsum('eft,dt->efd', a, b, preferred_element_type=F32).astype(BF16)  13.8 us
    dot_general x3, matrix products, to_hidden(): return jnp.einsum('efd,dt->eft', w, a, preferred_element_type=F32)  9.32 us
    unnamed x49, local copies, waits for them, and re-layouts  4.88 us
    select_n x10, other arithmetic, ring_order(): jnp.where(swap, pieces[i ^ bit], pieces[i])  3.36 us
    dot_general x1, matrix products, body(): jnp.einsum('efd,eft->dt', w_up, d_pre_up, preferred_element_type=F32)  2.72 us
    dot_general x1, matrix products, body(): jnp.einsum('efd,eft->dt', w_gate, d_pre_gate, preferred_element_type=F32)  2.64 us
  transfers between devices with their start and end apart: 29, of which 7 were waited for; matrix products, arithmetic and copies ran while one was open for 27% of the time, Pallas kernels for 0%

profile of v6, /device:TPU:0, one launch (start us, length us, event | category | flops | bytes accessed | tf_op | source)
XLA Modules:
  0.0 101.6 jit_solution(3857978994609781904)
XLA Ops:
  0.6 5.1 %collective-permute-start.8 = (bf16[360,128]{1,0:T(8,128)(2,1)}, bf16[360,128]{1,0:T(8,128)(2,1)S(1)}, u32[]{:S(2)}, u32[]{:S(2)}) collective-permute-start(bf16[360,128]{1,0:T(8,128)(2,1)} %bitcast.132), channel_id=1, source_target_pairs={{0,6},{2,4},{4,2},{6,0},{1,7},{3,5},{5,3},{7,1},{8,14},{10,12},{12... | collective-permute-start | bytes 276488 | tf_op jit(solution)/shard_map/ppermute | solution.py:11
  9.0 2.7 %collective-permute-start.6 = (bf16[744,128]{1,0:T(8,128)(2,1)S(1)}, bf16[744,128]{1,0:T(8,128)(2,1)S(1)}, u32[]{:S(2)}, u32[]{:S(2)}) collective-permute-start(bf16[744,128]{1,0:T(8,128)(2,1)S(1)} %get-tuple-element.100), channel_id=1, source_target_pairs={{0,24},{8,16},{16,8},{24,0},{1,25},{9,17},{17,9},{25,1},{2,26},{10... | collective-permute-start | bytes 571400 | tf_op jit(solution)/shard_map/ppermute | solution.py:11
  13.5 2.8 %collective-permute-start.3 = (bf16[360,128]{1,0:T(8,128)(2,1)}, bf16[360,128]{1,0:T(8,128)(2,1)S(1)}, u32[]{:S(2)}, u32[]{:S(2)}) collective-permute-start(bf16[360,128]{1,0:T(8,128)(2,1)} %bitcast.140), channel_id=1, source_target_pairs={{0,6},{2,4},{4,2},{6,0},{1,7},{3,5},{5,3},{7,1},{8,14},{10,12},{12... | collective-permute-start | bytes 276488 | tf_op jit(solution)/shard_map/ppermute | solution.py:11
  17.4 2.9 %collective-permute-start.10 = (bf16[2,360,128]{2,1,0:T(8,128)(2,1)S(1)}, bf16[2,360,128]{2,1,0:T(8,128)(2,1)S(1)}, u32[]{:S(2)}, u32[]{:S(2)}) collective-permute-start(bf16[2,360,128]{2,1,0:T(8,128)(2,1)S(1)} %pad_maximum_fusion.11), channel_id=1, source_target_pairs={{0,24},{8,16},{16,8},{24,0},{1,25},{9,17},{17,9},{25,1},{2,26},{10... | collective-permute-start | bytes 552968 | tf_op jit(solution)/shard_map/ppermute | solution.py:11
  20.8 2.0 %collective-permute-start.9 = (bf16[2,360,128]{2,1,0:T(8,128)(2,1)S(1)}, bf16[2,360,128]{2,1,0:T(8,128)(2,1)S(1)}, u32[]{:S(2)}, u32[]{:S(2)}) collective-permute-start(bf16[2,360,128]{2,1,0:T(8,128)(2,1)S(1)} %pad_maximum_fusion.11), channel_id=1, source_target_pairs={{0,8},{8,0},{16,24},{24,16},{1,9},{9,1},{17,25},{25,17},{2,10},{10... | collective-permute-start | bytes 552968 | tf_op jit(solution)/shard_map/ppermute | solution.py:11
  23.0 1.7 %collective-permute-start.16 = (bf16[3,360,128]{2,1,0:T(8,128)(2,1)S(1)}, bf16[3,360,128]{2,1,0:T(8,128)(2,1)S(1)}, u32[]{:S(2)}, u32[]{:S(2)}) collective-permute-start(bf16[3,360,128]{2,1,0:T(8,128)(2,1)S(1)} %pad_maximum_fusion.10), channel_id=1, source_target_pairs={{0,2},{2,0},{4,6},{6,4},{1,3},{3,1},{5,7},{7,5},{8,10},{10,8},{12,... | collective-permute-start | bytes 829448 | tf_op jit(solution)/shard_map/ppermute | solution.py:11
  26.3 6.9 %collective-permute-done.1 = bf16[360,128]{1,0:T(8,128)(2,1)S(1)} collective-permute-done((bf16[360,128]{1,0:T(8,128)(2,1)S(1)}, bf16[360,128]{1,0:T(8,128)(2,1)S(1)}, u32[]{:S(2)}, u32[]{:S(2)}) %collective-permute-start.1) | collective-permute-done | bytes 92192 | tf_op jit(solution)/shard_map/ppermute | solution.py:11
  35.2 1.6 %collective-permute-start.11 = (bf16[2,360,128]{2,1,0:T(8,128)(2,1)S(1)}, bf16[2,360,128]{2,1,0:T(8,128)(2,1)S(1)}, u32[]{:S(2)}, u32[]{:S(2)}) collective-permute-start(bf16[2,360,128]{2,1,0:T(8,128)(2,1)S(1)} %pad_maximum_fusion.12), channel_id=1, source_target_pairs={{0,8},{8,0},{16,24},{24,16},{1,9},{9,1},{17,25},{25,17},{2,10},{10... | collective-permute-start | bytes 552968 | tf_op jit(solution)/shard_map/ppermute | solution.py:11
  37.2 1.7 %collective-permute-start.14 = (bf16[3,360,128]{2,1,0:T(8,128)(2,1)S(1)}, bf16[3,360,128]{2,1,0:T(8,128)(2,1)S(1)}, u32[]{:S(2)}, u32[]{:S(2)}) collective-permute-start(bf16[3,360,128]{2,1,0:T(8,128)(2,1)S(1)} %pad_maximum_fusion.9), channel_id=1, source_target_pairs={{0,2},{2,0},{4,6},{6,4},{1,3},{3,1},{5,7},{7,5},{8,10},{10,8},{12,... | collective-permute-start | bytes 829448 | tf_op jit(solution)/shard_map/ppermute | solution.py:11
  41.6 1.8 %slice-done.6 = s8[4194304]{0:T(1024)(128)(4,1)S(1)} async-done(((s8[4239360]{0:T(1024)(128)(4,1)}), s8[4194304]{0:T(1024)(128)(4,1)S(1)}, s32[]{:S(2)}) %slice-start.6) | async-done | bytes 4194328
  43.4 2.4 %fusion.17 = f32[512,2,360]{0,2,1:T(8,128)S(1)} fusion(bf16[2880,512,1]{1,0,2:T(8,128)(2,1)S(1)} %bitcast.149, bf16[2,360,2880]{2,1,0:T(8,128)(2,1)S(1)} %bitcast.178), kind=kOutput, calls=%fused_computation.122 | convolution fusion | flops 2123366400 | bytes 8570880 | tf_op jit(solution)/shard_map/efd,dt->eft/dot_general | solution.py:84
  45.9 4.4 %bitcast_multiply_fusion.1 = (f32[2,360,512]{2,1,0:T(8,128)S(1)}, bf16[2,360,512]{2,1,0:T(8,128)(2,1)}, f32[2,360,512]{2,1,0:T(8,128)}) fusion(f32[512,2,360]{0,2,1:T(8,128)S(1)} %fusion.17, f32[2,512]{1,0:T(2,128)S(1)} %dynamic-slice_add_fusion, bf16[2880,512,1]{1,0,2:T(8,128)(2,1)S(1)} %bitcast.150, bf16[2,360,2880]{2,1,0:T(8,128)(2,1)S(1)} %bitcast.174), kind=kOutput, calls=%fused_computation.18 | convolution fusion | flops 2128527360 | bytes 12261376 | tf_op jit(solution)/shard_map/efd,dt->eft/dot_general | solution.py:84
  53.2 2.4 %collective-permute-done.18 = bf16[4,360,512]{2,1,0:T(8,128)(2,1)} collective-permute-done((bf16[4,360,512]{2,1,0:T(8,128)(2,1)}, bf16[4,360,512]{2,1,0:T(8,128)(2,1)}, u32[]{:S(2)}, u32[]{:S(2)}) %collective-permute-start.18) | collective-permute-done | bytes 1474592 | tf_op jit(solution)/shard_map/ppermute | solution.py:11
  59.2 2.4 %bitcast_multiply_fusion = f32[2,360,512]{2,1,0:T(8,128)S(1)} fusion(bf16[2880,512,1]{1,0,2:T(8,128)(2,1)S(1)} %bitcast.153, bf16[2,360,2880]{2,1,0:T(8,128)(2,1)S(1)} %bitcast.172, f32[2,512]{1,0:T(2,128)S(1)} %dynamic-slice_add_fusion), kind=kOutput, calls=%fused_computation.17 | convolution fusion | flops 2123735040 | bytes 8574976 | tf_op jit(solution)/shard_map/efd,dt->eft/dot_general | solution.py:84
  62.4 2.6 %fusion.18 = f32[512,2880,1]{0,1,2:T(8,128)S(1)} fusion(bf16[2,360,512]{2,1,0:T(8,128)(2,1)S(1)} %get-tuple-element.79, bf16[2,360,2880]{2,1,0:T(8,128)(2,1)S(1)} %bitcast.176), kind=kOutput, calls=%fused_computation.123 | convolution fusion | flops 2123366400 | bytes 10782720 | tf_op jit(solution)/shard_map/efd,eft->dt/dot_general | solution.py:128
  65.1 2.7 %fusion = bf16[512,2880]{0,1:T(8,128)(2,1)S(1)} fusion(f32[512,2880,1]{0,1,2:T(8,128)S(1)} %fusion.18, bf16[2,360,512]{2,1,0:T(8,128)(2,1)S(1)} %get-tuple-element.80, bf16[2,360,2880]{2,1,0:T(8,128)(2,1)S(1)} %bitcast.180), kind=kOutput, calls=%fused_computation.1 | convolution fusion | flops 2126315520 | bytes 13731840 | tf_op jit(solution)/shard_map/efd,eft->dt/dot_general | solution.py:129
  69.2 3.3 %collective-permute-done.19 = bf16[4,360,512]{2,1,0:T(8,128)(2,1)S(1)} collective-permute-done((bf16[4,360,512]{2,1,0:T(8,128)(2,1)}, bf16[4,360,512]{2,1,0:T(8,128)(2,1)S(1)}, u32[]{:S(2)}, u32[]{:S(2)}) %collective-permute-start.19) | collective-permute-done | bytes 1474592 | tf_op jit(solution)/shard_map/ppermute | solution.py:11
  75.0 1.8 %collective-permute-start.20 = (bf16[2,360,128]{2,1,0:T(8,128)(2,1)S(1)}, bf16[2,360,128]{2,1,0:T(8,128)(2,1)S(1)}, u32[]{:S(2)}, u32[]{:S(2)}) collective-permute-start(bf16[2,360,128]{2,1,0:T(8,128)(2,1)S(1)} %get-tuple-element.127), channel_id=1, source_target_pairs={{0,24},{8,16},{16,8},{24,0},{1,25},{9,17},{17,9},{25,1},{2,26},{10... | collective-permute-start | bytes 552968 | tf_op jit(solution)/shard_map/ppermute | solution.py:11
  78.4 4.5 %convolution_convert_fusion.2 = bf16[2,360,2880]{2,1,0:T(8,128)(2,1)} fusion(bf16[2,360,512]{2,1,0:T(8,128)(2,1)S(1)} %copy-done.10, bf16[2880,512,1]{1,0,2:T(8,128)(2,1)S(1)} %bitcast.151), kind=kOutput, calls=%fused_computation.4 | convolution fusion | flops 2125440000 | bytes 7833600 | tf_op jit(solution)/shard_map/eft,dt->efd/dot_general | solution.py:126
  82.9 4.8 %convolution_convert_fusion.1 = bf16[2,360,2880]{2,1,0:T(8,128)(2,1)} fusion(bf16[2,360,512]{2,1,0:T(8,128)(2,1)S(1)} %copy-done.8, bf16[2880,512,1]{1,0,2:T(8,128)(2,1)S(1)} %bitcast.152), kind=kOutput, calls=%fused_computation.3 | convolution fusion | flops 2125440000 | bytes 7833600 | tf_op jit(solution)/shard_map/eft,dt->efd/dot_general | solution.py:126
  89.9 1.6 %collective-permute-start.26 = (bf16[360,128]{1,0:T(8,128)(2,1)S(1)}, bf16[360,128]{1,0:T(8,128)(2,1)S(1)}, u32[]{:S(2)}, u32[]{:S(2)}) collective-permute-start(bf16[360,128]{1,0:T(8,128)(2,1)S(1)} %get-tuple-element.130), channel_id=1, source_target_pairs={{0,24},{8,16},{16,8},{24,0},{1,25},{9,17},{17,9},{25,1},{2,26},{10... | collective-permute-start | bytes 276488 | tf_op jit(solution)/shard_map/ppermute | solution.py:11
  91.7 2.8 %collective-permute-start.25 = (bf16[360,128]{1,0:T(8,128)(2,1)S(1)}, bf16[360,128]{1,0:T(8,128)(2,1)S(1)}, u32[]{:S(2)}, u32[]{:S(2)}) collective-permute-start(bf16[360,128]{1,0:T(8,128)(2,1)S(1)} %get-tuple-element.152), channel_id=1, source_target_pairs={{0,4},{2,6},{4,0},{6,2},{1,5},{3,7},{5,1},{7,3},{8,12},{10,14},{12... | collective-permute-start | bytes 276488 | tf_op jit(solution)/shard_map/ppermute | solution.py:11
  94.5 4.5 %convolution_convert_fusion = bf16[2,360,2880]{2,1,0:T(8,128)(2,1)} fusion(bf16[2,360,512]{2,1,0:T(8,128)(2,1)S(1)} %copy-done.11, bf16[2880,512,1]{1,0,2:T(8,128)(2,1)S(1)} %bitcast.154), kind=kOutput, calls=%fused_computation.2 | convolution fusion | flops 2125440000 | bytes 7833600 | tf_op jit(solution)/shard_map/eft,dt->efd/dot_general | solution.py:126
  99.2 1.7 %collective-permute-done.24 = bf16[360,128]{1,0:T(8,128)(2,1)S(1)} collective-permute-done((bf16[360,128]{1,0:T(8,128)(2,1)S(1)}, bf16[360,128]{1,0:T(8,128)(2,1)S(1)}, u32[]{:S(2)}, u32[]{:S(2)}) %collective-permute-start.24) | collective-permute-done | bytes 92192 | tf_op jit(solution)/shard_map/ppermute | solution.py:11
  (153 shorter events, 29.2 us)
Async XLA Ops:
  0.6 12.8 %collective-permute-start.8 = (bf16[360,128]{1,0:T(8,128)(2,1)}, bf16[360,128]{1,0:T(8,128)(2,1)S(1)}, u32[]{:S(2)}, u32[]{:S(2)}) collective-permute-start(bf16[360,128]{1,0:T(8,128)(2,1)} %bitcast.132), channel_id=1, source_target_pairs={{0,6},{2,4},{4,2},{6,0},{1,7},{3,5},{5,3},{7,1},{8,14},{10,12},{12... | collective-permute-start | bytes 276488 | tf_op jit(solution)/shard_map/ppermute | solution.py:11
  5.8 10.5 %collective-permute-start.7 = (bf16[360,128]{1,0:T(8,128)(2,1)}, bf16[360,128]{1,0:T(8,128)(2,1)S(1)}, u32[]{:S(2)}, u32[]{:S(2)}) collective-permute-start(bf16[360,128]{1,0:T(8,128)(2,1)} %bitcast.133), channel_id=1, source_target_pairs={{0,4},{2,6},{4,0},{6,2},{1,5},{3,7},{5,1},{7,3},{8,12},{10,14},{12... | collective-permute-start | bytes 276488 | tf_op jit(solution)/shard_map/ppermute | solution.py:11
  9.0 8.4 %collective-permute-start.6 = (bf16[744,128]{1,0:T(8,128)(2,1)S(1)}, bf16[744,128]{1,0:T(8,128)(2,1)S(1)}, u32[]{:S(2)}, u32[]{:S(2)}) collective-permute-start(bf16[744,128]{1,0:T(8,128)(2,1)S(1)} %get-tuple-element.100), channel_id=1, source_target_pairs={{0,24},{8,16},{16,8},{24,0},{1,25},{9,17},{17,9},{25,1},{2,26},{10... | collective-permute-start | bytes 571400 | tf_op jit(solution)/shard_map/ppermute | solution.py:11
  11.6 9.2 %collective-permute-start.5 = (bf16[744,128]{1,0:T(8,128)(2,1)S(1)}, bf16[744,128]{1,0:T(8,128)(2,1)S(1)}, u32[]{:S(2)}, u32[]{:S(2)}) collective-permute-start(bf16[744,128]{1,0:T(8,128)(2,1)S(1)} %get-tuple-element.100), channel_id=1, source_target_pairs={{0,16},{8,24},{16,0},{24,8},{1,17},{9,25},{17,1},{25,9},{2,18},{10... | collective-permute-start | bytes 571400 | tf_op jit(solution)/shard_map/ppermute | solution.py:11
  12.1 10.7 %collective-permute-start.4 = (bf16[744,128]{1,0:T(8,128)(2,1)S(1)}, bf16[744,128]{1,0:T(8,128)(2,1)S(1)}, u32[]{:S(2)}, u32[]{:S(2)}) collective-permute-start(bf16[744,128]{1,0:T(8,128)(2,1)S(1)} %get-tuple-element.100), channel_id=1, source_target_pairs={{0,8},{8,0},{16,24},{24,16},{1,9},{9,1},{17,25},{25,17},{2,10},{10... | collective-permute-start | bytes 571400 | tf_op jit(solution)/shard_map/ppermute | solution.py:11
  13.5 11.2 %collective-permute-start.3 = (bf16[360,128]{1,0:T(8,128)(2,1)}, bf16[360,128]{1,0:T(8,128)(2,1)S(1)}, u32[]{:S(2)}, u32[]{:S(2)}) collective-permute-start(bf16[360,128]{1,0:T(8,128)(2,1)} %bitcast.140), channel_id=1, source_target_pairs={{0,6},{2,4},{4,2},{6,0},{1,7},{3,5},{5,3},{7,1},{8,14},{10,12},{12... | collective-permute-start | bytes 276488 | tf_op jit(solution)/shard_map/ppermute | solution.py:11
  16.3 9.0 %collective-permute-start.2 = (bf16[360,128]{1,0:T(8,128)(2,1)}, bf16[360,128]{1,0:T(8,128)(2,1)S(1)}, u32[]{:S(2)}, u32[]{:S(2)}) collective-permute-start(bf16[360,128]{1,0:T(8,128)(2,1)} %bitcast.141), channel_id=1, source_target_pairs={{0,4},{2,6},{4,0},{6,2},{1,5},{3,7},{5,1},{7,3},{8,12},{10,14},{12... | collective-permute-start | bytes 276488 | tf_op jit(solution)/shard_map/ppermute | solution.py:11
  17.4 15.8 %collective-permute-start.10 = (bf16[2,360,128]{2,1,0:T(8,128)(2,1)S(1)}, bf16[2,360,128]{2,1,0:T(8,128)(2,1)S(1)}, u32[]{:S(2)}, u32[]{:S(2)}) collective-permute-start(bf16[2,360,128]{2,1,0:T(8,128)(2,1)S(1)} %pad_maximum_fusion.11), channel_id=1, source_target_pairs={{0,24},{8,16},{16,8},{24,0},{1,25},{9,17},{17,9},{25,1},{2,26},{10... | collective-permute-start | bytes 552968 | tf_op jit(solution)/shard_map/ppermute | solution.py:11
  20.8 12.4 %collective-permute-start.9 = (bf16[2,360,128]{2,1,0:T(8,128)(2,1)S(1)}, bf16[2,360,128]{2,1,0:T(8,128)(2,1)S(1)}, u32[]{:S(2)}, u32[]{:S(2)}) collective-permute-start(bf16[2,360,128]{2,1,0:T(8,128)(2,1)S(1)} %pad_maximum_fusion.11), channel_id=1, source_target_pairs={{0,8},{8,0},{16,24},{24,16},{1,9},{9,1},{17,25},{25,17},{2,10},{10... | collective-permute-start | bytes 552968 | tf_op jit(solution)/shard_map/ppermute | solution.py:11
  23.0 13.8 %collective-permute-start.16 = (bf16[3,360,128]{2,1,0:T(8,128)(2,1)S(1)}, bf16[3,360,128]{2,1,0:T(8,128)(2,1)S(1)}, u32[]{:S(2)}, u32[]{:S(2)}) collective-permute-start(bf16[3,360,128]{2,1,0:T(8,128)(2,1)S(1)} %pad_maximum_fusion.10), channel_id=1, source_target_pairs={{0,2},{2,0},{4,6},{6,4},{1,3},{3,1},{5,7},{7,5},{8,10},{10,8},{12,... | collective-permute-start | bytes 829448 | tf_op jit(solution)/shard_map/ppermute | solution.py:11
  24.7 8.5 %collective-permute-start.1 = (bf16[360,128]{1,0:T(8,128)(2,1)S(1)}, bf16[360,128]{1,0:T(8,128)(2,1)S(1)}, u32[]{:S(2)}, u32[]{:S(2)}) collective-permute-start(bf16[360,128]{1,0:T(8,128)(2,1)S(1)} %bitcast.142), channel_id=1, source_target_pairs={{0,2},{2,0},{4,6},{6,4},{1,3},{3,1},{5,7},{7,5},{8,10},{10,8},{12,... | collective-permute-start | bytes 276488 | tf_op jit(solution)/shard_map/ppermute | solution.py:11
  25.3 11.7 %collective-permute-start.15 = (bf16[2,360,128]{2,1,0:T(8,128)(2,1)S(1)}, bf16[2,360,128]{2,1,0:T(8,128)(2,1)S(1)}, u32[]{:S(2)}, u32[]{:S(2)}) collective-permute-start(bf16[2,360,128]{2,1,0:T(8,128)(2,1)S(1)} %pad_maximum_fusion.11), channel_id=1, source_target_pairs={{0,16},{8,24},{16,0},{24,8},{1,17},{9,25},{17,1},{25,9},{2,18},{10... | collective-permute-start | bytes 552968 | tf_op jit(solution)/shard_map/ppermute | solution.py:11
  33.2 17.1 %collective-permute-start.13 = (bf16[2,360,128]{2,1,0:T(8,128)(2,1)S(1)}, bf16[2,360,128]{2,1,0:T(8,128)(2,1)S(1)}, u32[]{:S(2)}, u32[]{:S(2)}) collective-permute-start(bf16[2,360,128]{2,1,0:T(8,128)(2,1)S(1)} %pad_maximum_fusion.12), channel_id=1, source_target_pairs={{0,24},{8,16},{16,8},{24,0},{1,25},{9,17},{17,9},{25,1},{2,26},{10... | collective-permute-start | bytes 552968 | tf_op jit(solution)/shard_map/ppermute | solution.py:11
  34.5 15.8 %collective-permute-start.12 = (bf16[2,360,128]{2,1,0:T(8,128)(2,1)S(1)}, bf16[2,360,128]{2,1,0:T(8,128)(2,1)S(1)}, u32[]{:S(2)}, u32[]{:S(2)}) collective-permute-start(bf16[2,360,128]{2,1,0:T(8,128)(2,1)S(1)} %pad_maximum_fusion.12), channel_id=1, source_target_pairs={{0,16},{8,24},{16,0},{24,8},{1,17},{9,25},{17,1},{25,9},{2,18},{10... | collective-permute-start | bytes 552968 | tf_op jit(solution)/shard_map/ppermute | solution.py:11
  35.2 15.1 %collective-permute-start.11 = (bf16[2,360,128]{2,1,0:T(8,128)(2,1)S(1)}, bf16[2,360,128]{2,1,0:T(8,128)(2,1)S(1)}, u32[]{:S(2)}, u32[]{:S(2)}) collective-permute-start(bf16[2,360,128]{2,1,0:T(8,128)(2,1)S(1)} %pad_maximum_fusion.12), channel_id=1, source_target_pairs={{0,8},{8,0},{16,24},{24,16},{1,9},{9,1},{17,25},{25,17},{2,10},{10... | collective-permute-start | bytes 552968 | tf_op jit(solution)/shard_map/ppermute | solution.py:11
  37.2 13.1 %collective-permute-start.14 = (bf16[3,360,128]{2,1,0:T(8,128)(2,1)S(1)}, bf16[3,360,128]{2,1,0:T(8,128)(2,1)S(1)}, u32[]{:S(2)}, u32[]{:S(2)}) collective-permute-start(bf16[3,360,128]{2,1,0:T(8,128)(2,1)S(1)} %pad_maximum_fusion.9), channel_id=1, source_target_pairs={{0,2},{2,0},{4,6},{6,4},{1,3},{3,1},{5,7},{7,5},{8,10},{10,8},{12,... | collective-permute-start | bytes 829448 | tf_op jit(solution)/shard_map/ppermute | solution.py:11
  73.2 14.5 %collective-permute-start.22 = (bf16[2,360,128]{2,1,0:T(8,128)(2,1)S(1)}, bf16[2,360,128]{2,1,0:T(8,128)(2,1)S(1)}, u32[]{:S(2)}, u32[]{:S(2)}) collective-permute-start(bf16[2,360,128]{2,1,0:T(8,128)(2,1)S(1)} %get-tuple-element.125), channel_id=1, source_target_pairs={{0,8},{8,0},{16,24},{24,16},{1,9},{9,1},{17,25},{25,17},{2,10},{10... | collective-permute-start | bytes 552968 | tf_op jit(solution)/shard_map/ppermute | solution.py:11
  73.7 14.1 %collective-permute-start.21 = (bf16[2,360,128]{2,1,0:T(8,128)(2,1)S(1)}, bf16[2,360,128]{2,1,0:T(8,128)(2,1)S(1)}, u32[]{:S(2)}, u32[]{:S(2)}) collective-permute-start(bf16[2,360,128]{2,1,0:T(8,128)(2,1)S(1)} %get-tuple-element.126), channel_id=1, source_target_pairs={{0,16},{8,24},{16,0},{24,8},{1,17},{9,25},{17,1},{25,9},{2,18},{10... | collective-permute-start | bytes 552968 | tf_op jit(solution)/shard_map/ppermute | solution.py:11
  75.0 12.7 %collective-permute-start.20 = (bf16[2,360,128]{2,1,0:T(8,128)(2,1)S(1)}, bf16[2,360,128]{2,1,0:T(8,128)(2,1)S(1)}, u32[]{:S(2)}, u32[]{:S(2)}) collective-permute-start(bf16[2,360,128]{2,1,0:T(8,128)(2,1)S(1)} %get-tuple-element.127), channel_id=1, source_target_pairs={{0,24},{8,16},{16,8},{24,0},{1,25},{9,17},{17,9},{25,1},{2,26},{10... | collective-permute-start | bytes 552968 | tf_op jit(solution)/shard_map/ppermute | solution.py:11
  76.8 11.0 %collective-permute-start.23 = (bf16[360,512]{1,0:T(8,128)(2,1)S(1)}, bf16[360,512]{1,0:T(8,128)(2,1)S(1)}, u32[]{:S(2)}, u32[]{:S(2)}) collective-permute-start(bf16[360,512]{1,0:T(8,128)(2,1)S(1)} %get-tuple-element.106), channel_id=1, source_target_pairs={{0,2},{2,0},{4,6},{6,4},{1,3},{3,1},{5,7},{7,5},{8,10},{10,8},{12,... | collective-permute-start | bytes 1105928 | tf_op jit(solution)/shard_map/ppermute | solution.py:11
  88.0 11.1 %collective-permute-start.28 = (bf16[360,128]{1,0:T(8,128)(2,1)S(1)}, bf16[360,128]{1,0:T(8,128)(2,1)S(1)}, u32[]{:S(2)}, u32[]{:S(2)}) collective-permute-start(bf16[360,128]{1,0:T(8,128)(2,1)S(1)} %get-tuple-element.128), channel_id=1, source_target_pairs={{0,8},{8,0},{16,24},{24,16},{1,9},{9,1},{17,25},{25,17},{2,10},{10... | collective-permute-start | bytes 276488 | tf_op jit(solution)/shard_map/ppermute | solution.py:11
  88.6 10.5 %collective-permute-start.27 = (bf16[360,128]{1,0:T(8,128)(2,1)S(1)}, bf16[360,128]{1,0:T(8,128)(2,1)S(1)}, u32[]{:S(2)}, u32[]{:S(2)}) collective-permute-start(bf16[360,128]{1,0:T(8,128)(2,1)S(1)} %get-tuple-element.129), channel_id=1, source_target_pairs={{0,16},{8,24},{16,0},{24,8},{1,17},{9,25},{17,1},{25,9},{2,18},{10... | collective-permute-start | bytes 276488 | tf_op jit(solution)/shard_map/ppermute | solution.py:11
  89.9 9.2 %collective-permute-start.26 = (bf16[360,128]{1,0:T(8,128)(2,1)S(1)}, bf16[360,128]{1,0:T(8,128)(2,1)S(1)}, u32[]{:S(2)}, u32[]{:S(2)}) collective-permute-start(bf16[360,128]{1,0:T(8,128)(2,1)S(1)} %get-tuple-element.130), channel_id=1, source_target_pairs={{0,24},{8,16},{16,8},{24,0},{1,25},{9,17},{17,9},{25,1},{2,26},{10... | collective-permute-start | bytes 276488 | tf_op jit(solution)/shard_map/ppermute | solution.py:11
  91.7 7.6 %collective-permute-start.25 = (bf16[360,128]{1,0:T(8,128)(2,1)S(1)}, bf16[360,128]{1,0:T(8,128)(2,1)S(1)}, u32[]{:S(2)}, u32[]{:S(2)}) collective-permute-start(bf16[360,128]{1,0:T(8,128)(2,1)S(1)} %get-tuple-element.152), channel_id=1, source_target_pairs={{0,4},{2,6},{4,0},{6,2},{1,5},{3,7},{5,1},{7,3},{8,12},{10,14},{12... | collective-permute-start | bytes 276488 | tf_op jit(solution)/shard_map/ppermute | solution.py:11
  (27 other events, 131.3 us)
